TPU v7x, 32 devices: a whole 2x2x4 slice. The times are simulated.
32 devices in a mesh: dp: 16 (over z, y, x), mp: 2 (over core).
Axes of the slice: x: 2, y: 2, z: 4, core: 2. Of those that a mesh axis runs over, the one named last changes fastest.
Arguments:
- text: bfloat16 [16000, 768], P('dp', 'mp'), may hold values from -6 to 6
- patches: bfloat16 [400, 145, 1024], P('dp'), may hold values from -6 to 6
- segment_ids: int32 [400, 40], P('dp'), may hold values from 0 to 4, never falling along the last dimension, each value on 1 to 20 neighbouring positions
- row_image: int32 [400], P('dp'), may hold values from 0 to 399, as said below
- self_qkv: bfloat16 [3, 768, 768], P(None, None, 'mp'), may hold values from -0.21875 to 0.21875
- self_bias: bfloat16 [2, 768], P(None, 'mp'), may hold values from -3 to 3
- self_out: bfloat16 [768, 768], P('mp'), may hold values from -0.4375 to 0.4375
- cross_query: bfloat16 [768, 768], P(None, 'mp'), may hold values from -0.21875 to 0.21875
- cross_bias: bfloat16 [2, 768], P(None, 'mp'), may hold values from -3 to 3
- cross_kv: bfloat16 [2, 1024, 768], P(None, None, 'mp'), may hold values from -0.1875 to 0.1875
- cross_out: bfloat16 [768, 768], P('mp'), may hold values from -1.25 to 1.25
- ffn_in: bfloat16 [768, 3072], P(None, 'mp'), may hold values from -0.21875 to 0.21875
- ffn_in_bias: bfloat16 [3072], P('mp'), may hold values from -3 to 3
- ffn_out: bfloat16 [3072, 768], P('mp'), may hold values from -0.109375 to 0.109375
- branch_bias: bfloat16 [3, 768], P(None, 'mp'), may hold values from -3 to 3
- norm_gain: bfloat16 [3, 768], P(None, 'mp'), may hold values from 0.25 to 1.75
- norm_bias: bfloat16 [3, 768], P(None, 'mp'), may hold values from -3 to 3
- cotangent: bfloat16 [16000, 768], P('dp', 'mp'), may hold values from -6 to 6
Outputs:
- joined: float32 [16000, 768], P('dp', 'mp')
- text_grad: float32 [16000, 768], P('dp', 'mp')
- patch_grad: float32 [400, 145, 1024], P('dp', None, 'mp')
- grad_self_qkv: float32 [3, 768, 768], P(None, 'dp', 'mp')
- grad_self_bias: float32 [2, 768], P(None, 'mp')
- grad_self_out: float32 [768, 768], P('mp', 'dp')
- grad_cross_query: float32 [768, 768], P('dp', 'mp')
- grad_cross_bias: float32 [2, 768], P(None, 'mp')
- grad_cross_kv: float32 [2, 1024, 768], P(None, 'dp', 'mp')
- grad_cross_out: float32 [768, 768], P('mp', 'dp')
- grad_ffn_in: float32 [768, 3072], P('dp', 'mp')
- grad_ffn_in_bias: float32 [3072], P('mp')
- grad_ffn_out: float32 [3072, 768], P('mp', 'dp')
- grad_branch_bias: float32 [3, 768], P(None, 'mp')
- grad_norm_gain: float32 [3, 768], P(None, 'mp')
- grad_norm_bias: float32 [3, 768], P(None, 'mp')
Inputs may be any that keep to these rules, and one draw needn't show every extreme that they name: `segment_ids`: within a row the ids never fall; a token attends only to tokens of its own row with its own id. `row_image`: the image of row r lies among the 25 images that start at r // 25 * 25.
All inputs are finite; a program needn't handle non-finite values.
Results may differ from a plain program's by a relative error of at most 0.024.
Values may be sent and summed in bfloat16 or wider, within the bound.
A program may use at most 256 MiB of HBM per device.

v0:
```python
from functools import partial

import jax
import jax.numpy as jnp
from jax import lax
from jax.sharding import PartitionSpec as P

D = 768
HD = 64


EPS = 1e-06
BIG_NEG = -1000000000.0


def product(left, right):
    return jnp.dot(left, right, preferred_element_type=jnp.float32)


def left_product(left, right):
    return lax.dot_general(
        left, right, (((0,), (0,)), ((), ())), preferred_element_type=jnp.float32
    )


def right_product(left, right):
    return lax.dot_general(
        left, right, (((1,), (1,)), ((), ())), preferred_element_type=jnp.float32
    )


def softmax_rows(scores):
    peak = jnp.max(scores, axis=-1, keepdims=True)
    weight = jnp.exp(scores - peak)
    return weight / jnp.sum(weight, axis=-1, keepdims=True)


def widen(block):
    return lax.all_gather(block, "mp", axis=1, tiled=True)


def widen_grad(block):
    return lax.all_gather(block, "mp", axis=1, tiled=True)


def fold_branch(terms):
    return lax.psum_scatter(terms, "mp", scatter_dimension=1, tiled=True)


def fold_grad(terms):
    return lax.psum_scatter(terms, "mp", scatter_dimension=1, tiled=True)


def norm_forward(resid, gain, shift):
    total, square = lax.psum((jnp.sum(resid, axis=1), jnp.sum(resid * resid, axis=1)), "mp")
    mean = total / D
    spread = lax.rsqrt(square / D - mean * mean + EPS)
    normed = (resid - mean[:, None]) * spread[:, None]
    return (normed * gain + shift, normed, spread)


def norm_backward(incoming, normed, spread, gain):
    scaled = incoming * gain
    total, inner = lax.psum((jnp.sum(scaled, axis=1), jnp.sum(scaled * normed, axis=1)), "mp")
    grad_resid = spread[:, None] * (scaled - total[:, None] / D - normed * (inner[:, None] / D))
    return (grad_resid, jnp.sum(incoming * normed, axis=0), jnp.sum(incoming, axis=0))


def attend_forward(query, keys, values, allowed):
    scores = jnp.einsum("rqhd,rkhd->rhqk", query, keys, preferred_element_type=jnp.float32) * 0.125
    if allowed is not None:
        scores = jnp.where(allowed, scores, BIG_NEG)
    probs = softmax_rows(scores)
    probs_low = probs.astype(jnp.bfloat16)
    context = jnp.einsum("rhqk,rkhd->rqhd", probs_low, values, preferred_element_type=jnp.float32)
    return (probs, probs_low, context)


def attend_backward(grad_context, query, keys, values, probs, probs_low):
    grad_probs = jnp.einsum(
        "rqhd,rkhd->rhqk", grad_context, values, preferred_element_type=jnp.float32
    )
    grad_values = jnp.einsum(
        "rhqk,rqhd->rkhd", probs_low, grad_context, preferred_element_type=jnp.float32
    )
    grad_scores = probs * (grad_probs - jnp.sum(grad_probs * probs, axis=-1, keepdims=True))
    grad_scores = grad_scores.astype(jnp.bfloat16)
    grad_query = (
        jnp.einsum("rhqk,rkhd->rqhd", grad_scores, keys, preferred_element_type=jnp.float32) * 0.125
    )
    grad_keys = (
        jnp.einsum("rhqk,rqhd->rkhd", grad_scores, query, preferred_element_type=jnp.float32)
        * 0.125
    )
    return (grad_query, grad_keys, grad_values)


def local(
    text,
    patches,
    segment_ids,
    row_image,
    self_qkv,
    self_bias,
    self_out,
    cross_query,
    cross_bias,
    cross_kv,
    cross_out,
    ffn_in,
    ffn_in_bias,
    ffn_out,
    branch_bias,
    norm_gain,
    norm_bias,
    cotangent,
):
    bfloat = jnp.bfloat16
    single = jnp.float32
    row_count, row_length = segment_ids.shape
    image_count, patch_count, visual = patches.shape
    width_here = self_qkv.shape[2]
    head_count = width_here // HD
    token_count = text.shape[0]

    def split_heads(block, count):
        return block.reshape(count, -1, head_count, HD)

    gains = norm_gain.astype(single)
    shifts = norm_bias.astype(single)
    biases = branch_bias.astype(single)
    text_full = widen(text)
    projected = jnp.einsum("td,sdc->stc", text_full, self_qkv, preferred_element_type=single)
    query = (projected[0] + self_bias[0].astype(single)).astype(bfloat)
    keys = projected[1].astype(bfloat)
    values = (projected[2] + self_bias[1].astype(single)).astype(bfloat)
    allowed = (segment_ids[:, :, None] == segment_ids[:, None, :])[:, None]
    probs, probs_low, context = attend_forward(
        split_heads(query, row_count),
        split_heads(keys, row_count),
        split_heads(values, row_count),
        allowed,
    )
    context = context.reshape(token_count, width_here).astype(bfloat)
    first = text.astype(single) + fold_branch(product(context, self_out)) + biases[0]
    middle, normed_one, spread_one = norm_forward(first, gains[0], shifts[0])
    middle_full = widen(middle.astype(bfloat))
    cross_q = (product(middle_full, cross_query) + cross_bias[0].astype(single)).astype(bfloat)
    patch_rows = patches.reshape(image_count * patch_count, visual)
    kv_pair = jnp.einsum("pv,svc->spc", patch_rows, cross_kv, preferred_element_type=single)
    cross_k = kv_pair[0].astype(bfloat)
    cross_v = (kv_pair[1] + cross_bias[1].astype(single)).astype(bfloat)
    local_image = row_image - lax.axis_index("dp") * image_count
    row_keys = jnp.take(cross_k.reshape(image_count, patch_count, width_here), local_image, axis=0)
    row_values = jnp.take(
        cross_v.reshape(image_count, patch_count, width_here), local_image, axis=0
    )
    cross_probs, cross_low, cross_context = attend_forward(
        split_heads(cross_q, row_count),
        split_heads(row_keys, row_count),
        split_heads(row_values, row_count),
        None,
    )
    cross_context = cross_context.reshape(token_count, width_here).astype(bfloat)
    second = middle + fold_branch(product(cross_context, cross_out)) + biases[1]
    later, normed_two, spread_two = norm_forward(second, gains[1], shifts[1])
    later_full = widen(later.astype(bfloat))
    hidden_pre = product(later_full, ffn_in) + ffn_in_bias.astype(single)
    activated, gelu_back = jax.vjp(partial(jax.nn.gelu, approximate=False), hidden_pre)
    activated = activated.astype(bfloat)
    third = later + fold_branch(product(activated, ffn_out)) + biases[2]
    joined, normed_three, spread_three = norm_forward(third, gains[2], shifts[2])
    grad_third, gain_three, shift_three = norm_backward(
        cotangent.astype(single), normed_three, spread_three, gains[2]
    )
    third_full = widen_grad(grad_third.astype(bfloat))
    grad_ffn_out = left_product(activated, third_full)
    grad_activated = right_product(third_full, ffn_out).astype(bfloat)
    (grad_hidden,) = gelu_back(grad_activated.astype(single))
    hidden_low = grad_hidden.astype(bfloat)
    grad_ffn_in = left_product(later_full, hidden_low)
    grad_later = grad_third + fold_grad(right_product(hidden_low, ffn_in))
    grad_second, gain_two, shift_two = norm_backward(grad_later, normed_two, spread_two, gains[1])
    second_full = widen_grad(grad_second.astype(bfloat))
    grad_cross_out = left_product(cross_context, second_full)
    grad_cross_ctx = right_product(second_full, cross_out).astype(bfloat)
    grad_cross_q, grad_row_keys, grad_row_values = attend_backward(
        split_heads(grad_cross_ctx, row_count),
        split_heads(cross_q, row_count),
        split_heads(row_keys, row_count),
        split_heads(row_values, row_count),
        cross_probs,
        cross_low,
    )
    picker = (jnp.arange(image_count, dtype=jnp.int32)[:, None] == local_image[None, :]).astype(
        single
    )
    row_pair = jnp.stack(
        (grad_row_keys.reshape(row_count, -1), grad_row_values.reshape(row_count, -1))
    )
    grad_pair = jnp.einsum("ir,srx->six", picker, row_pair, precision=lax.Precision.HIGHEST)
    grad_pair = grad_pair.reshape(2, image_count * patch_count, width_here)
    pair_low = grad_pair.astype(bfloat)
    grad_cross_kv = jnp.einsum("pv,spc->svc", patch_rows, pair_low, preferred_element_type=single)
    patch_terms = jnp.einsum("spc,svc->pv", pair_low, cross_kv, preferred_element_type=single)
    patch_grad = lax.psum_scatter(
        patch_terms.reshape(image_count, patch_count, visual).astype(jnp.bfloat16),
        "mp",
        scatter_dimension=2,
        tiled=True,
    ).astype(jnp.float32)
    grad_cross_q = grad_cross_q.reshape(token_count, width_here)
    cross_q_low = grad_cross_q.astype(bfloat)
    grad_cross_query = left_product(middle_full, cross_q_low)
    grad_cross_bias = jnp.stack((jnp.sum(grad_cross_q, axis=0), jnp.sum(grad_pair[1], axis=0)))
    grad_middle = grad_second + fold_grad(right_product(cross_q_low, cross_query))
    grad_first, gain_one, shift_one = norm_backward(grad_middle, normed_one, spread_one, gains[0])
    first_full = widen_grad(grad_first.astype(bfloat))
    grad_self_out = left_product(context, first_full)
    grad_context = right_product(first_full, self_out).astype(bfloat)
    grad_query, grad_keys, grad_values = attend_backward(
        split_heads(grad_context, row_count),
        split_heads(query, row_count),
        split_heads(keys, row_count),
        split_heads(values, row_count),
        probs,
        probs_low,
    )
    grad_qkv = jnp.stack((grad_query, grad_keys, grad_values)).reshape(3, token_count, width_here)
    qkv_low = grad_qkv.astype(bfloat)
    grad_self_qkv = jnp.einsum("td,stc->sdc", text_full, qkv_low, preferred_element_type=single)
    grad_self_bias = jnp.stack((jnp.sum(grad_qkv[0], axis=0), jnp.sum(grad_qkv[2], axis=0)))
    text_grad = grad_first + fold_grad(
        jnp.einsum("stc,sdc->td", qkv_low, self_qkv, preferred_element_type=single)
    )
    (
        grad_self_qkv,
        grad_self_out,
        grad_cross_query,
        grad_cross_kv,
        grad_cross_out,
        grad_ffn_in,
        grad_ffn_out,
    ) = (
        lax.psum_scatter(grad_self_qkv, "dp", scatter_dimension=1, tiled=True),
        lax.psum_scatter(grad_self_out, "dp", scatter_dimension=1, tiled=True),
        lax.psum_scatter(grad_cross_query, "dp", scatter_dimension=0, tiled=True),
        lax.psum_scatter(grad_cross_kv, "dp", scatter_dimension=1, tiled=True),
        lax.psum_scatter(grad_cross_out, "dp", scatter_dimension=1, tiled=True),
        lax.psum_scatter(grad_ffn_in, "dp", scatter_dimension=0, tiled=True),
        lax.psum_scatter(grad_ffn_out, "dp", scatter_dimension=1, tiled=True),
    )
    branch_grads = jnp.stack(
        (jnp.sum(grad_first, axis=0), jnp.sum(grad_second, axis=0), jnp.sum(grad_third, axis=0))
    )
    gain_grads = jnp.stack((gain_one, gain_two, gain_three))
    shift_grads = jnp.stack((shift_one, shift_two, shift_three))
    grad_self_bias, grad_cross_bias, grad_ffn_in_bias, branch_grads, gain_grads, shift_grads = (
        lax.psum(
            (
                grad_self_bias,
                grad_cross_bias,
                jnp.sum(grad_hidden, axis=0),
                branch_grads,
                gain_grads,
                shift_grads,
            ),
            "dp",
        )
    )
    return (
        joined,
        text_grad,
        patch_grad,
        grad_self_qkv,
        grad_self_bias,
        grad_self_out,
        grad_cross_query,
        grad_cross_bias,
        grad_cross_kv,
        grad_cross_out,
        grad_ffn_in,
        grad_ffn_in_bias,
        grad_ffn_out,
        branch_grads,
        gain_grads,
        shift_grads,
    )


def solution(mesh):
    return jax.shard_map(
        local,
        mesh=mesh,
        in_specs=(
            P("dp", "mp"),
            P("dp", None, None),
            P("dp", None),
            P("dp"),
            P(None, None, "mp"),
            P(None, "mp"),
            P("mp", None),
            P(None, "mp"),
            P(None, "mp"),
            P(None, None, "mp"),
            P("mp", None),
            P(None, "mp"),
            P("mp"),
            P("mp", None),
            P(None, "mp"),
            P(None, "mp"),
            P(None, "mp"),
            P("dp", "mp"),
        ),
        out_specs=(
            P("dp", "mp"),
            P("dp", "mp"),
            P("dp", None, "mp"),
            P(None, "dp", "mp"),
            P(None, "mp"),
            P("mp", "dp"),
            P("dp", "mp"),
            P(None, "mp"),
            P(None, "dp", "mp"),
            P("mp", "dp"),
            P("dp", "mp"),
            P("mp"),
            P("mp", "dp"),
            P(None, "mp"),
            P(None, "mp"),
            P(None, "mp"),
        ),
        check_vma=False,
    )
```

profile of v0, /device:TPU:0, one launch (start us, length us, event | category | flops | bytes accessed | tf_op | source)
XLA Modules:
  0.0 1505.3 jit_solution(9310503396126265464)
XLA Ops:
  9.9 12.1 all-gather.7.cloned.1.call-done
  22.0 4.2 convolution_bitcast_fusion.3
  30.6 3.9 squeeze.9
  34.5 3.9 squeeze.8
  53.1 4.0 fusion.88
  57.4 8.1 reshape.186
  65.5 9.4 convolution_bitcast_fusion.1
  79.6 4.6 convert_element_type.149
  84.2 6.3 squeeze.10
  99.2 4.7 gather_fusion.1
  104.0 5.1 add_convert_fusion
  109.1 4.8 gather_fusion
  113.8 6.2 broadcast_select_fusion
  120.0 6.0 copy.111
  126.0 6.0 copy.110
  135.3 3.7 reshape.155
  139.0 4.3 fusion.56
  143.3 26.0 %fusion.85 = (f32[25,6,40]{2,1,0:T(8,128)S(1)}, f32[25,6,40,145]{3,2,1,0:T(8,128)S(1)}) fusion(f32[25,6,40,145]{3,2,1,0:T(8,128)S(1)} %fusion.56), kind=kOutput, calls=%fused_computation.195 | output fusion | flops 3480144 | bytes 6984000 | tf_op jit(solution)/shard_map/sub | solution.py:34
  176.8 3.9 fusion.89
  180.8 12.0 reduce-scatter.15.cloned.1.call-done
  201.9 10.5 all-gather.11.cloned.1.call-done
  212.4 18.2 %multiply_convert_fusion.1 = (bf16[1000,1536]{1,0:T(8,128)(2,1)S(1)}, f32[1000,1536]{1,0:T(8,128)}, f32[1000,1536]{1,0:T(8,128)}) fusion(f32[1536]{0:T(1024)S(1)} %convert_element_type.155, bf16[1000,768]{1,0:T(8,128)(2,1)} %all-gather.11.cloned.1.call-done, bf16[768,1536]{1,0:T(8,128)(2,1)S(1)} %copy-done), kind=kOutput, calls=%fused_computation.23 | convolution fusion | flops 2460672000 | bytes 19261440 | tf_op jit(solution)/shard_map/dot_general | solution.py:17
  232.3 4.2 fusion.90
  236.6 12.1 reduce-scatter.17.cloned.1.call-done
  265.6 10.8 all-gather.13.cloned.1.call-done
  276.4 10.7 fusion.87
  288.7 4.2 fusion.34
  293.0 12.1 reduce-scatter.19.cloned.1.call-done
  305.1 4.1 multiply_reduce_fusion.3
  316.6 10.8 all-gather.15.cloned.1.call-done
  333.4 6.3 multiply_reduce_fusion
  339.7 4.5 multiply_convert_fusion
  349.0 3.8 fusion.91
  352.9 12.1 reduce-scatter.21.cloned.1.call-done
  375.2 11.0 all-gather.17.cloned.1.call-done
  392.6 3.8 multiply_reduce_fusion.2
  420.4 3.8 convolution_bitcast_fusion.6
  425.8 7.7 multiply_bitcast_fusion
  433.5 14.2 copy.126
  447.7 17.3 %stack_reshape.6 = f32[1,25,55680]{2,1,0:T(8,128)} reshape(f32[25,145,6,64]{3,2,1,0:T(8,128)} %copy.126) | data formatting | bytes 11136000 | tf_op jit(solution)/shard_map/stack;reshape | solution.py:198
  465.0 8.3 convolution_bitcast_fusion.2
  473.3 14.0 copy.128
  487.3 17.1 %stack_reshape.7 = f32[1,25,55680]{2,1,0:T(8,128)} reshape(f32[25,145,6,64]{3,2,1,0:T(8,128)} %copy.128) | data formatting | bytes 11136000 | tf_op jit(solution)/shard_map/stack;reshape | solution.py:198
  504.5 15.0 fusion.86
  519.5 12.1 convert_element_type.171
  531.6 11.6 convolution_bitcast_fusion.5
  543.1 6.0 copy.130
  549.2 5.3 convolution_bitcast_fusion.4
  554.5 6.3 copy.129
  560.9 5.4 dot_general.133
  566.2 12.1 bitcast_convert_fusion
  579.8 6.2 fusion.95
  587.3 6.2 fusion.32
  608.4 6.3 slice.104
  614.7 6.2 squeeze.11
  628.9 78.4 %all-reduce.2 = (f32[2,384]{1,0:T(2,128)}, f32[2,384]{1,0:T(2,128)}, f32[1536]{0:T(1024)}, f32[3,384]{1,0:T(4,128)}, f32[3,384]{1,0:T(4,128)}, /*index=5*/f32[3,384]{1,0:T(4,128)}) all-reduce(f32[2,384]{1,0:T(2,128)S(1)} %pad_maximum_fusion.3, f32[2,384]{1,0:T(2,128)S(1)} %pad_maximum_fusion.4, ...), channel_id=1, replica_groups=mesh['dp'=16,'mp'=2] {'dp'}, use_global_device_ids=true, to_apply=%region_40.42 | all-reduce | flops 6528 | bytes 52224 | tf_op jit(solution)/shard_map/psum | solution.py:259
  710.0 97.9 %all-reduce.12.cloned.1.call-done = (f32[3,768,384]{2,0,1:T(4,128)}, f32[2,1024,384]{2,0,1:T(2,128)}) async-done(((f32[3,768,384]{2,0,1:T(4,128)}, f32[2,1024,384]{2,0,1:T(2,128)}), (f32[3,768,384]{2,0,1:T(4,128)}, f32[2,1024,384]{2,0,1:T(2,128)})) %all-reduce.12.cloned.1.call-update) | async-done | bytes 6684688
  811.3 14.9 reduce-scatter.25.cloned.1.call-done
  826.2 6.6 convert_element_type.173
  832.8 138.4 %reduce-scatter.35.cloned.1.call-done = f32[1536,48]{0,1:T(8,128)} async-done(((f32[1536,768]{0,1:T(8,128)}), f32[1536,48]{0,1:T(8,128)}) %reduce-scatter.35.cloned.1.call-update) | async-done | bytes 294928 | tf_op jit(solution)/shard_map/reduce_scatter | solution.py:251
  971.2 141.7 %reduce-scatter.33.cloned.1.call-done = f32[48,1536]{1,0:T(8,128)} async-done(((f32[768,1536]{1,0:T(8,128)}), f32[48,1536]{1,0:T(8,128)}) %reduce-scatter.33.cloned.1.call-update) | async-done | bytes 294928 | tf_op jit(solution)/shard_map/reduce_scatter | solution.py:250
  1112.9 128.4 %reduce-scatter.31.cloned.1.call-done = f32[384,48]{0,1:T(8,128)} async-done(((f32[384,768]{0,1:T(8,128)}), f32[384,48]{0,1:T(8,128)}) %reduce-scatter.31.cloned.1.call-update) | async-done | bytes 73744 | tf_op jit(solution)/shard_map/reduce_scatter | solution.py:249
  1241.3 128.4 %reduce-scatter.29.cloned.1.call-done = f32[48,384]{1,0:T(8,128)} async-done(((f32[768,384]{1,0:T(8,128)}), f32[48,384]{1,0:T(8,128)}) %reduce-scatter.29.cloned.1.call-update) | async-done | bytes 73744 | tf_op jit(solution)/shard_map/reduce_scatter | solution.py:247
  1369.7 128.6 %reduce-scatter.27.cloned.1.call-done = f32[384,48]{0,1:T(8,128)} async-done(((f32[384,768]{0,1:T(8,128)}), f32[384,48]{0,1:T(8,128)}) %reduce-scatter.27.cloned.1.call-update) | async-done | bytes 73744 | tf_op jit(solution)/shard_map/reduce_scatter | solution.py:246
  (278 shorter events, 165.9 us)
Async XLA Ops:
  7.2 205.2 %copy-start = (bf16[768,1536]{1,0:T(8,128)(2,1)S(1)}, bf16[768,1536]{1,0:T(8,128)(2,1)}, u32[]{:S(2)}) copy-start(bf16[768,1536]{1,0:T(8,128)(2,1)} %param.31) | copy-start | bytes 7077892
  7.2 14.8 all-gather.7.cloned.1.call-start
  7.9 82.6 %reduce-scatter.13.cloned.1.call-start = ((), (), s32[]{:S(2)}) async-start(), calls=%async_computation.13 | async-start | bytes 4608000 | tf_op jit(solution)/shard_map/reduce_scatter | solution.py:47
  38.3 4.1 copy-start.12
  53.0 4.1 copy-start.20
  57.1 74.9 %all-gather.9.cloned.1.call-start = ((), (), s32[]{:S(2)}) async-start(), calls=%async_computation.14 | async-start | bytes 2304000 | tf_op jit(solution)/shard_map/all_gather | solution.py:39
  76.7 2.9 copy-start.46
  76.7 2.9 copy-start.47
  76.7 2.9 copy-start.48
  84.2 6.3 copy-start.25
  90.5 8.2 copy-start.51
  98.4 94.4 %reduce-scatter.15.cloned.1.call-start = ((), (), s32[]{:S(2)}) async-start(), calls=%async_computation.15 | async-start | bytes 4608000 | tf_op jit(solution)/shard_map/reduce_scatter | solution.py:47
  99.2 4.7 copy-start.44
  126.0 6.0 copy-start.31
  135.2 34.0 %slice-start.2 = ((s8[4915200]{0:T(1024)(128)(4,1)}), s8[720896]{0:T(1024)(128)(4,1)S(1)}, s32[]{:S(2)}) async-start(s8[4915200]{0:T(1024)(128)(4,1)} %bitcast.107), calls=%async_computation.33 | async-start | bytes 1441792
  139.0 30.3 %slice-start.3 = ((s8[4915200]{0:T(1024)(128)(4,1)}), s8[4194304]{0:T(1024)(128)(4,1)S(1)}, s32[]{:S(2)}) async-start(s8[4915200]{0:T(1024)(128)(4,1)} %bitcast.107), calls=%async_computation.34 | async-start | bytes 8388608
  169.3 2.7 copy-start.5
  176.8 3.9 copy-start.22
  180.7 31.7 %all-gather.11.cloned.1.call-start = ((), (), s32[]{:S(2)}) async-start(), calls=%async_computation.16 | async-start | bytes 2304000 | tf_op jit(solution)/shard_map/all_gather | solution.py:39
  192.8 9.1 copy-start.45
  201.4 47.3 %reduce-scatter.17.cloned.1.call-start = ((), (), s32[]{:S(2)}) async-start(), calls=%async_computation.17 | async-start | bytes 4608000 | tf_op jit(solution)/shard_map/reduce_scatter | solution.py:47
  212.4 19.9 %copy-start.52 = (bf16[1536,768]{1,0:T(8,128)(2,1)S(1)}, bf16[1536,768]{1,0:T(8,128)(2,1)}, u32[]{:S(2)}) copy-start(bf16[1536,768]{1,0:T(8,128)(2,1)} %param.33) | copy-start | bytes 7077892
  236.5 18.1 %copy-start.19 = (bf16[1000,384]{1,0:T(8,128)(2,1)S(1)}, bf16[1000,384]{1,0:T(8,128)(2,1)}, u32[]{:S(2)}) copy-start(bf16[1000,384]{1,0:T(8,128)(2,1)} %param.37) | copy-start | bytes 2304004
  236.5 39.9 %all-gather.13.cloned.1.call-start = ((), (), s32[]{:S(2)}) async-start(), calls=%async_computation.18 | async-start | bytes 2304000 | tf_op jit(solution)/shard_map/all_gather | solution.py:43
  265.4 39.7 %reduce-scatter.19.cloned.1.call-start = ((), (), s32[]{:S(2)}) async-start(), calls=%async_computation.19 | async-start | bytes 4608000 | tf_op jit(solution)/shard_map/reduce_scatter | solution.py:51
  292.9 12.2 copy-start.2
  293.0 34.4 %all-gather.15.cloned.1.call-start = ((), (), s32[]{:S(2)}) async-start(), calls=%async_computation.20 | async-start | bytes 2304000 | tf_op jit(solution)/shard_map/all_gather | solution.py:43
  311.6 15.7 %copy-start.30 = (bf16[384,768]{1,0:T(8,128)(2,1)S(1)}, bf16[384,768]{1,0:T(8,128)(2,1)}, u32[]{:S(2)}) copy-start(bf16[384,768]{1,0:T(8,128)(2,1)} %param.30) | copy-start | bytes 1769476
  316.3 48.6 %reduce-scatter.21.cloned.1.call-start = ((), (), s32[]{:S(2)}) async-start(), calls=%async_computation.21 | async-start | bytes 4608000 | tf_op jit(solution)/shard_map/reduce_scatter | solution.py:51
  327.4 16.9 %slice-start = ((s8[4915200]{0:T(1024)(128)(4,1)}), s8[720896]{0:T(1024)(128)(4,1)S(1)}, s32[]{:S(2)}) async-start(s8[4915200]{0:T(1024)(128)(4,1)} %bitcast.102), calls=%async_computation.31 | async-start | bytes 1441792
  333.4 6.3 copy-start.26
  333.4 10.9 slice-start.1
  344.3 3.1 copy-start.4
  349.0 16.0 %copy-start.3 = (f32[1000,384]{1,0:T(8,128)S(1)}, f32[1000,384]{1,0:T(8,128)}, u32[]{:S(2)}) copy-start(f32[1000,384]{1,0:T(8,128)} %get-tuple-element.144) | copy-start | bytes 4608004
  352.8 33.3 %all-gather.17.cloned.1.call-start = ((), (), s32[]{:S(2)}) async-start(), calls=%async_computation.22 | async-start | bytes 2304000 | tf_op jit(solution)/shard_map/all_gather | solution.py:43
  370.9 15.2 %copy-start.32 = (bf16[384,768]{1,0:T(8,128)(2,1)S(1)}, bf16[384,768]{1,0:T(8,128)(2,1)}, u32[]{:S(2)}) copy-start(bf16[384,768]{1,0:T(8,128)(2,1)} %param.26) | copy-start | bytes 1769476
  375.1 17.4 %copy-start.36 = (f32[25,6,40]{2,1,0:T(8,128)S(1)}, f32[25,6,40]{2,1,0:T(8,128)}, u32[]{:S(2)}) copy-start(f32[25,6,40]{2,1,0:T(8,128)} %copy-done.35) | copy-start | bytes 72004
  375.1 332.2 %reduce-scatter.23.cloned.1.call-start = ((), (), s32[]{:S(2)}) async-start(), calls=%async_computation.23 | async-start | bytes 4608000 | tf_op jit(solution)/shard_map/reduce_scatter | solution.py:51
  392.5 3.9 copy-start.17
  416.1 2.6 copy-start.24
  416.1 4.2 copy-start.53
  424.2 383.7 %all-reduce.12.cloned.1.call-start = ((), (), s32[]{:S(2)}) async-start(), calls=%async_computation.30 | async-start | bytes 15728640
  447.7 17.4 %copy-start.27 = (bf16[25,40,6,64]{3,2,1,0:T(8,128)(2,1)S(1)}, bf16[25,40,6,64]{3,2,1,0:T(8,128)(2,1)}, u32[]{:S(2)}) copy-start(bf16[25,40,6,64]{3,2,1,0:T(8,128)(2,1)} %copy-done.26) | copy-start | bytes 2304004
  487.3 17.2 %copy-start.50 = (s32[25]{0:T(128)S(1)}, s32[25]{0:T(128)}, u32[]{:S(2)}) copy-start(s32[25]{0:T(128)} %copy-done.49) | copy-start | bytes 304
  543.1 6.0 copy-start.34
  560.8 265.5 %reduce-scatter.25.cloned.1.call-start = ((), (), s32[]{:S(2)}) async-start(), calls=%async_computation.24 | async-start | bytes 11673600 | tf_op jit(solution)/shard_map/reduce_scatter | solution.py:206
  560.8 5.4 copy-start.54
  578.4 392.8 %reduce-scatter.35.cloned.1.call-start = ((), (), s32[]{:S(2)}) async-start(), calls=%async_computation.29 | async-start | bytes 5013504 | tf_op jit(solution)/shard_map/reduce_scatter | solution.py:251
  586.0 526.9 %reduce-scatter.33.cloned.1.call-start = ((), (), s32[]{:S(2)}) async-start(), calls=%async_computation.28 | async-start | bytes 5013504 | tf_op jit(solution)/shard_map/reduce_scatter | solution.py:250
  593.6 4.6 copy-start.55
  593.6 647.6 %reduce-scatter.31.cloned.1.call-start = ((), (), s32[]{:S(2)}) async-start(), calls=%async_computation.27 | async-start | bytes 1253376 | tf_op jit(solution)/shard_map/reduce_scatter | solution.py:249
  598.2 2.3 copy-start.21
  598.2 771.5 %reduce-scatter.29.cloned.1.call-start = ((), (), s32[]{:S(2)}) async-start(), calls=%async_computation.26 | async-start | bytes 1253376 | tf_op jit(solution)/shard_map/reduce_scatter | solution.py:247
  600.3 3.7 copy-start.57
  600.3 5.6 copy-start.40
  600.3 5.6 copy-start.39
  600.3 5.6 copy-start.41
  600.4 5.6 copy-start.38
  600.4 5.6 copy-start.37
  600.4 5.7 copy-start.42
  600.4 897.9 %reduce-scatter.27.cloned.1.call-start = ((), (), s32[]{:S(2)}) async-start(), calls=%async_computation.25 | async-start | bytes 1253376 | tf_op jit(solution)/shard_map/reduce_scatter | solution.py:246
  624.3 4.7 copy-start.43
  624.3 83.1 %copy-start.9 = (f32[1000,384]{1,0:T(8,128)S(1)}, f32[1000,384]{1,0:T(8,128)}, u32[]{:S(2)}) copy-start(f32[1000,384]{1,0:T(8,128)} %copy-done.8) | copy-start | bytes 4608004
  826.2 672.1 %copy-start.1 = (bf16[768,1536]{1,0:T(8,128)(2,1)S(1)}, bf16[768,1536]{1,0:T(8,128)(2,1)}, u32[]{:S(2)}) copy-start(bf16[768,1536]{1,0:T(8,128)(2,1)} %param.31) | copy-start | bytes 7077892
  (18 other events, 26.7 us)
Sparse Core Ops, SparseCore 0:
  9.6 12.3 all-gather.6
  57.2 11.9 reduce-scatter.12
  98.5 10.8 all-gather.8
  180.9 11.9 reduce-scatter.14
  201.5 10.8 all-gather.10
  236.6 11.9 reduce-scatter.16
  265.5 10.8 all-gather.12
  293.1 11.9 reduce-scatter.18
  316.5 10.8 all-gather.14
  353.0 11.9 reduce-scatter.20
  375.3 10.8 all-gather.16
  424.4 11.9 reduce-scatter.22
  560.9 246.9 all-reduce.11
  810.8 15.4 reduce-scatter.24
  832.7 138.5 reduce-scatter.34
  976.8 136.0 reduce-scatter.32
  1118.8 122.4 reduce-scatter.30
  1247.2 122.4 reduce-scatter.28
  1375.7 122.5 reduce-scatter.26
where the time goes:
time: 1520 us; the launch traced here: 1510 us
  waiting for transfers between devices  883 us (58%)
  local copies, waits for them, and re-layouts  219 us (14%)
  matrix products  187 us (12%)
  other arithmetic  105 us (7%)
  blocking collectives  93.2 us (6%)
  between operations  16.7 us (1%)
    reduce_scatter x1, waiting for transfers between devices, local(): lax.psum_scatter(grad_ffn_in, 'dp', scatter_dimension=0, tiled=True)  142 us
    reduce_scatter x1, waiting for transfers between devices, local(): lax.psum_scatter(grad_ffn_out, 'dp', scatter_dimension=1, tiled=True)  138 us
    reduce_scatter x1, waiting for transfers between devices, local(): lax.psum_scatter(grad_self_out, 'dp', scatter_dimension=1, tiled=True)  129 us
    reduce_scatter x1, waiting for transfers between devices, local(): lax.psum_scatter(grad_cross_query, 'dp', scatter_dimension=0, tiled=True)  128 us
    reduce_scatter x1, waiting for transfers between devices, local(): lax.psum_scatter(grad_cross_out, 'dp', scatter_dimension=1, tiled=True)  128 us
    unnamed x20, waiting for transfers between devices  98.8 us
    psum x1, blocking collectives, local(): lax.psum((grad_self_bias, grad_cross_bias, jnp.sum(grad_hidden, axis=0),...  78.4 us
    another operation x2, local copies, waits for them, and re-layouts, local(): jnp.stack((grad_row_keys.reshape(row_count, -1), grad_row_values.reshape(...  34.5 us
  transfers between devices with their start and end apart: 19, of which 16 were waited for; matrix products, arithmetic and copies ran while one was open for 18% of the time, Pallas kernels for 0%

commit v1 on v0

v1 whole, which is shorter than its diff:
```python
import math
from functools import partial

import jax
import jax.numpy as jnp
from jax import lax
from jax.experimental import pallas as pl
from jax.experimental.pallas import tpu as pltpu
from jax.sharding import PartitionSpec as P

HD = 64
EPS = 1e-06
BIG_NEG = -1000000000.0
SCALE = 0.125
BF = jnp.bfloat16
F32 = jnp.float32
MIB = 1 << 20


def nn(a, b):
    return lax.dot_general(a, b, (((1,), (0,)), ((), ())), preferred_element_type=F32)


def nt(a, b):
    return lax.dot_general(a, b, (((1,), (1,)), ((), ())), preferred_element_type=F32)


def tn(a, b):
    return lax.dot_general(a, b, (((0,), (0,)), ((), ())), preferred_element_type=F32)


def head_mask(width, head, dtype):
    lane = lax.broadcasted_iota(jnp.int32, (1, width), 1)
    return ((lane >= head * HD) & (lane < (head + 1) * HD)).astype(F32).astype(dtype)


def whole(shape):
    zeros = (0,) * len(shape)
    return pl.BlockSpec(shape, lambda i, *_: zeros, pipeline_mode=pl.Buffered(1))


def tiled(shape):
    zeros = (0,) * (len(shape) - 1)
    return pl.BlockSpec(shape, lambda i, *_: (i,) + zeros)


def call(body, name, grid, ins, outs, scratch, flops, nbytes, scalars=0, vmem=60):
    return pl.pallas_call(
        body,
        name=name,
        out_shape=[jax.ShapeDtypeStruct(s, d) for s, d, _ in outs],
        grid_spec=pltpu.PrefetchScalarGridSpec(
            num_scalar_prefetch=scalars,
            grid=(grid,),
            in_specs=ins,
            out_specs=[spec for _, _, spec in outs],
            scratch_shapes=scratch,
        ),
        compiler_params=pltpu.CompilerParams(
            dimension_semantics=("arbitrary",), vmem_limit_bytes=vmem * MIB
        ),
        cost_estimate=pl.CostEstimate(flops=flops, bytes_accessed=nbytes, transcendentals=0),
    )


def norm(z):
    mu = jnp.mean(z, axis=1, keepdims=True)
    sq = jnp.mean(z * z, axis=1, keepdims=True)
    r = lax.rsqrt(sq - mu * mu + EPS)
    return (z - mu) * r, r


def norm_back(e, n, r, gain):
    a = e * gain
    ma = jnp.mean(a, axis=1, keepdims=True)
    mn = jnp.mean(a * n, axis=1, keepdims=True)
    return r * (a - ma - n * mn)


def colsum(v):
    return jnp.sum(v, axis=0, keepdims=True)


def softmax_cols(s):
    e = jnp.exp(s - jnp.max(s, axis=0, keepdims=True))
    return e * (1.0 / jnp.sum(e, axis=0, keepdims=True))


def softmax_rows(s):
    e = jnp.exp(s - jnp.max(s, axis=1, keepdims=True))
    return e * (1.0 / jnp.sum(e, axis=1, keepdims=True))


def project_patches(patches, cross_kv, bias, padded):
    images, count, visual = patches.shape
    width = cross_kv.shape[2]
    group = 5

    def body(p_ref, w_ref, b_ref, k_ref, v_ref, rows, wcat):
        @pl.when(pl.program_id(0) == 0)
        def _():
            wcat[:, :width] = w_ref[0]
            wcat[:, width:] = w_ref[1]
            rows[...] = jnp.zeros_like(rows)

        for i in range(group):
            rows[padded * i : padded * i + count, :] = p_ref[i]
        out = nn(rows[...], wcat[...])
        k_ref[...] = out[:, :width].astype(BF)
        v_ref[...] = (out[:, width:] + b_ref[1:2, :].astype(F32)).astype(BF)

    tall = (images * padded, width)
    return call(
        body,
        "project_patches",
        images // group,
        [tiled((group, count, visual)), whole(cross_kv.shape), whole(bias.shape)],
        [(tall, BF, tiled((group * padded, width)))] * 2,
        [pltpu.VMEM((group * padded, visual), BF), pltpu.VMEM((visual, 2 * width), BF)],
        2 * images * padded * visual * 2 * width,
        patches.size * 2 + cross_kv.size * 2 + 4 * images * padded * width,
    )(patches, cross_kv, bias)


def self_forward(text, qkv_w, qkv_b, out_w, ids_col, ids_row, tile):
    tokens, width = text.shape
    here = out_w.shape[0]

    def body(x_ref, w_ref, b_ref, o_ref, ic_ref, ir_ref, qkv_ref, c_ref, part_ref, wcat):
        @pl.when(pl.program_id(0) == 0)
        def _():
            for s in range(3):
                wcat[:, s * here : (s + 1) * here] = w_ref[s]

        qkv = (nn(x_ref[...], wcat[...]) + b_ref[...]).astype(BF)
        qkv_ref[...] = qkv
        same = ic_ref[...] == ir_ref[0]
        parts = []
        for p in range(here // 128):
            q = qkv[:, 128 * p : 128 * p + 128]
            k = qkv[:, here + 128 * p : here + 128 * p + 128]
            v = qkv[:, 2 * here + 128 * p : 2 * here + 128 * p + 128]
            total = None
            for a in range(2):
                mask = head_mask(128, a, BF)
                s = jnp.where(same, nt(q * mask, k) * SCALE, BIG_NEG)
                o = nn(softmax_rows(s).astype(BF), v * mask)
                total = o if total is None else total + o
            parts.append(total)
        c = jnp.concatenate(parts, axis=1).astype(BF)
        c_ref[...] = c
        part_ref[...] = nn(c, o_ref[...]).astype(BF)

    return call(
        body,
        "self_forward",
        tokens // tile,
        [
            tiled((tile, width)),
            whole(qkv_w.shape),
            whole(qkv_b.shape),
            whole(out_w.shape),
            tiled((tile, 1)),
            tiled((1, 1, tile)),
        ],
        [
            ((tokens, 3 * here), BF, tiled((tile, 3 * here))),
            ((tokens, here), BF, tiled((tile, here))),
            ((tokens, width), BF, tiled((tile, width))),
        ],
        [pltpu.VMEM((width, 3 * here), BF)],
        2 * tokens * width * 4 * here,
        tokens * (width + 4 * here + width) * 2 + 4 * width * here * 2,
    )(text, qkv_w, qkv_b, out_w, ids_col, ids_row)


def quads(here):
    return [(at, min(256, here - at)) for at in range(0, here, 256)]


def stacked(rows, span):
    return jnp.concatenate(
        [rows * head_mask(span, h, F32) for h in range(span // HD)], axis=0
    ).astype(BF)


def unstacked(tall, span, length):
    total = None
    for h in range(span // HD):
        piece = tall[h * length : (h + 1) * length] * head_mask(span, h, F32)
        total = piece if total is None else total + piece
    return total


def cross_forward(picks, text, mine, other, params, query_w, query_b, keys, values, out_w,
                  tile, length, count, padded):
    tokens, width = text.shape
    here = out_w.shape[0]
    rows = tile // length

    def body(pick, x_ref, m_ref, t_ref, pr_ref, w_ref, b_ref, k_ref, v_ref, o_ref,
             n_ref, r_ref, y_ref, q_ref, c_ref, part_ref, q32, c32):
        h = x_ref[...].astype(F32) + (m_ref[...].astype(F32) + t_ref[...].astype(F32)) + pr_ref[0:1, :]
        n, r = norm(h)
        n_ref[...] = n
        r_ref[...] = r
        y = (n * pr_ref[3:4, :] + pr_ref[6:7, :]).astype(BF)
        y_ref[...] = y
        q = nn(y, w_ref[...]) + b_ref[0:1, :].astype(F32)
        q32[...] = q
        q_ref[...] = q.astype(BF)
        base = pl.program_id(0) * rows
        for j in range(rows):
            at = pl.multiple_of(pick[base + j] * padded, padded)
            for lo, span in quads(here):
                qs = stacked(q32[j * length : (j + 1) * length, lo : lo + span], span)
                s = nt(qs, k_ref[pl.ds(at, padded), lo : lo + span]) * SCALE
                live = lax.broadcasted_iota(jnp.int32, s.shape, 1) < count
                p = softmax_rows(jnp.where(live, s, -1e30))
                o = nn(p.astype(BF), v_ref[pl.ds(at, padded), lo : lo + span])
                c32[j * length : (j + 1) * length, lo : lo + span] = unstacked(o, span, length)
        c = c32[...].astype(BF)
        c_ref[...] = c
        part_ref[...] = nn(c, o_ref[...]).astype(BF)

    full = tiled((tile, width))
    half = tiled((tile, here))
    return call(
        body,
        "cross_forward",
        tokens // tile,
        [full, full, full, whole(params.shape), whole(query_w.shape), whole(query_b.shape),
         whole(keys.shape), whole(values.shape), whole(out_w.shape)],
        [
            ((tokens, width), F32, full),
            ((tokens, 1), F32, tiled((tile, 1))),
            ((tokens, width), BF, full),
            ((tokens, here), BF, half),
            ((tokens, here), BF, half),
            ((tokens, width), BF, full),
        ],
        [pltpu.VMEM((tile, here), F32)] * 2,
        2 * tokens * width * 2 * here + 4 * tokens * padded * here * 4,
        tokens * width * 14 + keys.size * 4,
        scalars=1,
    )(picks, text, mine, other, params, query_w, query_b, keys, values, out_w)


def ffn_forward(normed, mine, other, params, in_w, in_b, out_w, tile):
    tokens, width = normed.shape
    hidden = in_w.shape[1]

    def body(n1_ref, m_ref, t_ref, pr_ref, w_ref, b_ref, o_ref,
             n_ref, r_ref, y_ref, g_ref, d_ref, part_ref):
        h = (n1_ref[...] * pr_ref[3:4, :] + pr_ref[6:7, :]) + (
            m_ref[...].astype(F32) + t_ref[...].astype(F32)
        ) + pr_ref[1:2, :]
        n, r = norm(h)
        n_ref[...] = n
        r_ref[...] = r
        y = (n * pr_ref[4:5, :] + pr_ref[7:8, :]).astype(BF)
        y_ref[...] = y
        u = nn(y, w_ref[...]) + b_ref[...].astype(F32)
        phi = 0.5 * (1.0 + lax.erf(u * math.sqrt(0.5)))
        g = (u * phi).astype(BF)
        g_ref[...] = g
        density = jnp.exp(u * u * -0.5) * (1.0 / math.sqrt(2.0 * math.pi))
        d_ref[...] = (phi + u * density).astype(BF)
        part_ref[...] = nn(g, o_ref[...]).astype(BF)

    full = tiled((tile, width))
    wide = tiled((tile, hidden))
    return call(
        body,
        "ffn_forward",
        tokens // tile,
        [full, full, full, whole(params.shape), whole(in_w.shape), whole(in_b.shape),
         whole(out_w.shape)],
        [
            ((tokens, width), F32, full),
            ((tokens, 1), F32, tiled((tile, 1))),
            ((tokens, width), BF, full),
            ((tokens, hidden), BF, wide),
            ((tokens, hidden), BF, wide),
            ((tokens, width), BF, full),
        ],
        [],
        2 * tokens * width * 2 * hidden,
        tokens * width * 16 + tokens * hidden * 4 + width * hidden * 4,
    )(normed, mine, other, params, in_w, in_b, out_w)


def ffn_backward(side, normed, mine, other, params, cot, slope, in_w, out_w, tile):
    tokens, width = normed.shape
    hidden = in_w.shape[1]
    here = width // 2

    def body(side_ref, n2_ref, m_ref, t_ref, pr_ref, e_ref, d_ref, w_ref, o_ref,
             j_ref, dh_ref, dhb_ref, du_ref, part_ref, sum_ref, sumu_ref, wt, ot):
        @pl.when(pl.program_id(0) == 0)
        def _():
            wt[...] = w_ref[...].T
            ot[...] = o_ref[...].T
            sum_ref[...] = jnp.zeros_like(sum_ref)
            sumu_ref[...] = jnp.zeros_like(sumu_ref)

        h = (n2_ref[...] * pr_ref[4:5, :] + pr_ref[7:8, :]) + (
            m_ref[...].astype(F32) + t_ref[...].astype(F32)
        ) + pr_ref[2:3, :]
        n, r = norm(h)
        joined = n * pr_ref[5:6, :] + pr_ref[8:9, :]
        j_ref[...] = jnp.where(side_ref[0] == 0, joined[:, :here], joined[:, here:])
        e = e_ref[...].astype(F32)
        dh = norm_back(e, n, r, pr_ref[5:6, :])
        dh_ref[...] = dh
        dhb = dh.astype(BF)
        dhb_ref[...] = dhb
        sum_ref[0:1, :] += colsum(e * n)
        sum_ref[1:2, :] += colsum(e)
        sum_ref[2:3, :] += colsum(dh)
        dg = nn(dhb, ot[...]).astype(BF)
        du = dg.astype(F32) * d_ref[...].astype(F32)
        sumu_ref[0:1, :] += colsum(du)
        dub = du.astype(BF)
        du_ref[...] = dub
        part_ref[...] = nn(dub, wt[...]).astype(BF)

    full = tiled((tile, width))
    wide = tiled((tile, hidden))
    return call(
        body,
        "ffn_backward",
        tokens // tile,
        [full, full, full, whole(params.shape), full, wide, whole(in_w.shape), whole(out_w.shape)],
        [
            ((tokens, here), F32, tiled((tile, here))),
            ((tokens, width), F32, full),
            ((tokens, width), BF, full),
            ((tokens, hidden), BF, wide),
            ((tokens, width), BF, full),
            ((8, width), F32, whole((8, width))),
            ((8, hidden), F32, whole((8, hidden))),
        ],
        [pltpu.VMEM((hidden, width), BF), pltpu.VMEM((width, hidden), BF)],
        2 * tokens * width * 2 * hidden,
        tokens * width * 22 + tokens * hidden * 4 + width * hidden * 4,
        scalars=1,
    )(side, normed, mine, other, params, cot, slope, in_w, out_w)


def cross_backward(picks, grad, mine, other, params, normed, spread, query, keys, values,
                   query_w, out_w, tile, length, count, padded):
    tokens, width = grad.shape
    here = out_w.shape[0]
    rows = tile // length
    steps = tokens // tile
    tall = keys.shape[0]

    def body(pick, g_ref, m_ref, t_ref, pr_ref, n_ref, r_ref, q_ref, k_ref, v_ref, w_ref, o_ref,
             dh_ref, dhb_ref, dq_ref, part_ref, kv_ref, sum_ref,
             wt, ot, q32, c32, dq32, dk_acc, dv_acc):
        @pl.when(pl.program_id(0) == 0)
        def _():
            wt[...] = w_ref[...].T
            ot[...] = o_ref[...].T
            sum_ref[...] = jnp.zeros_like(sum_ref)
            dk_acc[...] = jnp.zeros_like(dk_acc)
            dv_acc[...] = jnp.zeros_like(dv_acc)

        e = g_ref[...] + (m_ref[...].astype(F32) + t_ref[...].astype(F32))
        n = n_ref[...]
        dh = norm_back(e, n, r_ref[...], pr_ref[4:5, :])
        dh_ref[...] = dh
        dhb = dh.astype(BF)
        dhb_ref[...] = dhb
        sum_ref[0:1, :] += colsum(e * n)
        sum_ref[1:2, :] += colsum(e)
        sum_ref[2:3, :] += colsum(dh)
        c32[...] = nn(dhb, ot[...])
        q32[...] = q_ref[...].astype(F32)
        base = pl.program_id(0) * rows
        for j in range(rows):
            at = pl.multiple_of(pick[base + j] * padded, padded)
            for lo, span in quads(here):
                here_rows = slice(j * length, (j + 1) * length)
                cols = slice(lo, lo + span)
                qs = stacked(q32[here_rows, cols], span)
                cs = stacked(c32[here_rows, cols], span)
                k = k_ref[pl.ds(at, padded), cols]
                s = nt(k, qs) * SCALE
                live = lax.broadcasted_iota(jnp.int32, s.shape, 0) < count
                p = softmax_cols(jnp.where(live, s, -1e30))
                dp = nt(v_ref[pl.ds(at, padded), cols], cs)
                ds = (p * (dp - jnp.sum(dp * p, axis=0, keepdims=True))).astype(BF)
                dv_acc[pl.ds(at, padded), cols] += nn(p.astype(BF), cs)
                dk_acc[pl.ds(at, padded), cols] += nn(ds, qs) * SCALE
                dq32[here_rows, cols] = unstacked(tn(ds, k), span, length) * SCALE
        dq = dq32[...]
        sum_ref[3:4, :here] += colsum(dq)
        dqb = dq.astype(BF)
        dq_ref[...] = dqb
        part_ref[...] = nn(dqb, wt[...]).astype(BF)

        @pl.when(pl.program_id(0) == steps - 1)
        def _():
            def step(i, total):
                at = pl.ds(pl.multiple_of(i * padded, padded), padded)
                kv_ref[at, :here] = dk_acc[at, :].astype(BF)
                dv = dv_acc[at, :]
                kv_ref[at, here:] = dv.astype(BF)
                return total + colsum(dv)

            total = lax.fori_loop(0, tall // padded, step, jnp.zeros((1, here), F32))
            sum_ref[3:4, here:] = total

    full = tiled((tile, width))
    half = tiled((tile, here))
    return call(
        body,
        "cross_backward",
        steps,
        [full, full, full, whole(params.shape), full, tiled((tile, 1)), half, whole(keys.shape),
         whole(values.shape), whole(query_w.shape), whole(out_w.shape)],
        [
            ((tokens, width), F32, full),
            ((tokens, width), BF, full),
            ((tokens, here), BF, half),
            ((tokens, width), BF, full),
            ((tall, 2 * here), BF, whole((tall, 2 * here))),
            ((8, width), F32, whole((8, width))),
        ],
        [pltpu.VMEM((here, width), BF), pltpu.VMEM((width, here), BF)]
        + [pltpu.VMEM((tile, here), F32)] * 3
        + [pltpu.VMEM((tall, here), F32)] * 2,
        2 * tokens * width * 2 * here + 10 * tokens * padded * here * 4,
        tokens * width * 20 + keys.size * 8,
        scalars=1,
    )(picks, grad, mine, other, params, normed, spread, query, keys, values, query_w, out_w)


def self_backward(side, grad, mine, other, params, normed, spread, qkv, qkv_w, out_w,
                  ids_col, ids_row, tile):
    tokens, width = grad.shape
    here = out_w.shape[0]

    def body(side_ref, g_ref, m_ref, t_ref, pr_ref, n_ref, r_ref, q_ref, w_ref, o_ref,
             ic_ref, ir_ref, dhb_ref, dq_ref, keep_ref, send_ref, sum_ref, wt, ot):
        @pl.when(pl.program_id(0) == 0)
        def _():
            for s in range(3):
                wt[s * here : (s + 1) * here, :] = w_ref[s].T
            ot[...] = o_ref[...].T
            sum_ref[...] = jnp.zeros_like(sum_ref)

        e = g_ref[...] + (m_ref[...].astype(F32) + t_ref[...].astype(F32))
        n = n_ref[...]
        dh = norm_back(e, n, r_ref[...], pr_ref[3:4, :])
        dhb = dh.astype(BF)
        dhb_ref[...] = dhb
        sum_ref[0:1, :] += colsum(e * n)
        sum_ref[1:2, :] += colsum(e)
        sum_ref[2:3, :] += colsum(dh)
        dc = nn(dhb, ot[...]).astype(BF)
        same = ic_ref[...] == ir_ref[0]
        grads = [[], [], []]
        for p in range(here // 128):
            q = q_ref[:, 128 * p : 128 * p + 128]
            k = q_ref[:, here + 128 * p : here + 128 * p + 128]
            v = q_ref[:, 2 * here + 128 * p : 2 * here + 128 * p + 128]
            c = dc[:, 128 * p : 128 * p + 128]
            sums = [None, None, None]
            for a in range(2):
                mask = head_mask(128, a, BF)
                qm = q * mask
                cm = c * mask
                s = jnp.where(same, nt(k, qm) * SCALE, BIG_NEG)
                pt = softmax_cols(s)
                dp = nt(v, cm)
                ds = (pt * (dp - jnp.sum(dp * pt, axis=0, keepdims=True))).astype(BF)
                new = (tn(ds, k * mask), nn(ds, qm), nn(pt.astype(BF), cm))
                sums = [b if a_ is None else a_ + b for a_, b in zip(sums, new)]
            grads[0].append(sums[0] * SCALE)
            grads[1].append(sums[1] * SCALE)
            grads[2].append(sums[2])
        dq, dk, dv = (jnp.concatenate(g, axis=1) for g in grads)
        sum_ref[3:4, :here] += colsum(dq)
        sum_ref[3:4, here:] += colsum(dv)
        dqkv = jnp.concatenate((dq, dk, dv), axis=1).astype(BF)
        dq_ref[...] = dqkv
        part = nn(dqkv, wt[...])
        first = side_ref[0] == 0
        keep_ref[...] = jnp.where(
            first, dh[:, :here] + part[:, :here], dh[:, here:] + part[:, here:]
        )
        send_ref[...] = jnp.where(first, part[:, here:], part[:, :here]).astype(BF)

    full = tiled((tile, width))
    half = tiled((tile, here))
    return call(
        body,
        "self_backward",
        tokens // tile,
        [full, full, full, whole(params.shape), full, tiled((tile, 1)), tiled((tile, 3 * here)),
         whole(qkv_w.shape), whole(out_w.shape), tiled((tile, 1)), tiled((1, 1, tile))],
        [
            ((tokens, width), BF, full),
            ((tokens, 3 * here), BF, tiled((tile, 3 * here))),
            ((tokens, here), F32, half),
            ((tokens, here), BF, half),
            ((8, width), F32, whole((8, width))),
        ],
        [pltpu.VMEM((3 * here, width), BF), pltpu.VMEM((width, here), BF)],
        2 * tokens * width * 4 * here + 10 * tokens * tile * here,
        tokens * width * 16 + 8 * width * here,
        scalars=1,
    )(side, grad, mine, other, params, normed, spread, qkv, qkv_w, out_w, ids_col, ids_row)


def patch_send(side, pair, cross_kv, images, count, padded):
    width = cross_kv.shape[2]
    visual = cross_kv.shape[1]
    half = visual // 2
    group = 5

    def body(side_ref, p_ref, w_ref, s_ref, wt):
        @pl.when(pl.program_id(0) == 0)
        def _():
            wt[:width, :] = w_ref[0].T
            wt[width:, :] = w_ref[1].T

        out = nn(p_ref[...], wt[...])
        for i in range(group):
            s_ref[i] = out[padded * i : padded * i + count].astype(BF)

    return call(
        body,
        "patch_send",
        images // group,
        [
            tiled((group * padded, 2 * width)),
            pl.BlockSpec((2, half, width), lambda i, s: (0, 1 - s[0], 0), pipeline_mode=pl.Buffered(1)),
        ],
        [((images, count, half), BF, tiled((group, count, half)))],
        [pltpu.VMEM((2 * width, half), BF)],
        2 * images * padded * half * 2 * width,
        images * padded * (2 * width + half) * 2,
        scalars=1,
    )(side, pair, cross_kv)[0]


def patch_keep(side, pair, cross_kv, arrived, padded):
    images, count, half = arrived.shape
    width = cross_kv.shape[2]
    group = 5

    def body(side_ref, p_ref, w_ref, a_ref, o_ref, wt):
        @pl.when(pl.program_id(0) == 0)
        def _():
            wt[:width, :] = w_ref[0].T
            wt[width:, :] = w_ref[1].T

        out = nn(p_ref[...], wt[...])
        for i in range(group):
            o_ref[i] = out[padded * i : padded * i + count] + a_ref[i].astype(F32)

    return call(
        body,
        "patch_keep",
        images // group,
        [
            tiled((group * padded, 2 * width)),
            pl.BlockSpec((2, half, width), lambda i, s: (0, s[0], 0), pipeline_mode=pl.Buffered(1)),
            tiled((group, count, half)),
        ],
        [((images, count, half), F32, tiled((group, count, half)))],
        [pltpu.VMEM((2 * width, half), BF)],
        2 * images * padded * half * 2 * width,
        images * padded * (2 * width + half * 3) * 2,
        scalars=1,
    )(side, pair, cross_kv, arrived)[0]


def shards_of(bit, count):
    return [i for i in range(count) if not (i >> bit) & 1]


def split_rows(acc, send_ref, keep_ref, bits_ref, bit, shards, size):
    mine = bits_ref[bit]
    for slot, shard in enumerate(shards_of(bit, shards)):
        kept = pl.multiple_of((shard + (mine << bit)) * size, size)
        sent = pl.multiple_of((shard + ((1 - mine) << bit)) * size, size)
        keep_ref[slot] = acc[pl.ds(kept, size), :].astype(BF)
        send_ref[slot] = acc[pl.ds(sent, size), :].astype(BF)


def split_outside(full, bit, shards, bits):
    size = full.shape[0] // shards
    inner = 1 << bit
    view = full.reshape(shards // (2 * inner), 2, inner, size, full.shape[1])
    return [
        lax.dynamic_index_in_dim(view, at, 1, keepdims=False).reshape(
            shards // 2, size, full.shape[1]
        )
        for at in (1 - bits[bit], bits[bit])
    ]


def grad_weight(bits, groups, shards, name, tile):
    tokens, width = groups[0][1][0][0].shape
    size = width // shards
    inside = size % 16 == 0
    terms, specs, outs, operands = [], [], [], []
    at = 0
    for number, (bit, members) in enumerate(groups):
        first = at
        for left, right, column, columns in members:
            terms.append((at, columns // tile, number, bit))
            operands += [left, right]
            specs += [
                whole(left.shape),
                pl.BlockSpec(
                    (tokens, tile),
                    lambda i, *_, a=at, n=columns // tile, c=column // tile: (
                        0, c + jnp.clip(i - a, 0, n - 1)),
                ),
            ]
            at += columns // tile
        span = at - first
        if inside:
            for _ in range(2):
                outs.append((
                    (shards // 2, size, span * tile), BF,
                    pl.BlockSpec(
                        (shards // 2, size, tile),
                        lambda i, *_, a=first, n=span: (0, 0, jnp.clip(i - a, 0, n - 1)),
                    ),
                ))
        else:
            outs.append((
                (width, span * tile), BF,
                pl.BlockSpec(
                    (width, tile),
                    lambda i, *_, a=first, n=span: (0, jnp.clip(i - a, 0, n - 1)),
                ),
            ))
    total = at

    def body(bits_ref, *refs):
        ins = refs[: len(operands)]
        results = refs[len(operands) : -2]
        lt, acc = refs[-2:]
        step = pl.program_id(0)
        for which, (start, count, number, bit) in enumerate(terms):
            l_ref, r_ref = ins[2 * which : 2 * which + 2]

            if which == 0 or operands[2 * which] is not operands[2 * which - 2]:
                @pl.when(step == start)
                def _(l_ref=l_ref):
                    lt[...] = l_ref[...].T

            @pl.when((step >= start) & (step < start + count))
            def _(r_ref=r_ref, number=number, bit=bit):
                acc[...] = nn(lt[...], r_ref[...])
                if inside:
                    split_rows(acc, results[2 * number], results[2 * number + 1], bits_ref, bit,
                               shards, size)
                else:
                    results[number][...] = acc[...].astype(BF)

    made = call(
        body,
        name,
        total,
        specs,
        outs,
        [pltpu.VMEM((width, tokens), BF), pltpu.VMEM((width, tile), F32)],
        2 * tokens * width * total * tile,
        tokens * (width + total * tile) * 2 + width * total * tile * 2,
        scalars=1,
    )(bits, *operands)
    if inside:
        return [made[2 * i : 2 * i + 2] for i in range(len(groups))]
    return [split_outside(m, g[0], shards, bits) for m, g in zip(made, groups)]


def grad_weight_patches(bits, patches, pair, padded, shards, bit):
    images, count, visual = patches.shape
    size = visual // shards
    wide = pair.shape[1]
    group = 5
    steps = images // group
    inside = size % 16 == 0

    def body(bits_ref, p_ref, g_ref, *refs):
        rows, acc = refs[-2:]
        at = pl.program_id(0)

        @pl.when(at == 0)
        def _():
            rows[...] = jnp.zeros_like(rows)

        for i in range(group):
            rows[padded * i : padded * i + count, :] = p_ref[i]
        new = tn(rows[...], g_ref[...])

        @pl.when(at == 0)
        def _():
            acc[...] = new

        @pl.when(at > 0)
        def _():
            acc[...] += new

        @pl.when(at == steps - 1)
        def _():
            if inside:
                split_rows(acc, refs[0], refs[1], bits_ref, bit, shards, size)
            else:
                refs[0][...] = acc[...].astype(BF)

    half = (shards // 2, size, wide)
    full = (visual, wide)
    made = call(
        body,
        "grad_weight_patches",
        steps,
        [tiled((group, count, visual)), tiled((group * padded, wide))],
        [(half, BF, whole(half))] * 2 if inside else [(full, BF, whole(full))],
        [pltpu.VMEM((group * padded, visual), BF), pltpu.VMEM((visual, wide), F32)],
        2 * images * padded * visual * wide,
        patches.size * 2 + pair.size * 2 + visual * wide * 2,
        scalars=1,
    )(bits, patches, pair)
    return made if inside else split_outside(made[0], bit, shards, bits)


def swap_dp(value, bit, shards):
    return lax.ppermute(value, "dp", [(i, i ^ (1 << bit)) for i in range(shards)])


def add_pair(keep, arrived):
    return keep.astype(F32) + arrived.astype(F32)


def split_next(total, position, mine):
    lead = total.shape[0]
    inner = 1 << position
    view = total.reshape((lead // (2 * inner), 2, inner) + total.shape[1:])
    send = lax.dynamic_index_in_dim(view, 1 - mine, 1, keepdims=False)
    keep = lax.dynamic_index_in_dim(view, mine, 1, keepdims=False)
    shape = (lead // 2,) + total.shape[1:]
    return send.reshape(shape).astype(BF), keep.reshape(shape).astype(BF)


class Sum:
    def __init__(self, first, second, join, bits, shards):
        self.bits, self.shards, self.join = bits, shards, join
        self.keep = [first[1], second[1]]
        self.sent = [swap_dp(first[0], 0, shards), swap_dp(second[0], 1, shards)]
        self.bit = 1

    def step(self, *behind):
        arrived = after(self.sent, behind)
        totals = [add_pair(k, a) for k, a in zip(self.keep, arrived)]
        bit, bits, shards = self.bit, self.bits, self.shards
        if bit == 1:
            pairs = [split_next(t, 0, bits[b]) for t, b in zip(totals, (1, 0))]
            self.keep = [keep for _, keep in pairs]
            self.sent = [swap_dp(send, b, shards) for (send, _), b in zip(pairs, (1, 0))]
        else:
            total = totals[0]
            if bit == 2:
                total = jnp.concatenate(totals, axis=self.join)
            if total.shape[0] == 1:
                return total[0]
            send, keep = split_next(total, 0, bits[bit])
            self.keep, self.sent = [keep], [swap_dp(send, bit, shards)]
        self.bit += 1
        return None

    def finish(self):
        done = None
        while done is None:
            done = self.step()
        return done


def after(values, behind):
    if not behind:
        return values
    return lax.optimization_barrier((values, behind))[0]


def sum_dp(value, shards):
    bit = 0
    while (1 << bit) < shards:
        value = value + swap_dp(value, bit, shards)
        bit += 1
    return value


def swap_mp(value):
    return lax.ppermute(value, "mp", [(0, 1), (1, 0)])


def local(
    shards,
    text,
    patches,
    segment_ids,
    row_image,
    self_qkv,
    self_bias,
    self_out,
    cross_query,
    cross_bias,
    cross_kv,
    cross_out,
    ffn_in,
    ffn_in_bias,
    ffn_out,
    branch_bias,
    norm_gain,
    norm_bias,
    cotangent,
):
    rows, length = segment_ids.shape
    images, count, visual = patches.shape
    tokens, here = text.shape
    padded = -(-count // 32) * 32
    tile = 5 * length
    hidden = ffn_in.shape[1]
    dp_at = lax.axis_index("dp")
    mp_at = lax.axis_index("mp")
    side = mp_at.reshape(1).astype(jnp.int32)
    bit_count = max(2, shards.bit_length() - 1)
    bits = (dp_at >> jnp.arange(bit_count, dtype=jnp.int32)) & 1
    bits = bits.astype(jnp.int32)
    bit_at = [(dp_at >> b) & 1 for b in range(bit_count)]

    def both(own):
        other = swap_mp(own)
        return jnp.where(
            mp_at == 0,
            jnp.concatenate((own, other), axis=1),
            jnp.concatenate((other, own), axis=1),
        )

    text_full = both(text)
    params = both(jnp.concatenate((branch_bias, norm_gain, norm_bias), axis=0)).astype(F32)
    cot_full = both(cotangent)

    picks = (row_image - dp_at * images).astype(jnp.int32)
    ids = segment_ids + 32 * (jnp.arange(rows, dtype=jnp.int32) % (tile // length))[:, None]
    ids_col = ids.reshape(tokens, 1)
    ids_row = ids.reshape(tokens // tile, 1, tile)
    zero = jnp.zeros((here,), F32)
    qkv_b = jnp.concatenate((self_bias[0].astype(F32), zero, self_bias[1].astype(F32)))[None]

    keys, values = project_patches(patches, cross_kv, cross_bias, padded)
    qkv, context, part_one = self_forward(
        text_full, self_qkv, qkv_b, self_out, ids_col, ids_row, tile
    )
    n_one, r_one, y_one, query, cross_ctx, part_two = cross_forward(
        picks, text_full, part_one, swap_mp(part_one), params, cross_query, cross_bias,
        keys, values, cross_out, tile, length, count, padded,
    )
    n_two, r_two, y_two, act, slope, part_three = ffn_forward(
        n_one, part_two, swap_mp(part_two), params, ffn_in, ffn_in_bias[None], ffn_out, tile
    )
    joined, dh_three, dhb_three, du, part_four, sums_three, sums_hidden = ffn_backward(
        side, n_two, part_three, swap_mp(part_three), params, cot_full, slope, ffn_in, ffn_out,
        tile,
    )
    other_four = swap_mp(part_four)
    ffn_groups = grad_weight(
        bits,
        [(0, [(dhb_three, act, 0, hidden)]), (1, [(y_two, du, 0, hidden)])],
        shards, "grad_ffn", 512,
    )
    ffn_sum = Sum(*ffn_groups, 2, bit_at, shards)

    part_four, _ = after([part_four, other_four], tuple(g[0] for g in ffn_groups))
    dh_two, dhb_two, dq_cross, part_five, pair, sums_two = cross_backward(
        picks, dh_three, part_four, other_four, params, n_two, r_two, query, keys, values,
        cross_query, cross_out, tile, length, count, padded,
    )
    other_five = swap_mp(part_five)
    ffn_sum.step(part_five)
    (out_pair,) = grad_weight(
        bits,
        [(0, [(dhb_two, cross_ctx, 0, here), (y_one, dq_cross, 0, here)])],
        shards, "grad_cross", here,
    )
    kv_pair = grad_weight_patches(bits, patches, pair, padded, shards, 1)
    cross_sum = Sum(out_pair, kv_pair, 1, bit_at, shards)
    ffn_sum.step(kv_pair[0])

    part_five, _ = after([part_five, other_five], (kv_pair[0],))
    dhb_one, dqkv, text_keep, text_send, sums_one = self_backward(
        side, dh_two, part_five, other_five, params, n_one, r_one, qkv, self_qkv, self_out,
        ids_col, ids_row, tile,
    )
    text_other = swap_mp(text_send)
    cross_sum.step(dhb_one)
    ffn_sum.step(dhb_one)
    self_groups = grad_weight(
        bits,
        [
            (0, [(text_full, dqkv, 0, 2 * here)]),
            (1, [(text_full, dqkv, 2 * here, here), (dhb_one, context, 0, here)]),
        ],
        shards, "grad_self", here,
    )
    self_sum = Sum(*self_groups, 2, bit_at, shards)
    cross_sum.step(self_groups[0][0])
    sent = patch_send(side, after([pair], (self_groups[0][0],))[0], cross_kv, images, count, padded)
    ffn_shard = ffn_sum.finish()
    arrived = swap_mp(sent)
    self_sum.step(sent)
    patch_grad = patch_keep(side, pair, cross_kv, arrived, padded)
    cross_shard = cross_sum.finish()
    self_shard = self_sum.finish()
    text_grad = text_keep + text_other.astype(F32)

    def mine(block):
        return jnp.where(mp_at == 0, block[:, :here], block[:, here:])

    smalls = jnp.concatenate(
        (
            mine(sums_one[:3]),
            mine(sums_two[:3]),
            mine(sums_three[:3]),
            sums_one[3].reshape(2, here),
            sums_two[3].reshape(2, here),
            sums_hidden[0].reshape(-1, here),
        ),
        axis=0,
    )
    smalls = sum_dp(smalls, shards)
    block = self_shard.shape[0]
    self_grad = jnp.stack([self_shard[:, i * here : (i + 1) * here] for i in range(3)])
    return (
        joined,
        text_grad,
        patch_grad,
        self_grad,
        smalls[9:11],
        self_shard[:, 3 * here :].T,
        cross_shard[:block, here:],
        smalls[11:13],
        jnp.stack((cross_shard[block:, :here], cross_shard[block:, here:])),
        cross_shard[:block, :here].T,
        ffn_shard[:, hidden:],
        smalls[13:].reshape(-1),
        ffn_shard[:, :hidden].T,
        jnp.stack((smalls[2], smalls[5], smalls[8])),
        jnp.stack((smalls[0], smalls[3], smalls[6])),
        jnp.stack((smalls[1], smalls[4], smalls[7])),
    )


def solution(mesh):
    return jax.shard_map(
        partial(local, mesh.shape["dp"]),
        mesh=mesh,
        in_specs=(
            P("dp", "mp"),
            P("dp", None, None),
            P("dp", None),
            P("dp"),
            P(None, None, "mp"),
            P(None, "mp"),
            P("mp", None),
            P(None, "mp"),
            P(None, "mp"),
            P(None, None, "mp"),
            P("mp", None),
            P(None, "mp"),
            P("mp"),
            P("mp", None),
            P(None, "mp"),
            P(None, "mp"),
            P(None, "mp"),
            P("dp", "mp"),
        ),
        out_specs=(
            P("dp", "mp"),
            P("dp", "mp"),
            P("dp", None, "mp"),
            P(None, "dp", "mp"),
            P(None, "mp"),
            P("mp", "dp"),
            P("dp", "mp"),
            P(None, "mp"),
            P(None, "dp", "mp"),
            P("mp", "dp"),
            P("dp", "mp"),
            P("mp"),
            P("mp", "dp"),
            P(None, "mp"),
            P(None, "mp"),
            P(None, "mp"),
        ),
        check_vma=False,
    )
```

time: 1520 us -> 300 us (0.20)
  waiting for transfers between devices: 883 us -> 42.7 us
  local copies, waits for them, and re-layouts: 219 us -> 20.2 us
  matrix products: 187 us -> 0 us
  Pallas kernels: 0 us -> 183 us
  blocking collectives: 93.2 us -> 0 us
  other arithmetic: 105 us -> 26.7 us
  starting transfers between devices: 2.27 us -> 24.3 us
  between operations: 16.7 us -> 1.13 us
    reduce_scatter x12 -> x0, waiting for transfers between devices: 729 us -> none  [the longest x1 142 us: local(): lax.psum_scatter(grad_ffn_in, 'dp', scatter_dimension=0, tiled=True)]
    dot_general x34 -> x0, matrix products: 187 us -> none  [the longest x5 33.5 us: product(): return jnp.dot(left, right, preferred_element_type=jnp.float32)]
    pallas_call x0 -> x13, Pallas kernels: none -> 183 us  [the longest x3 30.4 us: grad_weight(): call(body, name, total, specs, outs, [pltpu.VMEM((width, tokens), BF), pl...]
    unnamed x20 -> x0, waiting for transfers between devices: 98.8 us -> none
    psum x7 -> x0, blocking collectives: 93.2 us -> none  [the longest x1 78.4 us: local(): lax.psum((grad_self_bias, grad_cross_bias, jnp.sum(grad_hidden, axis=0),...]
    all_gather x6 -> x0, waiting for transfers between devices: 55.1 us -> none  [the longest x3 32.5 us: widen_grad(): return lax.all_gather(block, 'mp', axis=1, tiled=True)]
    another operation x21 -> x4, local copies, waits for them, and re-layouts: 43.4 us -> 0.04 us  [the longest x1 0.02 us: local(): jnp.stack((cross_shard[block:, :here], cross_shard[block:, here:]))]
    ppermute x0 -> x32, waiting for transfers between devices: none -> 42.7 us  [the longest x22 35.8 us: swap_dp(): return lax.ppermute(value, 'dp', [(i, i ^ 1 << bit) for i in range(shards)])]
  transfers between devices with their start and end apart: 19 -> 32, of which waited for: 16 -> 11; matrix products, arithmetic and copies ran while one was open for 18% -> 12% of each run, Pallas kernels for 0% -> 38%
where the time goes in v1:
time: 300 us; the launch traced here: 298 us
  Pallas kernels  183 us (61%)
  waiting for transfers between devices  42.7 us (14%)
  other arithmetic  26.7 us (9%)
  starting transfers between devices  24.3 us (8%)
  local copies, waits for them, and re-layouts  20.2 us (7%)
    ppermute x22, waiting for transfers between devices, swap_dp(): return lax.ppermute(value, 'dp', [(i, i ^ 1 << bit) for i in range(shards)])  35.8 us
    pallas_call x3, Pallas kernels, grad_weight(): call(body, name, total, specs, outs, [pltpu.VMEM((width, tokens), BF), pl...  30.4 us
    pallas_call x1, Pallas kernels, cross_backward(): call(body, 'cross_backward', steps, [full, full, full, whole(params.shape...  30 us
    ppermute x22, starting transfers between devices, swap_dp(): return lax.ppermute(value, 'dp', [(i, i ^ 1 << bit) for i in range(shards)])  22.2 us
    pallas_call x1, Pallas kernels, self_backward(): call(body, 'self_backward', tokens // tile, [full, full, full, whole(para...  19.9 us
    pallas_call x1, Pallas kernels, cross_forward(): call(body, 'cross_forward', tokens // tile, [full, full, full, whole(para...  19.4 us
    pallas_call x1, Pallas kernels, ffn_backward(): call(body, 'ffn_backward', tokens // tile, [full, full, full, whole(param...  15 us
    pallas_call x1, Pallas kernels, grad_weight_patches(): call(body, 'grad_weight_patches', steps, [tiled((group, count, visual)),...  14.9 us
  transfers between devices with their start and end apart: 32, of which 11 were waited for; matrix products, arithmetic and copies ran while one was open for 12% of the time, Pallas kernels for 38%

profile of v1, /device:TPU:0, one launch (start us, length us, event | category | flops | bytes accessed | tf_op | source)
XLA Modules:
  0.0 298.5 jit_solution(9727077646881613690)
XLA Ops:
  1.2 0.8 broadcast_add_fusion
  2.6 1.0 reshape.224.ic_ref
  3.7 0.8 convert_reduce_fusion.1
  5.1 3.0 maximum_select_fusion.x_ref.refs_0_.refs_2_
  8.0 11.4 %self_forward.1 = (bf16[1000,1152]{1,0:T(8,128)(2,1)}, bf16[1000,384]{1,0:T(8,128)(2,1)}, bf16[1000,768]{1,0:T(8,128)(2,1)}) custom-call(bf16[1000,768]{1,0:T(8,128)(2,1)} %maximum_select_fusion.x_ref.refs_0_.refs_2_, bf16[3,768,384]{2,1,0:T(8,128)(2,1)} %w_ref.15, f32[1,1152]{1,0:T(1,128)} %broadcast_in_dim.11.b_ref, bf16[384,768]{1,0:T(8,128)(2,1)} %o_ref.11, ...), custom_call_target="tpu_custom_call" | custom-call | flops 2359296000 | bytes 8503296 | tf_op jit(solution)/shard_map/self_forward/pallas_call | solution.py:154
  20.0 11.2 %project_patches.1 = (bf16[4000,384]{1,0:T(8,128)(2,1)}, bf16[4000,384]{1,0:T(8,128)(2,1)}) custom-call(bf16[25,145,1024]{2,1,0:T(8,128)(2,1)} %p_ref.3, bf16[2,1024,384]{2,1,0:T(8,128)(2,1)} %w_ref.17, bf16[2,384]{1,0:T(2,128)(2,1)} %b_ref.3), custom_call_target="tpu_custom_call" | custom-call | flops 6291456000 | bytes 15140864 | tf_op jit(solution)/shard_map/project_patches/pallas_call | solution.py:113
  32.3 1.1 copy-done.7
  33.5 19.4 %cross_forward.1 = (f32[1000,768]{1,0:T(8,128)}, f32[1000,1]{1,0:T(8,128)}, bf16[1000,768]{1,0:T(8,128)(2,1)}, bf16[1000,384]{1,0:T(8,128)(2,1)}, bf16[1000,384]{1,0:T(8,128)(2,1)}, /*index=5*/bf16[1000,768]{1,0:T(8,128)(2,1)}) custom-call(s32[25]{0:T(128)} %broadcast_subtract_fusion.pick, bf16[1000,768]{1,0:T(8,128)(2,1)} %maximum_select_fusion.x_ref.refs_0_.refs_2_, ...), custom_call_target="tpu_custom_call" | custom-call | flops 2162688000 | bytes 16896000 | tf_op jit(solution)/shard_map/cross_forward/pallas_call | solution.py:228
  53.6 2.9 collective-permute-done.3.t_ref
  56.5 1.1 copy-done.22
  57.6 12.2 %ffn_forward.1 = (f32[1000,768]{1,0:T(8,128)}, f32[1000,1]{1,0:T(8,128)}, bf16[1000,768]{1,0:T(8,128)(2,1)}, bf16[1000,1536]{1,0:T(8,128)(2,1)}, bf16[1000,1536]{1,0:T(8,128)(2,1)}, /*index=5*/bf16[1000,768]{1,0:T(8,128)(2,1)}) custom-call(f32[1000,768]{1,0:T(8,128)} %get-tuple-element.80.n1_ref.n_ref, bf16[1000,768]{1,0:T(8,128)(2,1)} %get-tuple-element.81.m_ref, ...), custom_call_target="tpu_custom_call" | custom-call | flops 4718592000 | bytes 23150592 | tf_op jit(solution)/shard_map/ffn_forward/pallas_call | solution.py:273
  70.4 3.9 %collective-permute-done.5 = bf16[1000,384]{1,0:T(8,128)(2,1)S(1)} collective-permute-done((bf16[1000,384]{1,0:T(8,128)(2,1)S(1)}, bf16[1000,384]{1,0:T(8,128)(2,1)S(1)}, u32[]{:S(2)}, u32[]{:S(2)}) %collective-permute-start.5) | collective-permute-done | bytes 768032 | tf_op jit(solution)/shard_map/ppermute | solution.py:803
  74.3 1.5 maximum_select_fusion.1.e_ref
  75.9 1.1 copy-done.21
  77.0 15.0 %ffn_backward.1 = (f32[1000,384]{1,0:T(8,128)}, f32[1000,768]{1,0:T(8,128)}, bf16[1000,768]{1,0:T(8,128)(2,1)}, bf16[1000,1536]{1,0:T(8,128)(2,1)}, bf16[1000,76...) custom-call(s32[1]{0:T(128)} %bitcast.side_ref, f32[1000,768]{1,0:T(8,128)} %get-tuple-element.82.n2_ref.n_ref, ...), custom_call_target="tpu_custom_call" | custom-call | flops 4718592000 | bytes 27758592 | tf_op jit(solution)/shard_map/ffn_backward/pallas_call | solution.py:330
  92.8 13.0 %grad_ffn.1 = (bf16[8,48,1536]{2,1,0:T(8,128)(2,1)}, bf16[8,48,1536]{2,1,0:T(8,128)(2,1)}, bf16[8,48,1536]{2,1,0:T(8,128)(2,1)}, bf16[8,48,1536]{2,1,0:T(8,128)(2,1)}) custom-call(s32[4]{0:T(128)} %shift-right-arithmetic_and_fusion.bits_ref, bf16[1000,768]{1,0:T(8,128)(2,1)} %get-tuple-element.88.refs_0_, bf16[1000,1536]{1,0:T(8,128)(2,1)} %get-tuple-element.89.refs_1_, ...), custom_call_target="tpu_custom_call" | custom-call | flops 4718592000 | bytes 12398592 | tf_op jit(solution)/shard_map/grad_ffn/pallas_call | solution.py:670
  105.7 2.9 collective-permute-start.26
  108.6 1.5 collective-permute-start.27
  110.1 0.8 slice_reduce_fusion
  111.0 1.1 copy-done.5
  112.1 30.0 %cross_backward.1 = (f32[1000,768]{1,0:T(8,128)}, bf16[1000,768]{1,0:T(8,128)(2,1)}, bf16[1000,384]{1,0:T(8,128)(2,1)}, bf16[1000,768]{1,0:T(8,128)(2,1)}, bf16[4000,768]{1,0:T(8,128)(2,1)}, /*index=5*/f32[8,768]{1,0:T(8,128)}) custom-call(s32[25]{0:T(128)} %broadcast_subtract_fusion.pick, f32[1000,768]{1,0:T(8,128)} %get-tuple-element.86.g_ref, ...), custom_call_target="tpu_custom_call" | custom-call | flops 3637248000 | bytes 27648000 | tf_op jit(solution)/shard_map/cross_backward/pallas_call | solution.py:418
  142.2 0.8 slice_reduce_fusion.1
  143.0 2.0 convert_add_fusion.1
  145.0 0.9 fusion.2
  146.4 1.6 convert_add_fusion
  148.0 0.9 fusion.3
  149.0 7.0 %grad_cross.1 = (bf16[8,48,768]{2,1,0:T(8,128)(2,1)}, bf16[8,48,768]{2,1,0:T(8,128)(2,1)}) custom-call(s32[4]{0:T(128)} %shift-right-arithmetic_and_fusion.bits_ref, bf16[1000,768]{1,0:T(8,128)(2,1)} %get-tuple-element.120.refs_0_, bf16[1000,384]{1,0:T(8,128)(2,1)} %get-tuple-element.121.refs_1_, bf16[1000,768]{1,0:T(8,128)(2,1)} %get-tuple-element.122.refs_2_, ...), custom_call_target="tpu_custom_call" | custom-call | flops 1179648000 | bytes 4251648 | tf_op jit(solution)/shard_map/grad_cross/pallas_call | solution.py:670
  156.0 1.9 collective-permute-start.20
  157.9 14.9 %grad_weight_patches.1 = (bf16[8,64,768]{2,1,0:T(8,128)(2,1)}, bf16[8,64,768]{2,1,0:T(8,128)(2,1)}) custom-call(s32[4]{0:T(128)} %shift-right-arithmetic_and_fusion.bits_ref, bf16[25,145,1024]{2,1,0:T(8,128)(2,1)} %p_ref.3, bf16[4000,768]{1,0:T(8,128)(2,1)} %get-tuple-element.110.g_ref.p_ref), custom_call_target="tpu_custom_call" | custom-call | flops 6291456000 | bytes 15140864 | tf_op jit(solution)/shard_map/grad_weight_patches/pallas_call | solution.py:723
  172.8 1.5 collective-permute-start.21
  174.4 1.2 convert_add_fusion.5
  175.6 1.2 convert_add_fusion.6
  177.0 1.6 collective-permute-start.30
  178.6 1.2 copy-done.6
  179.8 19.9 %self_backward.1 = (bf16[1000,768]{1,0:T(8,128)(2,1)}, bf16[1000,1152]{1,0:T(8,128)(2,1)}, f32[1000,384]{1,0:T(8,128)}, bf16[1000,384]{1,0:T(8,128)(2,1)}, f32[8,768]{1,0:T(8,128)}) custom-call(s32[1]{0:T(128)} %bitcast.side_ref, f32[1000,768]{1,0:T(8,128)} %get-tuple-element.97.g_ref, bf16[1000,768]{1,0:T(8,128)(2,1)} %get-tuple-element.101.m_ref, ...), custom_call_target="tpu_custom_call" | custom-call | flops 3127296000 | bytes 14647296 | tf_op jit(solution)/shard_map/self_backward/pallas_call | solution.py:499
  199.7 0.8 slice_reduce_fusion.2
  200.5 0.7 slice_select_fusion.2
  202.1 10.4 %grad_self.1 = (bf16[8,48,768]{2,1,0:T(8,128)(2,1)}, bf16[8,48,768]{2,1,0:T(8,128)(2,1)}, bf16[8,48,768]{2,1,0:T(8,128)(2,1)}, bf16[8,48,768]{2,1,0:T(8,128)(2,1)}) custom-call(s32[4]{0:T(128)} %shift-right-arithmetic_and_fusion.bits_ref, bf16[1000,768]{1,0:T(8,128)(2,1)} %maximum_select_fusion.x_ref.refs_0_.refs_2_, ...), custom_call_target="tpu_custom_call" | custom-call | flops 2359296000 | bytes 6967296 | tf_op jit(solution)/shard_map/grad_self/pallas_call | solution.py:670
  212.5 1.4 collective-permute-start.10
  214.0 1.2 convert_add_fusion.4
  215.2 2.7 collective-permute-start.31
  218.4 8.3 %patch_send.1 = bf16[25,145,512]{2,1,0:T(8,128)(2,1)} custom-call(s32[1]{0:T(128)} %bitcast.side_ref, bf16[4000,768]{1,0:T(8,128)(2,1)} %get-tuple-element.110.g_ref.p_ref, bf16[2,1024,384]{2,1,0:T(8,128)(2,1)} %w_ref.17), custom_call_target="tpu_custom_call" | custom-call | flops 3145728000 | bytes 10240000 | tf_op jit(solution)/shard_map/patch_send/pallas_call | solution.py:535
  226.8 1.4 convert_add_fusion.2
  228.2 1.6 collective-permute-start.17
  229.8 1.2 convert_add_fusion.7
  231.0 1.4 collective-permute-done.17
  232.8 0.8 fusion.6
  233.6 2.7 collective-permute-done.18
  236.8 4.7 %collective-permute-done.19 = f32[17,384]{1,0:T(8,128)S(1)} collective-permute-done((f32[17,384]{1,0:T(8,128)S(1)}, f32[17,384]{1,0:T(8,128)S(1)}, u32[]{:S(2)}, u32[]{:S(2)}) %collective-permute-start.19) | collective-permute-done | bytes 26144 | tf_op jit(solution)/shard_map/ppermute | solution.py:738
  241.5 1.3 collective-permute-start.22
  245.9 0.8 slice_bitcast_fusion
  246.7 1.6 collective-permute-done.22
  248.3 4.9 %collective-permute-done.23 = bf16[4,64,768]{2,1,0:T(8,128)(2,1)S(1)} collective-permute-done((bf16[4,64,768]{2,1,0:T(8,128)(2,1)}, bf16[4,64,768]{2,1,0:T(8,128)(2,1)S(1)}, u32[]{:S(2)}, u32[]{:S(2)}) %collective-permute-start.23) | collective-permute-done | bytes 393248 | tf_op jit(solution)/shard_map/ppermute | solution.py:738
  253.3 1.0 convert_add_fusion.12
  255.6 1.6 convert_add_fusion.8
  257.8 1.2 collective-permute-start.12
  259.0 5.5 %collective-permute-done.24 = bf16[2,112,768]{2,1,0:T(8,128)(2,1)S(1)} collective-permute-done((bf16[2,112,768]{2,1,0:T(8,128)(2,1)S(1)}, bf16[2,112,768]{2,1,0:T(8,128)(2,1)S(1)}, u32[]{:S(2)}, u32[]{:S(2)}) %collective-permute-start.24) | collective-permute-done | bytes 344096 | tf_op jit(solution)/shard_map/ppermute | solution.py:738
  264.7 2.4 convert_add_fusion.3
  267.8 8.0 %collective-permute-done.25 = bf16[1,112,768]{2,1,0:T(8,128)(2,1)S(1)} collective-permute-done((bf16[1,112,768]{2,1,0:T(8,128)(2,1)S(1)}, bf16[1,112,768]{2,1,0:T(8,128)(2,1)S(1)}, u32[]{:S(2)}, u32[]{:S(2)}) %collective-permute-start.25) | collective-permute-done | bytes 172064 | tf_op jit(solution)/shard_map/ppermute | solution.py:738
  275.9 1.6 collective-permute-done.14
  279.1 5.2 %collective-permute-done.15 = bf16[1,48,1536]{2,1,0:T(8,128)(2,1)S(1)} collective-permute-done((bf16[1,48,1536]{2,1,0:T(8,128)(2,1)S(1)}, bf16[1,48,1536]{2,1,0:T(8,128)(2,1)S(1)}, u32[]{:S(2)}, u32[]{:S(2)}) %collective-permute-start.15) | collective-permute-done | bytes 147488 | tf_op jit(solution)/shard_map/ppermute | solution.py:738
  285.0 0.7 pad_maximum_fusion.3
  285.7 2.0 copy-done
  287.7 10.8 %patch_keep.1 = f32[25,145,512]{2,1,0:T(8,128)} custom-call(s32[1]{0:T(128)} %bitcast.side_ref, bf16[4000,768]{1,0:T(8,128)(2,1)} %get-tuple-element.110.g_ref.p_ref, bf16[2,1024,384]{2,1,0:T(8,128)(2,1)} %w_ref.17, bf16[25,145,512]{2,1,0:T(8,128)(2,1)} %copy-done), custom_call_target="tpu_custom_call" | custom-call | flops 3145728000 | bytes 18432000 | tf_op jit(solution)/shard_map/patch_keep/pallas_call | solution.py:566
  (135 shorter events, 16.8 us)
Async XLA Ops:
  0.6 4.4 %collective-permute-start = (bf16[1000,384]{1,0:T(8,128)(2,1)}, bf16[1000,384]{1,0:T(8,128)(2,1)S(1)}, u32[]{:S(2)}, u32[]{:S(2)}) collective-permute-start(bf16[1000,384]{1,0:T(8,128)(2,1)} %param.18), channel_id=1, source_target_pairs={{0,1},{1,0},{2,3},{3,2},{4,5},{5,4},{6,7},{7,6},{8,9},{9,8},{10,11... | collective-permute-start | bytes 2304008 | tf_op jit(solution)/shard_map/ppermute | solution.py:803
  8.0 11.4 %copy-start.15 = (bf16[3,384]{1,0:T(4,128)(2,1)S(1)}, bf16[3,384]{1,0:T(4,128)(2,1)}, u32[]{:S(2)}) copy-start(bf16[3,384]{1,0:T(4,128)(2,1)} %param.34) | copy-start | bytes 6916
  8.0 11.4 %copy-start.16 = (bf16[3,384]{1,0:T(4,128)(2,1)S(1)}, bf16[3,384]{1,0:T(4,128)(2,1)}, u32[]{:S(2)}) copy-start(bf16[3,384]{1,0:T(4,128)(2,1)} %param.33) | copy-start | bytes 6916
  8.0 11.4 %copy-start.17 = (bf16[3,384]{1,0:T(4,128)(2,1)S(1)}, bf16[3,384]{1,0:T(4,128)(2,1)}, u32[]{:S(2)}) copy-start(bf16[3,384]{1,0:T(4,128)(2,1)} %param.32) | copy-start | bytes 6916
  19.4 12.9 %collective-permute-start.1 = (bf16[1000,768]{1,0:T(8,128)(2,1)}, bf16[1000,768]{1,0:T(8,128)(2,1)S(1)}, u32[]{:S(2)}, u32[]{:S(2)}) collective-permute-start(bf16[1000,768]{1,0:T(8,128)(2,1)} %get-tuple-element.77.m_ref), channel_id=1, source_target_pairs={{0,1},{1,0},{2,3},{3,2},{4,5},{5,4},{6,7},{7,6},{8,9},{9,8},{10,11... | collective-permute-start | bytes 4608008 | tf_op jit(solution)/shard_map/ppermute | solution.py:803
  19.5 12.2 %collective-permute-start.2 = (bf16[9,384]{1,0:T(8,128)(2,1)S(1)}, bf16[9,384]{1,0:T(8,128)(2,1)S(1)}, u32[]{:S(2)}, u32[]{:S(2)}) collective-permute-start(bf16[9,384]{1,0:T(8,128)(2,1)S(1)} %pad_maximum_fusion.5), channel_id=1, source_target_pairs={{0,1},{1,0},{2,3},{3,2},{4,5},{5,4},{6,7},{7,6},{8,9},{9,8},{10,11... | collective-permute-start | bytes 20744 | tf_op jit(solution)/shard_map/ppermute | solution.py:803
  20.0 11.2 %copy-start.23 = (s32[25]{0:T(128)S(1)}, s32[25]{0:T(128)}, u32[]{:S(2)}) copy-start(s32[25]{0:T(128)} %param.21) | copy-start | bytes 304
  32.3 1.1 copy-start.7
  33.5 19.5 %copy-start.20 = (bf16[1536]{0:T(1024)(128)(2,1)S(1)}, bf16[1536]{0:T(1024)(128)(2,1)}, u32[]{:S(2)}) copy-start(bf16[1536]{0:T(1024)(128)(2,1)} %param.30) | copy-start | bytes 9220
  52.9 3.6 %collective-permute-start.3 = (bf16[1000,768]{1,0:T(8,128)(2,1)}, bf16[1000,768]{1,0:T(8,128)(2,1)S(1)}, u32[]{:S(2)}, u32[]{:S(2)}) collective-permute-start(bf16[1000,768]{1,0:T(8,128)(2,1)} %get-tuple-element.81.m_ref), channel_id=1, source_target_pairs={{0,1},{1,0},{2,3},{3,2},{4,5},{5,4},{6,7},{7,6},{8,9},{9,8},{10,11... | collective-permute-start | bytes 4608008 | tf_op jit(solution)/shard_map/ppermute | solution.py:803
  56.5 1.1 copy-start.22
  57.6 12.4 %copy-start.11 = (bf16[1000,384]{1,0:T(8,128)(2,1)S(1)}, bf16[1000,384]{1,0:T(8,128)(2,1)}, u32[]{:S(2)}) copy-start(bf16[1000,384]{1,0:T(8,128)(2,1)} %param.35) | copy-start | bytes 2304004
  69.8 6.0 %collective-permute-start.4 = (bf16[1000,768]{1,0:T(8,128)(2,1)}, bf16[1000,768]{1,0:T(8,128)(2,1)S(1)}, u32[]{:S(2)}, u32[]{:S(2)}) collective-permute-start(bf16[1000,768]{1,0:T(8,128)(2,1)} %get-tuple-element.83.m_ref), channel_id=1, source_target_pairs={{0,1},{1,0},{2,3},{3,2},{4,5},{5,4},{6,7},{7,6},{8,9},{9,8},{10,11... | collective-permute-start | bytes 4608008 | tf_op jit(solution)/shard_map/ppermute | solution.py:803
  70.0 4.3 %collective-permute-start.5 = (bf16[1000,384]{1,0:T(8,128)(2,1)S(1)}, bf16[1000,384]{1,0:T(8,128)(2,1)S(1)}, u32[]{:S(2)}, u32[]{:S(2)}) collective-permute-start(bf16[1000,384]{1,0:T(8,128)(2,1)S(1)} %copy-done.11), channel_id=1, source_target_pairs={{0,1},{1,0},{2,3},{3,2},{4,5},{5,4},{6,7},{7,6},{8,9},{9,8},{10,11... | collective-permute-start | bytes 2304008 | tf_op jit(solution)/shard_map/ppermute | solution.py:803
  75.9 1.2 copy-start.21
  92.0 18.9 %collective-permute-start.6 = (bf16[1000,768]{1,0:T(8,128)(2,1)}, bf16[1000,768]{1,0:T(8,128)(2,1)S(1)}, u32[]{:S(2)}, u32[]{:S(2)}) collective-permute-start(bf16[1000,768]{1,0:T(8,128)(2,1)} %get-tuple-element.94.m_ref), channel_id=1, source_target_pairs={{0,1},{1,0},{2,3},{3,2},{4,5},{5,4},{6,7},{7,6},{8,9},{9,8},{10,11... | collective-permute-start | bytes 4608008 | tf_op jit(solution)/shard_map/ppermute | solution.py:803
  92.7 18.2 %copy-start.19 = (f32[8,768]{1,0:T(8,128)S(1)}, f32[8,768]{1,0:T(8,128)}, u32[]{:S(2)}) copy-start(f32[8,768]{1,0:T(8,128)} %get-tuple-element.118) | copy-start | bytes 73732
  105.7 36.5 %collective-permute-start.26 = (bf16[8,48,1536]{2,1,0:T(8,128)(2,1)}, bf16[8,48,1536]{2,1,0:T(8,128)(2,1)}, u32[]{:S(2)}, u32[]{:S(2)}) collective-permute-start(bf16[8,48,1536]{2,1,0:T(8,128)(2,1)} %get-tuple-element.92), channel_id=1, source_target_pairs={{0,2},{2,0},{4,6},{6,4},{8,10},{10,8},{12,14},{14,12},{16,18},{18,... | collective-permute-start | bytes 3538952 | tf_op jit(solution)/shard_map/ppermute | solution.py:738
  108.6 33.6 %collective-permute-start.27 = (bf16[8,48,1536]{2,1,0:T(8,128)(2,1)}, bf16[8,48,1536]{2,1,0:T(8,128)(2,1)}, u32[]{:S(2)}, u32[]{:S(2)}) collective-permute-start(bf16[8,48,1536]{2,1,0:T(8,128)(2,1)} %get-tuple-element.93), channel_id=1, source_target_pairs={{0,4},{2,6},{4,0},{6,2},{8,12},{10,14},{12,8},{14,10},{16,20},{18,... | collective-permute-start | bytes 3538952 | tf_op jit(solution)/shard_map/ppermute | solution.py:738
  111.0 1.1 copy-start.5
  142.1 36.5 %collective-permute-start.7 = (bf16[1000,768]{1,0:T(8,128)(2,1)}, bf16[1000,768]{1,0:T(8,128)(2,1)S(1)}, u32[]{:S(2)}, u32[]{:S(2)}) collective-permute-start(bf16[1000,768]{1,0:T(8,128)(2,1)} %get-tuple-element.101.m_ref), channel_id=1, source_target_pairs={{0,1},{1,0},{2,3},{3,2},{4,5},{5,4},{6,7},{7,6},{8,9},{9,8},{10,11... | collective-permute-start | bytes 4608008 | tf_op jit(solution)/shard_map/ppermute | solution.py:803
  143.0 3.5 %copy-start.9 = (bf16[8,48,1536]{2,1,0:T(8,128)(2,1)S(1)}, bf16[8,48,1536]{2,1,0:T(8,128)(2,1)}, u32[]{:S(2)}) copy-start(bf16[8,48,1536]{2,1,0:T(8,128)(2,1)} %get-tuple-element.133) | copy-start | bytes 3538948
  145.9 28.4 %collective-permute-start.28 = (bf16[4,48,1536]{2,1,0:T(8,128)(2,1)}, bf16[4,48,1536]{2,1,0:T(8,128)(2,1)}, u32[]{:S(2)}, u32[]{:S(2)}) collective-permute-start(bf16[4,48,1536]{2,1,0:T(8,128)(2,1)} %fusion.2), channel_id=1, source_target_pairs={{0,4},{2,6},{4,0},{6,2},{8,12},{10,14},{12,8},{14,10},{16,20},{18,... | collective-permute-start | bytes 1769480 | tf_op jit(solution)/shard_map/ppermute | solution.py:738
  148.9 25.5 %collective-permute-start.29 = (bf16[4,48,1536]{2,1,0:T(8,128)(2,1)}, bf16[4,48,1536]{2,1,0:T(8,128)(2,1)}, u32[]{:S(2)}, u32[]{:S(2)}) collective-permute-start(bf16[4,48,1536]{2,1,0:T(8,128)(2,1)} %fusion.3), channel_id=1, source_target_pairs={{0,2},{2,0},{4,6},{6,4},{8,10},{10,8},{12,14},{14,12},{16,18},{18,... | collective-permute-start | bytes 1769480 | tf_op jit(solution)/shard_map/ppermute | solution.py:738
  156.0 62.0 %collective-permute-start.20 = (bf16[8,48,768]{2,1,0:T(8,128)(2,1)}, bf16[8,48,768]{2,1,0:T(8,128)(2,1)}, u32[]{:S(2)}, u32[]{:S(2)}) collective-permute-start(bf16[8,48,768]{2,1,0:T(8,128)(2,1)} %get-tuple-element.125), channel_id=1, source_target_pairs={{0,2},{2,0},{4,6},{6,4},{8,10},{10,8},{12,14},{14,12},{16,18},{18,... | collective-permute-start | bytes 1769480 | tf_op jit(solution)/shard_map/ppermute | solution.py:738
  157.9 16.4 %copy-start.18 = (f32[8,768]{1,0:T(8,128)S(1)}, f32[8,768]{1,0:T(8,128)}, u32[]{:S(2)}) copy-start(f32[8,768]{1,0:T(8,128)} %get-tuple-element.117) | copy-start | bytes 73732
  172.8 45.6 %collective-permute-start.21 = (bf16[8,64,768]{2,1,0:T(8,128)(2,1)}, bf16[8,64,768]{2,1,0:T(8,128)(2,1)}, u32[]{:S(2)}, u32[]{:S(2)}) collective-permute-start(bf16[8,64,768]{2,1,0:T(8,128)(2,1)} %get-tuple-element.100), channel_id=1, source_target_pairs={{0,4},{2,6},{4,0},{6,2},{8,12},{10,14},{12,8},{14,10},{16,20},{18,... | collective-permute-start | bytes 2359304 | tf_op jit(solution)/shard_map/ppermute | solution.py:738
  177.0 25.2 %collective-permute-start.30 = (bf16[2,48,3072]{2,1,0:T(8,128)(2,1)S(1)}, bf16[2,48,3072]{2,1,0:T(8,128)(2,1)}, u32[]{:S(2)}, u32[]{:S(2)}) collective-permute-start(bf16[2,48,3072]{2,1,0:T(8,128)(2,1)S(1)} %fusion), channel_id=1, source_target_pairs={{0,8},{2,10},{4,12},{6,14},{8,0},{10,2},{12,4},{14,6},{16,24},{18,... | collective-permute-start | bytes 1769480 | tf_op jit(solution)/shard_map/ppermute | solution.py:738
  178.6 1.2 copy-start.6
  201.5 26.7 %collective-permute-start.16 = (f32[17,384]{1,0:T(8,128)S(1)}, f32[17,384]{1,0:T(8,128)S(1)}, u32[]{:S(2)}, u32[]{:S(2)}) collective-permute-start(f32[17,384]{1,0:T(8,128)S(1)} %concatenate.45), channel_id=1, source_target_pairs={{0,2},{2,0},{4,6},{6,4},{8,10},{10,8},{12,14},{14,12},{16,18},{18,... | collective-permute-start | bytes 78344 | tf_op jit(solution)/shard_map/ppermute | solution.py:738
  212.5 42.3 %collective-permute-start.10 = (bf16[8,48,768]{2,1,0:T(8,128)(2,1)}, bf16[8,48,768]{2,1,0:T(8,128)(2,1)}, u32[]{:S(2)}, u32[]{:S(2)}) collective-permute-start(bf16[8,48,768]{2,1,0:T(8,128)(2,1)} %get-tuple-element.109), channel_id=1, source_target_pairs={{0,2},{2,0},{4,6},{6,4},{8,10},{10,8},{12,14},{14,12},{16,18},{18,... | collective-permute-start | bytes 1769480 | tf_op jit(solution)/shard_map/ppermute | solution.py:738
  215.2 30.0 %collective-permute-start.31 = (bf16[1,48,3072]{2,1,0:T(8,128)(2,1)S(1)}, bf16[1,48,3072]{2,1,0:T(8,128)(2,1)S(1)}, u32[]{:S(2)}, u32[]{:S(2)}) collective-permute-start(bf16[1,48,3072]{2,1,0:T(8,128)(2,1)S(1)} %dynamic-slice_convert_fusion.2), channel_id=1, source_target_pairs={{0,16},{2,18},{4,20},{6,22},{8,24},{10,26},{12,28},{14,30},{16,0},... | collective-permute-start | bytes 884744 | tf_op jit(solution)/shard_map/ppermute | solution.py:738
  217.9 36.9 %collective-permute-start.11 = (bf16[8,48,768]{2,1,0:T(8,128)(2,1)}, bf16[8,48,768]{2,1,0:T(8,128)(2,1)}, u32[]{:S(2)}, u32[]{:S(2)}) collective-permute-start(bf16[8,48,768]{2,1,0:T(8,128)(2,1)} %get-tuple-element.112), channel_id=1, source_target_pairs={{0,4},{2,6},{4,0},{6,2},{8,12},{10,14},{12,8},{14,10},{16,20},{18,... | collective-permute-start | bytes 1769480 | tf_op jit(solution)/shard_map/ppermute | solution.py:738
  218.4 8.3 %copy-start.10 = (bf16[8,64,768]{2,1,0:T(8,128)(2,1)S(1)}, bf16[8,64,768]{2,1,0:T(8,128)(2,1)}, u32[]{:S(2)}) copy-start(bf16[8,64,768]{2,1,0:T(8,128)(2,1)} %get-tuple-element.127) | copy-start | bytes 2359300
  218.4 46.3 %collective-permute-start.8 = (bf16[1000,384]{1,0:T(8,128)(2,1)}, bf16[1000,384]{1,0:T(8,128)(2,1)}, u32[]{:S(2)}, u32[]{:S(2)}) collective-permute-start(bf16[1000,384]{1,0:T(8,128)(2,1)} %get-tuple-element.105), channel_id=1, source_target_pairs={{0,1},{1,0},{2,3},{3,2},{4,5},{5,4},{6,7},{7,6},{8,9},{9,8},{10,11... | collective-permute-start | bytes 2304008 | tf_op jit(solution)/shard_map/ppermute | solution.py:803
  226.8 3.0 %copy-start.14 = (bf16[8,48,768]{2,1,0:T(8,128)(2,1)S(1)}, bf16[8,48,768]{2,1,0:T(8,128)(2,1)}, u32[]{:S(2)}) copy-start(bf16[8,48,768]{2,1,0:T(8,128)(2,1)} %get-tuple-element.124) | copy-start | bytes 1769476
  228.1 8.6 %copy-start.1 = (bf16[8,64,768]{2,1,0:T(8,128)(2,1)}, bf16[8,64,768]{2,1,0:T(8,128)(2,1)S(1)}, u32[]{:S(2)}) copy-start(bf16[8,64,768]{2,1,0:T(8,128)(2,1)S(1)} %convert_add_fusion.2) | copy-start | bytes 2359300
  228.2 4.2 %collective-permute-start.17 = (f32[17,384]{1,0:T(8,128)S(1)}, f32[17,384]{1,0:T(8,128)S(1)}, u32[]{:S(2)}, u32[]{:S(2)}) collective-permute-start(f32[17,384]{1,0:T(8,128)S(1)} %add.158), channel_id=1, source_target_pairs={{0,4},{2,6},{4,0},{6,2},{8,12},{10,14},{12,8},{14,10},{16,20},{18,... | collective-permute-start | bytes 78344 | tf_op jit(solution)/shard_map/ppermute | solution.py:738
  231.0 10.5 %copy-start.3 = (bf16[8,48,768]{2,1,0:T(8,128)(2,1)}, bf16[8,48,768]{2,1,0:T(8,128)(2,1)S(1)}, u32[]{:S(2)}) copy-start(bf16[8,48,768]{2,1,0:T(8,128)(2,1)S(1)} %convert_add_fusion.7) | copy-start | bytes 1769476
  232.4 4.0 %collective-permute-start.18 = (f32[17,384]{1,0:T(8,128)S(1)}, f32[17,384]{1,0:T(8,128)S(1)}, u32[]{:S(2)}, u32[]{:S(2)}) collective-permute-start(f32[17,384]{1,0:T(8,128)S(1)} %add.159), channel_id=1, source_target_pairs={{0,8},{2,10},{4,12},{6,14},{8,0},{10,2},{12,4},{14,6},{16,24},{18,... | collective-permute-start | bytes 78344 | tf_op jit(solution)/shard_map/ppermute | solution.py:738
  236.4 5.1 %collective-permute-start.19 = (f32[17,384]{1,0:T(8,128)S(1)}, f32[17,384]{1,0:T(8,128)S(1)}, u32[]{:S(2)}, u32[]{:S(2)}) collective-permute-start(f32[17,384]{1,0:T(8,128)S(1)} %add.160), channel_id=1, source_target_pairs={{0,16},{2,18},{4,20},{6,22},{8,24},{10,26},{12,28},{14,30},{16,0},... | collective-permute-start | bytes 78344 | tf_op jit(solution)/shard_map/ppermute | solution.py:738
  241.5 6.8 %collective-permute-start.22 = (bf16[4,48,768]{2,1,0:T(8,128)(2,1)S(1)}, bf16[4,48,768]{2,1,0:T(8,128)(2,1)}, u32[]{:S(2)}, u32[]{:S(2)}) collective-permute-start(bf16[4,48,768]{2,1,0:T(8,128)(2,1)S(1)} %fusion.16), channel_id=1, source_target_pairs={{0,4},{2,6},{4,0},{6,2},{8,12},{10,14},{12,8},{14,10},{16,20},{18,... | collective-permute-start | bytes 884744 | tf_op jit(solution)/shard_map/ppermute | solution.py:738
  243.5 9.8 %copy-start.4 = (bf16[8,48,768]{2,1,0:T(8,128)(2,1)S(1)}, bf16[8,48,768]{2,1,0:T(8,128)(2,1)}, u32[]{:S(2)}) copy-start(bf16[8,48,768]{2,1,0:T(8,128)(2,1)} %copy-done.3) | copy-start | bytes 1769476
  245.3 9.0 %copy-start.2 = (bf16[8,64,768]{2,1,0:T(8,128)(2,1)S(1)}, bf16[8,64,768]{2,1,0:T(8,128)(2,1)}, u32[]{:S(2)}) copy-start(bf16[8,64,768]{2,1,0:T(8,128)(2,1)} %copy-done.1) | copy-start | bytes 2359300
  245.3 8.0 %collective-permute-start.23 = (bf16[4,64,768]{2,1,0:T(8,128)(2,1)}, bf16[4,64,768]{2,1,0:T(8,128)(2,1)S(1)}, u32[]{:S(2)}, u32[]{:S(2)}) collective-permute-start(bf16[4,64,768]{2,1,0:T(8,128)(2,1)} %fusion.6), channel_id=1, source_target_pairs={{0,2},{2,0},{4,6},{6,4},{8,10},{10,8},{12,14},{14,12},{16,18},{18,... | collective-permute-start | bytes 1179656 | tf_op jit(solution)/shard_map/ppermute | solution.py:738
  248.3 37.4 %collective-permute-start.9 = (bf16[25,145,512]{2,1,0:T(8,128)(2,1)}, bf16[25,145,512]{2,1,0:T(8,128)(2,1)S(1)}, u32[]{:S(2)}, u32[]{:S(2)}) collective-permute-start(bf16[25,145,512]{2,1,0:T(8,128)(2,1)} %patch_send.1), channel_id=1, source_target_pairs={{0,1},{1,0},{2,3},{3,2},{4,5},{5,4},{6,7},{7,6},{8,9},{9,8},{10,11... | collective-permute-start | bytes 11136008 | tf_op jit(solution)/shard_map/ppermute | solution.py:803
  254.3 1.1 copy-start.12
  254.3 1.2 copy-start.13
  254.5 9.9 %collective-permute-start.24 = (bf16[2,112,768]{2,1,0:T(8,128)(2,1)S(1)}, bf16[2,112,768]{2,1,0:T(8,128)(2,1)S(1)}, u32[]{:S(2)}, u32[]{:S(2)}) collective-permute-start(bf16[2,112,768]{2,1,0:T(8,128)(2,1)S(1)} %fusion.8), channel_id=1, source_target_pairs={{0,8},{2,10},{4,12},{6,14},{8,0},{10,2},{12,4},{14,6},{16,24},{18,... | collective-permute-start | bytes 1032200 | tf_op jit(solution)/shard_map/ppermute | solution.py:738
  257.1 7.6 %copy-start.8 = (f32[1000,384]{1,0:T(8,128)S(1)}, f32[1000,384]{1,0:T(8,128)}, u32[]{:S(2)}) copy-start(f32[1000,384]{1,0:T(8,128)} %get-tuple-element.104) | copy-start | bytes 4608004
  257.2 10.0 %collective-permute-start.13 = (bf16[4,48,768]{2,1,0:T(8,128)(2,1)S(1)}, bf16[4,48,768]{2,1,0:T(8,128)(2,1)S(1)}, u32[]{:S(2)}, u32[]{:S(2)}) collective-permute-start(bf16[4,48,768]{2,1,0:T(8,128)(2,1)S(1)} %fusion.14), channel_id=1, source_target_pairs={{0,2},{2,0},{4,6},{6,4},{8,10},{10,8},{12,14},{14,12},{16,18},{18,... | collective-permute-start | bytes 884744 | tf_op jit(solution)/shard_map/ppermute | solution.py:738
  257.8 9.4 %collective-permute-start.12 = (bf16[4,48,768]{2,1,0:T(8,128)(2,1)S(1)}, bf16[4,48,768]{2,1,0:T(8,128)(2,1)S(1)}, u32[]{:S(2)}, u32[]{:S(2)}) collective-permute-start(bf16[4,48,768]{2,1,0:T(8,128)(2,1)S(1)} %fusion.12), channel_id=1, source_target_pairs={{0,4},{2,6},{4,0},{6,2},{8,12},{10,14},{12,8},{14,10},{16,20},{18,... | collective-permute-start | bytes 884744 | tf_op jit(solution)/shard_map/ppermute | solution.py:738
  264.6 11.2 %collective-permute-start.25 = (bf16[1,112,768]{2,1,0:T(8,128)(2,1)S(1)}, bf16[1,112,768]{2,1,0:T(8,128)(2,1)S(1)}, u32[]{:S(2)}, u32[]{:S(2)}) collective-permute-start(bf16[1,112,768]{2,1,0:T(8,128)(2,1)S(1)} %dynamic-slice_convert_fusion.5), channel_id=1, source_target_pairs={{0,16},{2,18},{4,20},{6,22},{8,24},{10,26},{12,28},{14,30},{16,0},... | collective-permute-start | bytes 516104 | tf_op jit(solution)/shard_map/ppermute | solution.py:738
  267.4 10.1 %collective-permute-start.14 = (bf16[2,48,1536]{2,1,0:T(8,128)(2,1)S(1)}, bf16[2,48,1536]{2,1,0:T(8,128)(2,1)S(1)}, u32[]{:S(2)}, u32[]{:S(2)}) collective-permute-start(bf16[2,48,1536]{2,1,0:T(8,128)(2,1)S(1)} %fusion.10), channel_id=1, source_target_pairs={{0,8},{2,10},{4,12},{6,14},{8,0},{10,2},{12,4},{14,6},{16,24},{18,... | collective-permute-start | bytes 884744 | tf_op jit(solution)/shard_map/ppermute | solution.py:738
  277.6 6.7 %collective-permute-start.15 = (bf16[1,48,1536]{2,1,0:T(8,128)(2,1)S(1)}, bf16[1,48,1536]{2,1,0:T(8,128)(2,1)S(1)}, u32[]{:S(2)}, u32[]{:S(2)}) collective-permute-start(bf16[1,48,1536]{2,1,0:T(8,128)(2,1)S(1)} %dynamic-slice_convert_fusion.7), channel_id=1, source_target_pairs={{0,16},{2,18},{4,20},{6,22},{8,24},{10,26},{12,28},{14,30},{16,0},... | collective-permute-start | bytes 442376 | tf_op jit(solution)/shard_map/ppermute | solution.py:738
  285.7 2.0 copy-start

commit v2 on v1

--- a/solution.py
+++ b/solution.py
@@ -44,7 +44,8 @@
     return pl.BlockSpec(shape, lambda i, *_: (i,) + zeros)
 
 
-def call(body, name, grid, ins, outs, scratch, flops, nbytes, scalars=0, vmem=60):
+def call(body, name, grid, ins, outs, scratch, flops, nbytes, scalars=0, vmem=60,
+         collective=None):
     return pl.pallas_call(
         body,
         name=name,
@@ -57,7 +58,8 @@
             scratch_shapes=scratch,
         ),
         compiler_params=pltpu.CompilerParams(
-            dimension_semantics=("arbitrary",), vmem_limit_bytes=vmem * MIB
+            dimension_semantics=("arbitrary",), vmem_limit_bytes=vmem * MIB,
+            collective_id=collective, has_side_effects=collective is not None,
         ),
         cost_estimate=pl.CostEstimate(flops=flops, bytes_accessed=nbytes, transcendentals=0),
     )
@@ -296,13 +298,12 @@
     here = width // 2
 
     def body(side_ref, n2_ref, m_ref, t_ref, pr_ref, e_ref, d_ref, w_ref, o_ref,
-             j_ref, dh_ref, dhb_ref, du_ref, part_ref, sum_ref, sumu_ref, wt, ot):
+             j_ref, dh_ref, dhb_ref, du_ref, part_ref, sum_ref, wt, ot):
         @pl.when(pl.program_id(0) == 0)
         def _():
             wt[...] = w_ref[...].T
             ot[...] = o_ref[...].T
             sum_ref[...] = jnp.zeros_like(sum_ref)
-            sumu_ref[...] = jnp.zeros_like(sumu_ref)
 
         h = (n2_ref[...] * pr_ref[4:5, :] + pr_ref[7:8, :]) + (
             m_ref[...].astype(F32) + t_ref[...].astype(F32)
@@ -320,7 +321,9 @@
         sum_ref[2:3, :] += colsum(dh)
         dg = nn(dhb, ot[...]).astype(BF)
         du = dg.astype(F32) * d_ref[...].astype(F32)
-        sumu_ref[0:1, :] += colsum(du)
+        total = colsum(du)
+        sum_ref[4:5, :] += total[:, :width]
+        sum_ref[5:6, :] += total[:, width:]
         dub = du.astype(BF)
         du_ref[...] = dub
         part_ref[...] = nn(dub, wt[...]).astype(BF)
@@ -339,7 +342,6 @@
             ((tokens, hidden), BF, wide),
             ((tokens, width), BF, full),
             ((8, width), F32, whole((8, width))),
-            ((8, hidden), F32, whole((8, hidden))),
         ],
         [pltpu.VMEM((hidden, width), BF), pltpu.VMEM((width, hidden), BF)],
         2 * tokens * width * 2 * hidden,
@@ -438,6 +440,44 @@
     )(picks, grad, mine, other, params, normed, spread, query, keys, values, query_w, out_w)
 
 
+def self_tile(grad, mine, other, pr_ref, n, r, q_ref, wt, ot, same, sum_ref, keep_ref, send_ref,
+              first, here):
+    e = grad + (mine.astype(F32) + other.astype(F32))
+    dh = norm_back(e, n, r, pr_ref[3:4, :])
+    dhb = dh.astype(BF)
+    sum_ref[0:1, :] += colsum(e * n)
+    sum_ref[1:2, :] += colsum(e)
+    sum_ref[2:3, :] += colsum(dh)
+    dc = nn(dhb, ot[...]).astype(BF)
+    grads = [[], [], []]
+    for p in range(here // 128):
+        q = q_ref[:, 128 * p : 128 * p + 128]
+        k = q_ref[:, here + 128 * p : here + 128 * p + 128]
+        v = q_ref[:, 2 * here + 128 * p : 2 * here + 128 * p + 128]
+        c = dc[:, 128 * p : 128 * p + 128]
+        sums = [None, None, None]
+        for a in range(2):
+            mask = head_mask(128, a, BF)
+            qm = q * mask
+            cm = c * mask
+            pt = softmax_cols(jnp.where(same, nt(k, qm) * SCALE, BIG_NEG))
+            dp = nt(v, cm)
+            ds = (pt * (dp - jnp.sum(dp * pt, axis=0, keepdims=True))).astype(BF)
+            new = (tn(ds, k * mask), nn(ds, qm), nn(pt.astype(BF), cm))
+            sums = [b if a_ is None else a_ + b for a_, b in zip(sums, new)]
+        grads[0].append(sums[0] * SCALE)
+        grads[1].append(sums[1] * SCALE)
+        grads[2].append(sums[2])
+    dq, dk, dv = (jnp.concatenate(g, axis=1) for g in grads)
+    sum_ref[3:4, :here] += colsum(dq)
+    sum_ref[3:4, here:] += colsum(dv)
+    dqkv = jnp.concatenate((dq, dk, dv), axis=1).astype(BF)
+    part = nn(dqkv, wt[...])
+    keep_ref[...] = jnp.where(first, dh[:, :here] + part[:, :here], dh[:, here:] + part[:, here:])
+    send_ref[...] = jnp.where(first, part[:, here:], part[:, :here]).astype(BF)
+    return dhb, dqkv
+
+
 def self_backward(side, grad, mine, other, params, normed, spread, qkv, qkv_w, out_w,
                   ids_col, ids_row, tile):
     tokens, width = grad.shape
@@ -452,47 +492,12 @@
             ot[...] = o_ref[...].T
             sum_ref[...] = jnp.zeros_like(sum_ref)
 
-        e = g_ref[...] + (m_ref[...].astype(F32) + t_ref[...].astype(F32))
-        n = n_ref[...]
-        dh = norm_back(e, n, r_ref[...], pr_ref[3:4, :])
-        dhb = dh.astype(BF)
+        dhb, dqkv = self_tile(
+            g_ref[...], m_ref[...], t_ref[...], pr_ref, n_ref[...], r_ref[...], q_ref, wt, ot,
+            ic_ref[...] == ir_ref[0], sum_ref, keep_ref, send_ref, side_ref[0] == 0, here,
+        )
         dhb_ref[...] = dhb
-        sum_ref[0:1, :] += colsum(e * n)
-        sum_ref[1:2, :] += colsum(e)
-        sum_ref[2:3, :] += colsum(dh)
-        dc = nn(dhb, ot[...]).astype(BF)
-        same = ic_ref[...] == ir_ref[0]
-        grads = [[], [], []]
-        for p in range(here // 128):
-            q = q_ref[:, 128 * p : 128 * p + 128]
-            k = q_ref[:, here + 128 * p : here + 128 * p + 128]
-            v = q_ref[:, 2 * here + 128 * p : 2 * here + 128 * p + 128]
-            c = dc[:, 128 * p : 128 * p + 128]
-            sums = [None, None, None]
-            for a in range(2):
-                mask = head_mask(128, a, BF)
-                qm = q * mask
-                cm = c * mask
-                s = jnp.where(same, nt(k, qm) * SCALE, BIG_NEG)
-                pt = softmax_cols(s)
-                dp = nt(v, cm)
-                ds = (pt * (dp - jnp.sum(dp * pt, axis=0, keepdims=True))).astype(BF)
-                new = (tn(ds, k * mask), nn(ds, qm), nn(pt.astype(BF), cm))
-                sums = [b if a_ is None else a_ + b for a_, b in zip(sums, new)]
-            grads[0].append(sums[0] * SCALE)
-            grads[1].append(sums[1] * SCALE)
-            grads[2].append(sums[2])
-        dq, dk, dv = (jnp.concatenate(g, axis=1) for g in grads)
-        sum_ref[3:4, :here] += colsum(dq)
-        sum_ref[3:4, here:] += colsum(dv)
-        dqkv = jnp.concatenate((dq, dk, dv), axis=1).astype(BF)
         dq_ref[...] = dqkv
-        part = nn(dqkv, wt[...])
-        first = side_ref[0] == 0
-        keep_ref[...] = jnp.where(
-            first, dh[:, :here] + part[:, :here], dh[:, here:] + part[:, here:]
-        )
-        send_ref[...] = jnp.where(first, part[:, here:], part[:, :here]).astype(BF)
 
     full = tiled((tile, width))
     half = tiled((tile, here))
@@ -734,6 +739,520 @@
     return made if inside else split_outside(made[0], bit, shards, bits)
 
 
+ORDERS = ((0, 1, 2, 3), (1, 2, 0, 3), (2, 0, 1, 3))
+LINKS = (None, 0, 1, 2, 3)
+MESH = pl.DeviceIdType.MESH
+
+
+def digit(bit):
+    return (lax.axis_index("dp") // (1 << bit)) % 2
+
+
+def partner(bit):
+    dp_at, mp_at = lax.axis_index("dp"), lax.axis_index("mp")
+    if bit is None:
+        return {"dp": dp_at, "mp": 1 - mp_at}
+    return {"dp": dp_at + (1 << bit) - 2 * (1 << bit) * digit(bit), "mp": mp_at}
+
+
+def remote(source, target, send_sem, got_sem, bit):
+    return pltpu.make_async_remote_copy(
+        src_ref=source, dst_ref=target, send_sem=send_sem, recv_sem=got_sem,
+        device_id=partner(bit), device_id_type=MESH,
+    )
+
+
+def greet():
+    barrier = pltpu.get_barrier_semaphore()
+    for bit in LINKS:
+        pl.semaphore_signal(barrier, inc=1, device_id=partner(bit), device_id_type=MESH)
+
+
+def met():
+    pl.semaphore_wait(pltpu.get_barrier_semaphore(), len(LINKS))
+
+
+class Stream:
+    def __init__(self, rows, columns, order, first=0, last=3):
+        self.rows, self.columns, self.order = rows, columns, order
+        self.first, self.last = first, last
+
+    def shape(self, t):
+        return (8 >> t, self.rows, self.columns)
+
+    def position(self, t):
+        return sorted(set(self.order) - set(self.order[:t])).index(self.order[t])
+
+    def scratch(self, made):
+        steps = range(self.first, self.last + 1)
+        shapes = [pltpu.VMEM(self.shape(t), BF) for t in steps]
+        for t in range(made, self.last + 1):
+            shapes += [pltpu.VMEM(self.shape(t), BF)] * 2
+        return shapes + [pltpu.SemaphoreType.DMA((4,))] * 2
+
+    def bind(self, refs, made, given=None):
+        size = len(self.scratch(made))
+        mine, rest = refs[:size], refs[size:]
+        steps = self.last + 1 - self.first
+        self.got = {self.first + i: mine[i] for i in range(steps)}
+        self.pairs = {}
+        for i, t in enumerate(range(made, self.last + 1)):
+            self.pairs[t] = mine[steps + 2 * i : steps + 2 * i + 2]
+        if given is not None:
+            self.pairs[made - 1] = given
+        self.sems = mine[-2:]
+        return rest
+
+    def copy(self, t):
+        return remote(self.pairs[t][0], self.got[t], self.sems[0].at[t], self.sems[1].at[t],
+                      self.order[t])
+
+    def start(self, t):
+        self.copy(t).start()
+
+    def total(self, t, shard):
+        return self.pairs[t][1][shard].astype(F32) + self.got[t][shard].astype(F32)
+
+    def fold(self, t, target):
+        mine = digit(self.order[t + 1])
+        low = 1 << self.position(t + 1)
+        send, keep = target
+        for j in range(8 >> (t + 1)):
+            base = (j // low) * 2 * low + j % low
+            send[j] = self.total(t, base + (1 - mine) * low).astype(BF)
+            keep[j] = self.total(t, base + mine * low).astype(BF)
+
+    def advance(self, t):
+        self.copy(t).wait()
+        self.fold(t, self.pairs[t + 1])
+        self.start(t + 1)
+
+    def finish(self):
+        self.copy(3).wait()
+        return self.total(3, 0)
+
+
+def split_shards(full, columns, pair, bit, size):
+    mine = digit(bit)
+    for slot, shard in enumerate(shards_of(bit, 16)):
+        kept = pl.multiple_of((shard + mine * (1 << bit)) * size, 16)
+        sent = pl.multiple_of((shard + (1 - mine) * (1 << bit)) * size, 16)
+        pair[1][slot] = full[pl.ds(kept, size), columns].astype(BF)
+        pair[0][slot] = full[pl.ds(sent, size), columns].astype(BF)
+
+
+def small_out(shape, dtype=F32):
+    return (shape, dtype, whole(shape))
+
+
+def rows_backward(ffn_kept, ffn_got, cross_terms, grad, part, params, normed, spread, qkv,
+                  qkv_w, out_w, ids_col, ids_row, text, context, tile):
+    tokens, width = grad.shape
+    here = out_w.shape[0]
+    tiles = tokens // tile
+    size = width // 16
+    third = 2 * here // 3
+    ffn_cols = ffn_kept[0].shape[2]
+    self_cols = 4 * here // 3
+    dhb_two, cross_ctx, y_one, dq_cross = cross_terms
+    begin = 2
+    after_self = begin + tiles
+    steps = after_self + 4
+    ffn = [Stream(size, ffn_cols, order) for order in ORDERS]
+    cross = [Stream(size, third, order, 0, 0) for order in ORDERS]
+    self_streams = [Stream(size, self_cols, order) for order in ORDERS]
+
+    def body(*refs):
+        ffn_refs, refs = refs[:6], refs[6:]
+        (l0_ref, r0_ref, l1_ref, r1_ref, g_ref, part_ref, mine_ref, pr_ref, n_ref, r_ref, q_ref,
+         w_ref, o_ref, ic_ref, ir_ref, x_ref, c_ref) = refs[:17]
+        keep_ref, send_ref, sum_ref, ffn_ref = refs[17:21]
+        self_out, cross_out, rest = refs[21:27], refs[27:33], refs[33:]
+        (lt, acc, wt, ot, other, dq_all, dhb_all, full, part_sems) = rest[:9]
+        ffn_local, ffn_sems, rest = rest[9:15], rest[15], rest[16:]
+        for which, stream in enumerate(ffn):
+            rest = stream.bind(rest, 1)
+            stream.pairs[0] = (None, ffn_local[2 * which])
+            stream.got[0] = ffn_local[2 * which + 1]
+        for stream in cross:
+            rest = stream.bind(rest, 0)
+        at = pl.program_id(0)
+        side = lax.axis_index("mp")
+        loads = [
+            pltpu.make_async_copy(ffn_refs[i], ffn_local[i], ffn_sems.at[i]) for i in range(6)
+        ]
+        part_copy = remote(part_ref, other, part_sems.at[0], part_sems.at[1], None)
+
+        @pl.when(at == 0)
+        def _():
+            greet()
+            for load in loads:
+                load.start()
+            lt[...] = l0_ref[...].T
+            sum_ref[...] = jnp.zeros_like(sum_ref)
+            met()
+            part_copy.start()
+            acc[...] = nn(lt[...], r0_ref[...])
+            full[:, :here] = acc[...].astype(BF)
+            for load in loads:
+                load.wait()
+            for stream in ffn:
+                stream.fold(0, stream.pairs[1])
+                stream.start(1)
+
+        @pl.when(at == 1)
+        def _():
+            lt[...] = l1_ref[...].T
+            acc[...] = nn(lt[...], r1_ref[...])
+            full[:, here : 2 * here] = acc[...].astype(BF)
+            for which, stream in enumerate(cross):
+                split_shards(full, slice(which * third, (which + 1) * third), stream.pairs[0],
+                             stream.order[0], size)
+            for s in range(3):
+                wt[s * here : (s + 1) * here, :] = w_ref[s].T
+            ot[...] = o_ref[...].T
+            part_copy.wait()
+
+        @pl.when(at == begin + 2)
+        def _():
+            for stream in ffn:
+                stream.advance(1)
+
+        @pl.when(at == begin + 4)
+        def _():
+            for stream in ffn:
+                stream.advance(2)
+            for stream in cross:
+                stream.start(0)
+
+        @pl.when((at >= begin) & (at < after_self))
+        def _():
+            i = at - begin
+            dhb, dqkv = self_tile(
+                g_ref[...], mine_ref[...], other[i], pr_ref, n_ref[...], r_ref[...], q_ref,
+                wt, ot, ic_ref[...] == ir_ref[0], sum_ref, keep_ref, send_ref, side == 0, here,
+            )
+            for j in range(tiles):
+                @pl.when(i == j)
+                def _(j=j):
+                    dq_all[j * tile : (j + 1) * tile, :] = dqkv
+                    dhb_all[j * tile : (j + 1) * tile, :] = dhb
+
+        for j in range(4):
+            @pl.when(at == after_self + j)
+            def _(j=j):
+                if j == 0:
+                    lt[...] = x_ref[...].T
+                if j == 3:
+                    lt[...] = dhb_all[...].T
+                right = c_ref[...] if j == 3 else dq_all[:, j * here : (j + 1) * here]
+                acc[...] = nn(lt[...], right)
+                full[:, j * here : (j + 1) * here] = acc[...].astype(BF)
+                if j == 3:
+                    for which, stream in enumerate(self_streams):
+                        split_shards(
+                            full, slice(which * self_cols, (which + 1) * self_cols),
+                            self_out[2 * which : 2 * which + 2], stream.order[0], size,
+                        )
+                    for which, stream in enumerate(cross):
+                        stream.copy(0).wait()
+                        stream.fold(0, cross_out[2 * which : 2 * which + 2])
+                    for which, stream in enumerate(ffn):
+                        ffn_ref[:, which * ffn_cols : (which + 1) * ffn_cols] = stream.finish()
+
+    anywhere = pl.BlockSpec(memory_space=pl.ANY)
+
+    def rows(columns):
+        return pl.BlockSpec((tile, columns), lambda i: (jnp.clip(i - begin, 0, tiles - 1), 0))
+
+    ids_spec = pl.BlockSpec((1, 1, tile), lambda i: (jnp.clip(i - begin, 0, tiles - 1), 0, 0))
+    ffn_arrays = [a for pair in zip(ffn_kept, ffn_got) for a in pair]
+    operands = ffn_arrays + [
+        dhb_two, cross_ctx, y_one, dq_cross, grad, part.reshape(tiles, tile, width), part, params,
+        normed, spread, qkv, qkv_w, out_w, ids_col, ids_row, text, context,
+    ]
+    ins = [anywhere] * 6 + [
+        whole(dhb_two.shape), whole(cross_ctx.shape), whole(y_one.shape), whole(dq_cross.shape),
+        rows(width), anywhere, rows(width), whole(params.shape), rows(width), rows(1),
+        rows(3 * here), whole(qkv_w.shape), whole(out_w.shape), rows(1), ids_spec,
+        whole(text.shape), whole(context.shape),
+    ]
+    outs = [
+        ((tokens, here), F32, rows(here)),
+        ((tokens, here), BF, rows(here)),
+        small_out((8, width)),
+        small_out((size, 3 * ffn_cols)),
+    ]
+    outs += [small_out(self_streams[0].shape(0), BF)] * 6
+    outs += [small_out(cross[0].shape(1), BF)] * 6
+    scratch = [
+        pltpu.VMEM((width, tokens), BF),
+        pltpu.VMEM((width, here), F32),
+        pltpu.VMEM((3 * here, width), BF),
+        pltpu.VMEM((width, here), BF),
+        pltpu.VMEM((tiles, tile, width), BF),
+        pltpu.VMEM((tokens, 3 * here), BF),
+        pltpu.VMEM((tokens, width), BF),
+        pltpu.VMEM((width, 4 * here), BF),
+        pltpu.SemaphoreType.DMA((2,)),
+    ]
+    scratch += [pltpu.VMEM(ffn[0].shape(0), BF)] * 6 + [pltpu.SemaphoreType.DMA((6,))]
+    for stream in ffn:
+        stream.first = 1
+        scratch += stream.scratch(1)
+    for stream in cross:
+        scratch += stream.scratch(0)
+    made = call(
+        body, "rows_backward", steps, ins, outs, scratch,
+        2 * tokens * width * 10 * here, tokens * width * 30, collective=1,
+    )(*operands)
+    return made[:4], [made[4 + 2 * i : 6 + 2 * i] for i in range(3)], [
+        made[10 + 2 * i : 12 + 2 * i] for i in range(3)]
+
+
+def patch_backward(patches, pair, cross_kv, cross_pairs, self_pairs, sums, padded):
+    images, count, visual = patches.shape
+    width = cross_kv.shape[2]
+    half = visual // 2
+    wide = 2 * width
+    size = visual // 16
+    group = 5
+    steps = images // group
+    small = cross_pairs[0][0].shape[1]
+    third = wide // 3
+    self_cols = self_pairs[0][0].shape[2]
+    cross = [Stream(small, third, order, 1) for order in ORDERS]
+    selves = [Stream(small, self_cols, order) for order in ORDERS]
+    kvs = [Stream(size, third, order) for order in ORDERS]
+    given = list(cross_pairs) + list(self_pairs)
+
+    def body(p_ref, g_ref, w_ref, s1_ref, s2_ref, s3_ref, *refs):
+        firsts = [refs[2 * i : 2 * i + 2] for i in range(6)]
+        out_ref, cross_ref, self_ref, kv_ref, sum_ref = refs[12:17]
+        rows, acc, wt, send, got, send_sem, got_sem, sum_now, sum_got, sum_sems = refs[17:27]
+        rest = refs[27:]
+        for which, stream in enumerate(cross):
+            rest = stream.bind(rest, 2, firsts[which])
+        for which, stream in enumerate(selves):
+            rest = stream.bind(rest, 1, firsts[3 + which])
+        for stream in kvs:
+            rest = stream.bind(rest, 0)
+        side = lax.axis_index("mp")
+        at = pl.program_id(0)
+
+        def patch_copy(tile):
+            return remote(send.at[tile], got.at[tile], send_sem.at[tile], got_sem.at[tile], None)
+
+        def sum_copy(bit):
+            return remote(sum_now.at[bit], sum_got.at[bit], sum_sems.at[bit],
+                          sum_sems.at[4 + bit], bit)
+
+        @pl.when(at == 0)
+        def _():
+            greet()
+            rows[...] = jnp.zeros_like(rows)
+            sum_now[0, :8] = s3_ref[...]
+            sum_now[0, 8:12] = s1_ref[0:4]
+            sum_now[0, 12:16] = s2_ref[0:4]
+            met()
+            for stream in selves:
+                stream.start(0)
+            sum_copy(0).start()
+            for stream in cross:
+                stream.start(1)
+            wt[:width, :] = w_ref[0].T
+            wt[width:, :] = w_ref[1].T
+
+        for bit in range(4):
+            @pl.when(at == bit + 1)
+            def _(bit=bit):
+                sum_copy(bit).wait()
+                total = sum_now[bit] + sum_got[bit]
+                if bit == 3:
+                    sum_ref[...] = total
+                else:
+                    sum_now[bit + 1] = total
+                    sum_copy(bit + 1).start()
+
+        def plan(step, streams, t):
+            @pl.when(at == step)
+            def _():
+                for stream in streams:
+                    stream.advance(t)
+
+        plan(3, cross, 1)
+        plan(5, cross, 2)
+        plan(5, selves, 0)
+        plan(9, selves, 1)
+        plan(11, selves, 2)
+        plan(12, kvs, 0)
+        plan(13, kvs, 1)
+        plan(14, kvs, 2)
+
+        @pl.when(at < steps)
+        def _():
+            for i in range(group):
+                rows[padded * i : padded * i + count, :] = p_ref[i]
+            new = tn(rows[...], g_ref[...])
+
+            @pl.when(at == 0)
+            def _():
+                acc[...] = new
+
+            @pl.when(at > 0)
+            def _():
+                acc[...] += new
+
+            @pl.when(at == steps - 1)
+            def _():
+                for which, stream in enumerate(kvs):
+                    split_shards(acc, slice(which * third, (which + 1) * third), stream.pairs[0],
+                                 stream.order[0], size)
+                    stream.start(0)
+
+        def product(half_at):
+            lanes = pl.ds(pl.multiple_of(half_at * half, 128), half)
+            return nn(g_ref[...], wt[:, lanes])
+
+        @pl.when((at >= steps) & (at < 2 * steps))
+        def _():
+            tile = at - steps
+            out = product(1 - side)
+            for i in range(group):
+                send[tile, i] = out[padded * i : padded * i + count].astype(BF)
+            patch_copy(tile).start()
+
+        @pl.when(at >= 2 * steps)
+        def _():
+            tile = at - 2 * steps
+            out = product(side)
+            patch_copy(tile).wait()
+            for i in range(group):
+                mine = out[padded * i : padded * i + count]
+                out_ref[i] = (mine + got[tile, i].astype(F32)).astype(BF)
+
+        @pl.when(at == 3 * steps - 1)
+        def _():
+            for target, streams in ((cross_ref, cross), (self_ref, selves), (kv_ref, kvs)):
+                for which, stream in enumerate(streams):
+                    lo = which * stream.columns
+                    target[:, lo : lo + stream.columns] = stream.finish()
+
+    anywhere = pl.BlockSpec(memory_space=pl.ANY)
+    ins = [
+        pl.BlockSpec((group, count, visual), lambda i: (jnp.minimum(i, steps - 1), 0, 0)),
+        pl.BlockSpec((group * padded, wide), lambda i: (i % steps, 0)),
+        whole(cross_kv.shape),
+    ] + [whole(s.shape) for s in sums]
+    operands = [patches, pair, cross_kv, *sums]
+    for sent, kept in given:
+        ins += [anywhere, whole(kept.shape)]
+        operands += [sent, kept]
+    scratch = [
+        pltpu.VMEM((group * padded, visual), BF),
+        pltpu.VMEM((visual, wide), F32),
+        pltpu.VMEM((wide, visual), BF),
+        pltpu.VMEM((steps, group, count, half), BF),
+        pltpu.VMEM((steps, group, count, half), BF),
+        pltpu.SemaphoreType.DMA((steps,)),
+        pltpu.SemaphoreType.DMA((steps,)),
+        pltpu.VMEM((4, 16, wide), F32),
+        pltpu.VMEM((4, 16, wide), F32),
+        pltpu.SemaphoreType.DMA((8,)),
+    ]
+    for stream in cross:
+        scratch += stream.scratch(2)
+    for stream in selves:
+        scratch += stream.scratch(1)
+    for stream in kvs:
+        scratch += stream.scratch(0)
+    return call(
+        body,
+        "patch_backward",
+        3 * steps,
+        ins,
+        [
+            ((images, count, half), BF,
+             pl.BlockSpec((group, count, half), lambda i: (jnp.maximum(i - 2 * steps, 0), 0, 0))),
+            small_out((small, wide)),
+            small_out((small, 3 * self_cols)),
+            small_out((size, wide)),
+            small_out((16, wide)),
+        ],
+        scratch,
+        2 * images * padded * visual * wide * 2,
+        patches.size * 2 + pair.size * 6 + images * count * half * 4,
+        collective=2,
+    )(*operands)
+
+
+def finish(side, patch, text_keep, text_other, ffn, cross, self_sum, kv, sums):
+    images, count, half = patch.shape
+    tokens, here = text_keep.shape
+    block = ffn.shape[0]
+    hidden = ffn.shape[1] // 2
+    steps = 5
+    tile = tokens // steps
+    group = images // steps
+
+    def body(side_ref, p_ref, k_ref, t_ref, f_ref, c_ref, s_ref, v_ref, m_ref,
+             patch_out, text_out, qkv_out, so_out, cq_out, kv_out, co_out, fi_out, fo_out,
+             sb_out, cb_out, fb_out, br_out, ga_out, sh_out):
+        patch_out[...] = p_ref[...].astype(F32)
+        text_out[...] = k_ref[...] + t_ref[...].astype(F32)
+
+        @pl.when(pl.program_id(0) == 0)
+        def _():
+            for i in range(3):
+                qkv_out[i] = s_ref[:, i * here : (i + 1) * here]
+            so_out[...] = s_ref[:, 3 * here :]
+            cq_out[...] = c_ref[:, here:]
+            co_out[...] = c_ref[:, :here]
+            fi_out[...] = f_ref[:, hidden:]
+            fo_out[...] = f_ref[:, :hidden]
+            for i in range(2):
+                kv_out[i] = v_ref[:, i * here : (i + 1) * here]
+                sb_out[i : i + 1, :] = m_ref[11:12, i * here : (i + 1) * here]
+                cb_out[i : i + 1, :] = m_ref[15:16, i * here : (i + 1) * here]
+                fb_out[:, 2 * i * here : 2 * (i + 1) * here] = m_ref[4 + i : 5 + i, :]
+            first = side_ref[0] == 0
+            for out, at in ((ga_out, 0), (sh_out, 1), (br_out, 2)):
+                for i, row in enumerate((8 + at, 12 + at, at)):
+                    out[i : i + 1, :] = jnp.where(
+                        first, m_ref[row : row + 1, :here], m_ref[row : row + 1, here:]
+                    )
+
+    rows = tiled((tile, here))
+    blocks = tiled((group, count, half))
+    return call(
+        body,
+        "finish",
+        steps,
+        [blocks, rows, rows] + [whole(a.shape) for a in (ffn, cross, self_sum, kv, sums)],
+        [
+            (patch.shape, F32, blocks),
+            (text_keep.shape, F32, rows),
+            small_out((3, block, here)),
+            small_out((block, here)),
+            small_out((block, here)),
+            small_out((2, kv.shape[0], here)),
+            small_out((block, here)),
+            small_out((block, hidden)),
+            small_out((block, hidden)),
+            small_out((2, here)),
+            small_out((2, here)),
+            small_out((1, hidden)),
+            small_out((3, here)),
+            small_out((3, here)),
+            small_out((3, here)),
+        ],
+        [],
+        images * count * half,
+        images * count * half * 6,
+        scalars=1,
+    )(side, patch, text_keep, text_other, ffn, cross, self_sum, kv, sums)
+
+
 def swap_dp(value, bit, shards):
     return lax.ppermute(value, "dp", [(i, i ^ (1 << bit)) for i in range(shards)])
 
@@ -868,11 +1387,46 @@
     n_two, r_two, y_two, act, slope, part_three = ffn_forward(
         n_one, part_two, swap_mp(part_two), params, ffn_in, ffn_in_bias[None], ffn_out, tile
     )
-    joined, dh_three, dhb_three, du, part_four, sums_three, sums_hidden = ffn_backward(
+    joined, dh_three, dhb_three, du, part_four, sums_three = ffn_backward(
         side, n_two, part_three, swap_mp(part_three), params, cot_full, slope, ffn_in, ffn_out,
         tile,
     )
     other_four = swap_mp(part_four)
+    quick = shards == 16
+    if quick:
+        most, few = 2 * hidden // 3, hidden // 3
+        ffn_groups = grad_weight(
+            bits,
+            [
+                (0, [(dhb_three, act, 0, most)]),
+                (1, [(dhb_three, act, most, few), (y_two, du, 0, few)]),
+                (2, [(y_two, du, few, most)]),
+            ],
+            shards, "grad_ffn", few,
+        )
+        ffn_got = [swap_dp(g[0], b, shards) for b, g in enumerate(ffn_groups)]
+        part_four, _ = after([part_four, other_four], tuple(g[0] for g in ffn_groups))
+        dh_two, dhb_two, dq_cross, part_five, pair, sums_two = cross_backward(
+            picks, dh_three, part_four, other_four, params, n_two, r_two, query, keys, values,
+            cross_query, cross_out, tile, length, count, padded,
+        )
+        ffn_got = after(ffn_got, (part_five,))
+        (text_keep, text_send, sums_one, ffn_shard), self_pairs, cross_pairs = rows_backward(
+            [g[1] for g in ffn_groups], ffn_got, (dhb_two, cross_ctx, y_one, dq_cross), dh_two,
+            part_five, params, n_one, r_one, qkv, self_qkv, self_out, ids_col, ids_row,
+            text_full, context, tile,
+        )
+        text_other = swap_mp(text_send)
+        patch, cross_shard, self_shard, kv_shard, sums = patch_backward(
+            patches, pair, cross_kv, cross_pairs, self_pairs, (sums_one, sums_two, sums_three),
+            padded,
+        )
+        (patch_grad, text_grad, g_qkv, g_so, g_cq, g_kv, g_co, g_fi, g_fo, g_sb, g_cb, g_fb, g_br,
+         g_ga, g_sh) = finish(
+            side, patch, text_keep, text_other, ffn_shard, cross_shard, self_shard, kv_shard, sums
+        )
+        return (joined, text_grad, patch_grad, g_qkv, g_sb, g_so.T, g_cq, g_cb, g_kv, g_co.T, g_fi,
+                g_fb.reshape(-1), g_fo.T, g_br, g_ga, g_sh)
     ffn_groups = grad_weight(
         bits,
         [(0, [(dhb_three, act, 0, hidden)]), (1, [(y_two, du, 0, hidden)])],
@@ -933,7 +1487,7 @@
             mine(sums_three[:3]),
             sums_one[3].reshape(2, here),
             sums_two[3].reshape(2, here),
-            sums_hidden[0].reshape(-1, here),
+            sums_three[4:6].reshape(-1, here),
         ),
         axis=0,
     )

time: 300 us -> 259 us (0.86)
  Pallas kernels: 183 us -> 223 us
  waiting for transfers between devices: 42.7 us -> 6.89 us
  other arithmetic: 26.7 us -> 9.05 us
  starting transfers between devices: 24.3 us -> 7.99 us
  local copies, waits for them, and re-layouts: 20.2 us -> 9.75 us
    pallas_call x4 -> x3, Pallas kernels: 54 us -> 109 us  [the longest x1 59.9 us: patch_backward(): call(body, 'patch_backward', 3 * steps, ins, [((images, count, half), BF,...]
    ppermute x22 -> x3, waiting for transfers between devices: 35.8 us -> 0.01 us  [swap_dp(): return lax.ppermute(value, 'dp', [(i, i ^ 1 << bit) for i in range(shards)])]
    ppermute x22 -> x3, starting transfers between devices: 22.2 us -> 6.03 us  [swap_dp(): return lax.ppermute(value, 'dp', [(i, i ^ 1 << bit) for i in range(shards)])]
    pallas_call x3 -> x1, Pallas kernels: 30.4 us -> 14.8 us  [grad_weight(): call(body, name, total, specs, outs, [pltpu.VMEM((width, tokens), BF), pl...]
    add x19 -> x0, other arithmetic: 15.3 us -> none  [the longest x14 12.8 us: add_pair(): return keep.astype(F32) + arrived.astype(F32)]
    unnamed x48 -> x28, local copies, waits for them, and re-layouts: 8.53 us -> 6.84 us
    ppermute x10 -> x8, waiting for transfers between devices: 6.87 us -> 6.88 us  [swap_mp(): return lax.ppermute(value, 'mp', [(0, 1), (1, 0)])]
  transfers between devices with their start and end apart: 32 -> 11, of which waited for: 11 -> 2; matrix products, arithmetic and copies ran while one was open for 12% -> 3% of each run, Pallas kernels for 38% -> 45%
where the time goes in v2:
time: 259 us; the launch traced here: 258 us
  Pallas kernels  223 us (86%)
  local copies, waits for them, and re-layouts  9.75 us (4%)
  other arithmetic  9.05 us (3%)
  starting transfers between devices  7.99 us (3%)
  waiting for transfers between devices  6.89 us (3%)
    pallas_call x1, Pallas kernels, patch_backward(): call(body, 'patch_backward', 3 * steps, ins, [((images, count, half), BF,...  59.9 us
    pallas_call x1, Pallas kernels, rows_backward(): call(body, 'rows_backward', steps, ins, outs, scratch, 2 * tokens * width...  41.1 us
    pallas_call x1, Pallas kernels, cross_backward(): call(body, 'cross_backward', steps, [full, full, full, whole(params.shape...  30 us
    pallas_call x1, Pallas kernels, cross_forward(): call(body, 'cross_forward', tokens // tile, [full, full, full, whole(para...  19.4 us
    pallas_call x1, Pallas kernels, ffn_backward(): call(body, 'ffn_backward', tokens // tile, [full, full, full, whole(param...  14.9 us
    pallas_call x1, Pallas kernels, grad_weight(): call(body, name, total, specs, outs, [pltpu.VMEM((width, tokens), BF), pl...  14.8 us
    pallas_call x1, Pallas kernels, ffn_forward(): call(body, 'ffn_forward', tokens // tile, [full, full, full, whole(params...  12.1 us
    pallas_call x1, Pallas kernels, self_forward(): call(body, 'self_forward', tokens // tile, [tiled((tile, width)), whole(q...  11.4 us
  transfers between devices with their start and end apart: 11, of which 2 were waited for; matrix products, arithmetic and copies ran while one was open for 3% of the time, Pallas kernels for 45%

profile of v2, /device:TPU:0, one launch (start us, length us, event | category | flops | bytes accessed | tf_op | source)
XLA Modules:
  0.0 257.7 jit_solution(9474188423952339099)
XLA Ops:
  0.6 0.5 collective-permute-start
  1.2 0.8 broadcast_add_fusion
  2.0 0.7 reshape.64.ir_ref.refs_20_
  2.6 1.0 reshape.69.ic_ref.refs_19_
  3.7 0.8 convert_reduce_fusion.1
  4.5 0.6 broadcast_in_dim.11.b_ref
  5.1 0.0 collective-permute-done
  5.1 3.0 %maximum_select_fusion.x_ref.refs_21_ = bf16[1000,768]{1,0:T(8,128)(2,1)} fusion(bf16[1000,384]{1,0:T(8,128)(2,1)S(1)} %collective-permute-done, bf16[1000,384]{1,0:T(8,128)(2,1)} %param.18, pred[]{:T(512)S(6)} %eq.3), kind=kLoop, calls=%fused_computation | loop fusion | flops 6912000 | bytes 3072001 | tf_op jit(solution)/shard_map/jit(_where)/select_n | solution.py:1362
  8.0 0.0 copy-start.7
  8.0 0.0 copy-start.9
  8.0 11.4 %self_forward.1 = (bf16[1000,1152]{1,0:T(8,128)(2,1)}, bf16[1000,384]{1,0:T(8,128)(2,1)}, bf16[1000,768]{1,0:T(8,128)(2,1)}) custom-call(bf16[1000,768]{1,0:T(8,128)(2,1)} %maximum_select_fusion.x_ref.refs_21_, bf16[3,768,384]{2,1,0:T(8,128)(2,1)} %refs_17_.1, f32[1,1152]{1,0:T(1,128)} %broadcast_in_dim.11.b_ref, bf16[384,768]{1,0:T(8,128)(2,1)} %refs_18_.1, ...), custom_call_target="tpu_custom_call" | custom-call | flops 2359296000 | bytes 8503296 | tf_op jit(solution)/shard_map/self_forward/pallas_call | solution.py:156
  19.4 0.0 collective-permute-start.1
  19.5 0.0 copy-done.7
  19.5 0.0 copy-done.8
  19.5 0.0 copy-done.9
  19.5 0.5 collective-permute-start.2
  20.0 11.2 %project_patches.1 = (bf16[4000,384]{1,0:T(8,128)(2,1)}, bf16[4000,384]{1,0:T(8,128)(2,1)}) custom-call(bf16[25,145,1024]{2,1,0:T(8,128)(2,1)} %p_ref.3, bf16[2,1024,384]{2,1,0:T(8,128)(2,1)} %w_ref.13, bf16[2,384]{1,0:T(2,128)(2,1)} %b_ref.3), custom_call_target="tpu_custom_call" | custom-call | flops 6291456000 | bytes 15140864 | tf_op jit(solution)/shard_map/project_patches/pallas_call | solution.py:115
  31.2 0.0 copy-done.13
  31.2 0.5 broadcast_subtract_fusion.pick
  31.7 0.0 collective-permute-done.2
  31.7 0.6 fusion.pr_ref.refs_13_
  32.3 0.0 collective-permute-done.1.t_ref
  32.3 1.1 copy-done.1
  33.5 19.4 %cross_forward.1 = (f32[1000,768]{1,0:T(8,128)}, f32[1000,1]{1,0:T(8,128)}, bf16[1000,768]{1,0:T(8,128)(2,1)}, bf16[1000,384]{1,0:T(8,128)(2,1)}, bf16[1000,384]{1,0:T(8,128)(2,1)}, /*index=5*/bf16[1000,768]{1,0:T(8,128)(2,1)}) custom-call(s32[25]{0:T(128)} %broadcast_subtract_fusion.pick, bf16[1000,768]{1,0:T(8,128)(2,1)} %maximum_select_fusion.x_ref.refs_21_, ...), custom_call_target="tpu_custom_call" | custom-call | flops 2162688000 | bytes 16896000 | tf_op jit(solution)/shard_map/cross_forward/pallas_call | solution.py:230
  52.9 0.1 collective-permute-start.3
  53.0 0.0 copy-done.10
  53.0 0.6 broadcast_in_dim.12.b_ref
  53.6 2.9 %collective-permute-done.3.t_ref = bf16[1000,768]{1,0:T(8,128)(2,1)S(1)} collective-permute-done((bf16[1000,768]{1,0:T(8,128)(2,1)}, bf16[1000,768]{1,0:T(8,128)(2,1)S(1)}, u32[]{:S(2)}, u32[]{:S(2)}) %collective-permute-start.3) | collective-permute-done | bytes 1536032 | tf_op jit(solution)/shard_map/ppermute | solution.py:1322
  56.5 1.1 copy-done.12
  57.6 12.1 %ffn_forward.1 = (f32[1000,768]{1,0:T(8,128)}, f32[1000,1]{1,0:T(8,128)}, bf16[1000,768]{1,0:T(8,128)(2,1)}, bf16[1000,1536]{1,0:T(8,128)(2,1)}, bf16[1000,1536]{1,0:T(8,128)(2,1)}, /*index=5*/bf16[1000,768]{1,0:T(8,128)(2,1)}) custom-call(f32[1000,768]{1,0:T(8,128)} %get-tuple-element.94.n1_ref.refs_14_, bf16[1000,768]{1,0:T(8,128)(2,1)} %get-tuple-element.95.m_ref, ...), custom_call_target="tpu_custom_call" | custom-call | flops 4718592000 | bytes 23150592 | tf_op jit(solution)/shard_map/ffn_forward/pallas_call | solution.py:275
  69.8 0.2 collective-permute-start.4
  70.0 0.0 copy-done.5
  70.0 0.4 collective-permute-start.5
  70.3 3.9 %collective-permute-done.5 = bf16[1000,384]{1,0:T(8,128)(2,1)S(1)} collective-permute-done((bf16[1000,384]{1,0:T(8,128)(2,1)S(1)}, bf16[1000,384]{1,0:T(8,128)(2,1)S(1)}, u32[]{:S(2)}, u32[]{:S(2)}) %collective-permute-start.5) | collective-permute-done | bytes 768032 | tf_op jit(solution)/shard_map/ppermute | solution.py:1322
  74.3 1.5 maximum_select_fusion.1.e_ref
  75.8 0.0 collective-permute-done.4.t_ref
  75.8 1.1 copy-done.11
  77.0 14.9 %ffn_backward.1 = (f32[1000,384]{1,0:T(8,128)}, f32[1000,768]{1,0:T(8,128)}, bf16[1000,768]{1,0:T(8,128)(2,1)}, bf16[1000,1536]{1,0:T(8,128)(2,1)}, bf16[1000,768]{1,0:T(8,128)(2,1)}, /*index=5*/f32[8,768]{1,0:T(8,128)}) custom-call(s32[1]{0:T(128)} %bitcast.side_ref, f32[1000,768]{1,0:T(8,128)} %get-tuple-element.96.n2_ref.n_ref, ...), custom_call_target="tpu_custom_call" | custom-call | flops 4718592000 | bytes 27758592 | tf_op jit(solution)/shard_map/ffn_backward/pallas_call | solution.py:333
  91.9 0.2 collective-permute-start.6
  92.0 0.5 shift-right-arithmetic_and_fusion.bits_ref
  92.5 14.8 %grad_ffn.1 = (bf16[8,48,1024]{2,1,0:T(8,128)(2,1)}, bf16[8,48,1024]{2,1,0:T(8,128)(2,1)}, bf16[8,48,1024]{2,1,0:T(8,128)(2,1)}, bf16[8,48,1024]{2,1,0:T(8,128)(...) custom-call(s32[4]{0:T(128)} %shift-right-arithmetic_and_fusion.bits_ref, ...), custom_call_target="tpu_custom_call" | custom-call | flops 4718592000 | bytes 12398592 | tf_op jit(solution)/shard_map/grad_ffn/pallas_call | solution.py:675
  107.3 2.9 %collective-permute-start.7 = (bf16[8,48,1024]{2,1,0:T(8,128)(2,1)}, bf16[8,48,1024]{2,1,0:T(8,128)(2,1)S(1)}, u32[]{:S(2)}, u32[]{:S(2)}) collective-permute-start(bf16[8,48,1024]{2,1,0:T(8,128)(2,1)} %get-tuple-element.106), channel_id=1, source_target_pairs={{0,2},{2,0},{4,6},{6,4},{8,10},{10,8},{12,14},{14,12},{16,18},{18,... | collective-permute-start | bytes 2359304 | tf_op jit(solution)/shard_map/ppermute | solution.py:1257
  110.2 1.5 collective-permute-start.8
  111.8 1.6 collective-permute-start.9
  113.3 0.0 collective-permute-done.6.t_ref
  113.3 1.1 copy-done
  114.5 30.0 %cross_backward.1 = (f32[1000,768]{1,0:T(8,128)}, bf16[1000,768]{1,0:T(8,128)(2,1)}, bf16[1000,384]{1,0:T(8,128)(2,1)}, bf16[1000,768]{1,0:T(8,128)(2,1)}, bf16[4000,768]{1,0:T(8,128)(2,1)}, /*index=5*/f32[8,768]{1,0:T(8,128)}) custom-call(s32[25]{0:T(128)} %broadcast_subtract_fusion.pick, f32[1000,768]{1,0:T(8,128)} %get-tuple-element.100.g_ref, ...), custom_call_target="tpu_custom_call" | custom-call | flops 3637248000 | bytes 27648000 | tf_op jit(solution)/shard_map/cross_backward/pallas_call | solution.py:420
  144.5 0.0 collective-permute-done.7.refs_1_
  144.5 0.0 copy-start.2
  144.5 0.0 collective-permute-done.8.refs_3_
  144.5 0.0 copy-start.3
  144.5 0.0 collective-permute-done.9.refs_5_
  144.5 0.0 copy-start.4
  144.5 0.9 copy-done.2
  145.4 0.2 copy-done.3
  145.6 0.3 copy-done.4
  145.9 41.1 %rows_backward.1 = (f32[1000,384]{1,0:T(8,128)}, bf16[1000,384]{1,0:T(8,128)(2,1)}, f32[8,768]{1,0:T(8,128)}, f32[48,3072]{1,0:T(8,128)}, bf16[8,48,512]{2,1,0:T...) custom-call(bf16[8,48,1024]{2,1,0:T(8,128)(2,1)} %get-tuple-element., ...), custom_call_target="tpu_custom_call" | custom-call | flops 5898240000 | bytes 23040000 | tf_op jit(solution)/shard_map/rows_backward/pallas_call | solution.py:1005
  187.0 0.1 collective-permute-start.10
  187.1 59.9 %patch_backward.1 = (bf16[25,145,512]{2,1,0:T(8,128)(2,1)}, f32[48,768]{1,0:T(8,128)}, f32[48,1536]{1,0:T(8,128)}, f32[64,768]{1,0:T(8,128)}, f32[16,768]{1,0:T(8,128)}) custom-call(bf16[25,145,1024]{2,1,0:T(8,128)(2,1)} %p_ref.3, bf16[4000,768]{1,0:T(8,128)(2,1)} %get-tuple-element.112.g_ref, bf16[2,1024,384]{2,1,0:T(8,128)(2,1)} %w_ref.13, ...), custom_call_target="tpu_custom_call" | custom-call | flops 12582912000 | bytes 33280000 | tf_op jit(solution)/shard_map/patch_backward/pallas_call | solution.py:1169
  247.0 0.0 collective-permute-done.10.t_ref
  247.1 0.0 copy-start.6
  247.1 0.9 copy-done.6
  247.9 8.4 %finish.1 = (f32[25,145,512]{2,1,0:T(8,128)}, f32[1000,384]{1,0:T(8,128)}, f32[3,48,384]{2,1,0:T(8,128)}, f32[48,384]{1,0:T(8,128)}, f32[48,384]{1,0:T(8,128)}, ...) custom-call(s32[1]{0:T(128)} %bitcast.side_ref, ...), custom_call_target="tpu_custom_call" | custom-call | flops 1856000 | bytes 11136000 | tf_op jit(solution)/shard_map/finish/pallas_call | solution.py:1227
  256.4 1.3 reduce.2
  (12 shorter events, 0.0 us)
Async XLA Ops:
  0.6 4.4 %collective-permute-start = (bf16[1000,384]{1,0:T(8,128)(2,1)}, bf16[1000,384]{1,0:T(8,128)(2,1)S(1)}, u32[]{:S(2)}, u32[]{:S(2)}) collective-permute-start(bf16[1000,384]{1,0:T(8,128)(2,1)} %param.18), channel_id=1, source_target_pairs={{0,1},{1,0},{2,3},{3,2},{4,5},{5,4},{6,7},{7,6},{8,9},{9,8},{10,11... | collective-permute-start | bytes 2304008 | tf_op jit(solution)/shard_map/ppermute | solution.py:1322
  8.0 11.4 %copy-start.7 = (bf16[3,384]{1,0:T(4,128)(2,1)S(1)}, bf16[3,384]{1,0:T(4,128)(2,1)}, u32[]{:S(2)}) copy-start(bf16[3,384]{1,0:T(4,128)(2,1)} %param.34) | copy-start | bytes 6916
  8.0 11.4 %copy-start.8 = (bf16[3,384]{1,0:T(4,128)(2,1)S(1)}, bf16[3,384]{1,0:T(4,128)(2,1)}, u32[]{:S(2)}) copy-start(bf16[3,384]{1,0:T(4,128)(2,1)} %param.33) | copy-start | bytes 6916
  8.0 11.4 %copy-start.9 = (bf16[3,384]{1,0:T(4,128)(2,1)S(1)}, bf16[3,384]{1,0:T(4,128)(2,1)}, u32[]{:S(2)}) copy-start(bf16[3,384]{1,0:T(4,128)(2,1)} %param.32) | copy-start | bytes 6916
  19.4 12.9 %collective-permute-start.1 = (bf16[1000,768]{1,0:T(8,128)(2,1)}, bf16[1000,768]{1,0:T(8,128)(2,1)S(1)}, u32[]{:S(2)}, u32[]{:S(2)}) collective-permute-start(bf16[1000,768]{1,0:T(8,128)(2,1)} %get-tuple-element.91.m_ref), channel_id=1, source_target_pairs={{0,1},{1,0},{2,3},{3,2},{4,5},{5,4},{6,7},{7,6},{8,9},{9,8},{10,11... | collective-permute-start | bytes 4608008 | tf_op jit(solution)/shard_map/ppermute | solution.py:1322
  19.5 12.2 %collective-permute-start.2 = (bf16[9,384]{1,0:T(8,128)(2,1)S(1)}, bf16[9,384]{1,0:T(8,128)(2,1)S(1)}, u32[]{:S(2)}, u32[]{:S(2)}) collective-permute-start(bf16[9,384]{1,0:T(8,128)(2,1)S(1)} %pad_maximum_fusion), channel_id=1, source_target_pairs={{0,1},{1,0},{2,3},{3,2},{4,5},{5,4},{6,7},{7,6},{8,9},{9,8},{10,11... | collective-permute-start | bytes 20744 | tf_op jit(solution)/shard_map/ppermute | solution.py:1322
  20.0 11.2 %copy-start.13 = (s32[25]{0:T(128)S(1)}, s32[25]{0:T(128)}, u32[]{:S(2)}) copy-start(s32[25]{0:T(128)} %param.21) | copy-start | bytes 304
  32.3 1.1 copy-start.1
  33.5 19.5 %copy-start.10 = (bf16[1536]{0:T(1024)(128)(2,1)S(1)}, bf16[1536]{0:T(1024)(128)(2,1)}, u32[]{:S(2)}) copy-start(bf16[1536]{0:T(1024)(128)(2,1)} %param.30) | copy-start | bytes 9220
  52.9 3.6 %collective-permute-start.3 = (bf16[1000,768]{1,0:T(8,128)(2,1)}, bf16[1000,768]{1,0:T(8,128)(2,1)S(1)}, u32[]{:S(2)}, u32[]{:S(2)}) collective-permute-start(bf16[1000,768]{1,0:T(8,128)(2,1)} %get-tuple-element.95.m_ref), channel_id=1, source_target_pairs={{0,1},{1,0},{2,3},{3,2},{4,5},{5,4},{6,7},{7,6},{8,9},{9,8},{10,11... | collective-permute-start | bytes 4608008 | tf_op jit(solution)/shard_map/ppermute | solution.py:1322
  56.5 1.1 copy-start.12
  57.6 12.3 %copy-start.5 = (bf16[1000,384]{1,0:T(8,128)(2,1)S(1)}, bf16[1000,384]{1,0:T(8,128)(2,1)}, u32[]{:S(2)}) copy-start(bf16[1000,384]{1,0:T(8,128)(2,1)} %param.35) | copy-start | bytes 2304004
  69.8 6.0 %collective-permute-start.4 = (bf16[1000,768]{1,0:T(8,128)(2,1)}, bf16[1000,768]{1,0:T(8,128)(2,1)S(1)}, u32[]{:S(2)}, u32[]{:S(2)}) collective-permute-start(bf16[1000,768]{1,0:T(8,128)(2,1)} %get-tuple-element.97.m_ref), channel_id=1, source_target_pairs={{0,1},{1,0},{2,3},{3,2},{4,5},{5,4},{6,7},{7,6},{8,9},{9,8},{10,11... | collective-permute-start | bytes 4608008 | tf_op jit(solution)/shard_map/ppermute | solution.py:1322
  70.0 4.3 %collective-permute-start.5 = (bf16[1000,384]{1,0:T(8,128)(2,1)S(1)}, bf16[1000,384]{1,0:T(8,128)(2,1)S(1)}, u32[]{:S(2)}, u32[]{:S(2)}) collective-permute-start(bf16[1000,384]{1,0:T(8,128)(2,1)S(1)} %copy-done.5), channel_id=1, source_target_pairs={{0,1},{1,0},{2,3},{3,2},{4,5},{5,4},{6,7},{7,6},{8,9},{9,8},{10,11... | collective-permute-start | bytes 2304008 | tf_op jit(solution)/shard_map/ppermute | solution.py:1322
  75.8 1.1 copy-start.11
  91.9 21.5 %collective-permute-start.6 = (bf16[1000,768]{1,0:T(8,128)(2,1)}, bf16[1000,768]{1,0:T(8,128)(2,1)S(1)}, u32[]{:S(2)}, u32[]{:S(2)}) collective-permute-start(bf16[1000,768]{1,0:T(8,128)(2,1)} %get-tuple-element.109.m_ref), channel_id=1, source_target_pairs={{0,1},{1,0},{2,3},{3,2},{4,5},{5,4},{6,7},{7,6},{8,9},{9,8},{10,11... | collective-permute-start | bytes 4608008 | tf_op jit(solution)/shard_map/ppermute | solution.py:1322
  107.3 37.2 %collective-permute-start.7 = (bf16[8,48,1024]{2,1,0:T(8,128)(2,1)}, bf16[8,48,1024]{2,1,0:T(8,128)(2,1)S(1)}, u32[]{:S(2)}, u32[]{:S(2)}) collective-permute-start(bf16[8,48,1024]{2,1,0:T(8,128)(2,1)} %get-tuple-element.106), channel_id=1, source_target_pairs={{0,2},{2,0},{4,6},{6,4},{8,10},{10,8},{12,14},{14,12},{16,18},{18,... | collective-permute-start | bytes 2359304 | tf_op jit(solution)/shard_map/ppermute | solution.py:1257
  110.2 34.3 %collective-permute-start.8 = (bf16[8,48,1024]{2,1,0:T(8,128)(2,1)}, bf16[8,48,1024]{2,1,0:T(8,128)(2,1)S(1)}, u32[]{:S(2)}, u32[]{:S(2)}) collective-permute-start(bf16[8,48,1024]{2,1,0:T(8,128)(2,1)} %get-tuple-element.107), channel_id=1, source_target_pairs={{0,4},{2,6},{4,0},{6,2},{8,12},{10,14},{12,8},{14,10},{16,20},{18,... | collective-permute-start | bytes 2359304 | tf_op jit(solution)/shard_map/ppermute | solution.py:1257
  111.8 32.8 %collective-permute-start.9 = (bf16[8,48,1024]{2,1,0:T(8,128)(2,1)}, bf16[8,48,1024]{2,1,0:T(8,128)(2,1)S(1)}, u32[]{:S(2)}, u32[]{:S(2)}) collective-permute-start(bf16[8,48,1024]{2,1,0:T(8,128)(2,1)} %get-tuple-element.108), channel_id=1, source_target_pairs={{0,8},{2,10},{4,12},{6,14},{8,0},{10,2},{12,4},{14,6},{16,24},{18,... | collective-permute-start | bytes 2359304 | tf_op jit(solution)/shard_map/ppermute | solution.py:1257
  113.3 1.1 copy-start
  144.5 0.9 copy-start.2
  144.5 1.1 copy-start.3
  144.5 1.4 copy-start.4
  187.0 60.0 %collective-permute-start.10 = (bf16[1000,384]{1,0:T(8,128)(2,1)}, bf16[1000,384]{1,0:T(8,128)(2,1)S(1)}, u32[]{:S(2)}, u32[]{:S(2)}) collective-permute-start(bf16[1000,384]{1,0:T(8,128)(2,1)} %get-tuple-element.145), channel_id=1, source_target_pairs={{0,1},{1,0},{2,3},{3,2},{4,5},{5,4},{6,7},{7,6},{8,9},{9,8},{10,11... | collective-permute-start | bytes 2304008 | tf_op jit(solution)/shard_map/ppermute | solution.py:1322
  247.1 0.9 copy-start.6

commit v3 on v2

--- a/solution.py
+++ b/solution.py
@@ -93,6 +93,65 @@
     return e * (1.0 / jnp.sum(e, axis=1, keepdims=True))
 
 
+MESH = pl.DeviceIdType.MESH
+
+
+def digit(bit):
+    return (lax.axis_index("dp") // (1 << bit)) % 2
+
+
+def partner(bit):
+    dp_at, mp_at = lax.axis_index("dp"), lax.axis_index("mp")
+    if bit is None:
+        return {"dp": dp_at, "mp": 1 - mp_at}
+    return {"dp": dp_at + (1 << bit) - 2 * (1 << bit) * digit(bit), "mp": mp_at}
+
+
+def remote(source, target, send_sem, got_sem, bit):
+    return pltpu.make_async_remote_copy(
+        src_ref=source, dst_ref=target, send_sem=send_sem, recv_sem=got_sem,
+        device_id=partner(bit), device_id_type=MESH,
+    )
+
+
+def greet(links):
+    barrier = pltpu.get_barrier_semaphore()
+    for bit in links:
+        pl.semaphore_signal(barrier, inc=1, device_id=partner(bit), device_id_type=MESH)
+
+
+def met(links):
+    pl.semaphore_wait(pltpu.get_barrier_semaphore(), len(links))
+
+
+class Swap:
+    def __init__(self, tiles, tile, width):
+        self.tiles = tiles
+        self.shape = (tiles, tile, width)
+        self.scratch = [pltpu.VMEM(self.shape, BF)] + [pltpu.SemaphoreType.DMA((tiles,))] * 2
+
+    def bind(self, target, refs):
+        self.target = target
+        self.buffer, self.send, self.got = refs
+
+    def copy(self, tile):
+        return remote(self.buffer.at[tile], self.target.at[tile], self.send.at[tile],
+                      self.got.at[tile], None)
+
+    def put(self, tile, value):
+        @pl.when(tile == 0)
+        def _():
+            met((None,))
+
+        self.buffer[tile] = value
+        self.copy(tile).start()
+
+        @pl.when(tile == self.tiles - 1)
+        def _():
+            for i in range(self.tiles):
+                self.copy(i).wait()
+
+
 def project_patches(patches, cross_kv, bias, padded):
     images, count, visual = patches.shape
     width = cross_kv.shape[2]
@@ -124,16 +183,21 @@
     )(patches, cross_kv, bias)
 
 
-def self_forward(text, qkv_w, qkv_b, out_w, ids_col, ids_row, tile):
-    tokens, width = text.shape
-    here = out_w.shape[0]
-
-    def body(x_ref, w_ref, b_ref, o_ref, ic_ref, ir_ref, qkv_ref, c_ref, part_ref, wcat):
+def self_forward(side, own, other, qkv_w, qkv_b, out_w, ids_col, ids_row, tile):
+    tokens, here = own.shape
+    width = 2 * here
+
+    def body(side_ref, a_ref, z_ref, w_ref, b_ref, o_ref, ic_ref, ir_ref,
+             qkv_ref, c_ref, part_ref, x_ref, wcat):
         @pl.when(pl.program_id(0) == 0)
         def _():
             for s in range(3):
                 wcat[:, s * here : (s + 1) * here] = w_ref[s]
 
+        mine, theirs = a_ref[...], z_ref[...]
+        first = side_ref[0] == 0
+        x_ref[:, :here] = jnp.where(first, mine, theirs)
+        x_ref[:, here:] = jnp.where(first, theirs, mine)
         qkv = (nn(x_ref[...], wcat[...]) + b_ref[...]).astype(BF)
         qkv_ref[...] = qkv
         same = ic_ref[...] == ir_ref[0]
@@ -158,7 +222,8 @@
         "self_forward",
         tokens // tile,
         [
-            tiled((tile, width)),
+            tiled((tile, here)),
+            tiled((tile, here)),
             whole(qkv_w.shape),
             whole(qkv_b.shape),
             whole(out_w.shape),
@@ -169,11 +234,13 @@
             ((tokens, 3 * here), BF, tiled((tile, 3 * here))),
             ((tokens, here), BF, tiled((tile, here))),
             ((tokens, width), BF, tiled((tile, width))),
+            ((tokens, width), BF, tiled((tile, width))),
         ],
         [pltpu.VMEM((width, 3 * here), BF)],
         2 * tokens * width * 4 * here,
         tokens * (width + 4 * here + width) * 2 + 4 * width * here * 2,
-    )(text, qkv_w, qkv_b, out_w, ids_col, ids_row)
+        scalars=1,
+    )(side, own, other, qkv_w, qkv_b, out_w, ids_col, ids_row)
 
 
 def quads(here):
@@ -199,9 +266,18 @@
     tokens, width = text.shape
     here = out_w.shape[0]
     rows = tile // length
+    swap = Swap(tokens // tile, tile, width)
+    keys = keys.reshape(-1, padded, here)
+    values = values.reshape(-1, padded, here)
 
     def body(pick, x_ref, m_ref, t_ref, pr_ref, w_ref, b_ref, k_ref, v_ref, o_ref,
-             n_ref, r_ref, y_ref, q_ref, c_ref, part_ref, q32, c32):
+             n_ref, r_ref, y_ref, q_ref, c_ref, part_ref, got_ref, q32, c32, *swap_refs):
+        swap.bind(got_ref, swap_refs)
+
+        @pl.when(pl.program_id(0) == 0)
+        def _():
+            greet((None,))
+
         h = x_ref[...].astype(F32) + (m_ref[...].astype(F32) + t_ref[...].astype(F32)) + pr_ref[0:1, :]
         n, r = norm(h)
         n_ref[...] = n
@@ -213,17 +289,20 @@
         q_ref[...] = q.astype(BF)
         base = pl.program_id(0) * rows
         for j in range(rows):
-            at = pl.multiple_of(pick[base + j] * padded, padded)
+            k_row = k_ref[pick[base + j]]
+            v_row = v_ref[pick[base + j]]
             for lo, span in quads(here):
                 qs = stacked(q32[j * length : (j + 1) * length, lo : lo + span], span)
-                s = nt(qs, k_ref[pl.ds(at, padded), lo : lo + span]) * SCALE
+                s = nt(qs, k_row[:, lo : lo + span]) * SCALE
                 live = lax.broadcasted_iota(jnp.int32, s.shape, 1) < count
                 p = softmax_rows(jnp.where(live, s, -1e30))
-                o = nn(p.astype(BF), v_ref[pl.ds(at, padded), lo : lo + span])
+                o = nn(p.astype(BF), v_row[:, lo : lo + span])
                 c32[j * length : (j + 1) * length, lo : lo + span] = unstacked(o, span, length)
         c = c32[...].astype(BF)
         c_ref[...] = c
-        part_ref[...] = nn(c, o_ref[...]).astype(BF)
+        part = nn(c, o_ref[...]).astype(BF)
+        part_ref[...] = part
+        swap.put(pl.program_id(0), part)
 
     full = tiled((tile, width))
     half = tiled((tile, here))
@@ -240,20 +319,29 @@
             ((tokens, here), BF, half),
             ((tokens, here), BF, half),
             ((tokens, width), BF, full),
+            (swap.shape, BF, pl.BlockSpec(memory_space=pl.ANY)),
         ],
-        [pltpu.VMEM((tile, here), F32)] * 2,
+        [pltpu.VMEM((tile, here), F32)] * 2 + swap.scratch,
         2 * tokens * width * 2 * here + 4 * tokens * padded * here * 4,
         tokens * width * 14 + keys.size * 4,
         scalars=1,
+        collective=3,
     )(picks, text, mine, other, params, query_w, query_b, keys, values, out_w)
 
 
 def ffn_forward(normed, mine, other, params, in_w, in_b, out_w, tile):
     tokens, width = normed.shape
     hidden = in_w.shape[1]
+    swap = Swap(tokens // tile, tile, width)
 
     def body(n1_ref, m_ref, t_ref, pr_ref, w_ref, b_ref, o_ref,
-             n_ref, r_ref, y_ref, g_ref, d_ref, part_ref):
+             n_ref, r_ref, y_ref, g_ref, d_ref, part_ref, got_ref, *swap_refs):
+        swap.bind(got_ref, swap_refs)
+
+        @pl.when(pl.program_id(0) == 0)
+        def _():
+            greet((None,))
+
         h = (n1_ref[...] * pr_ref[3:4, :] + pr_ref[6:7, :]) + (
             m_ref[...].astype(F32) + t_ref[...].astype(F32)
         ) + pr_ref[1:2, :]
@@ -268,7 +356,9 @@
         g_ref[...] = g
         density = jnp.exp(u * u * -0.5) * (1.0 / math.sqrt(2.0 * math.pi))
         d_ref[...] = (phi + u * density).astype(BF)
-        part_ref[...] = nn(g, o_ref[...]).astype(BF)
+        part = nn(g, o_ref[...]).astype(BF)
+        part_ref[...] = part
+        swap.put(pl.program_id(0), part)
 
     full = tiled((tile, width))
     wide = tiled((tile, hidden))
@@ -285,10 +375,12 @@
             ((tokens, hidden), BF, wide),
             ((tokens, hidden), BF, wide),
             ((tokens, width), BF, full),
+            (swap.shape, BF, pl.BlockSpec(memory_space=pl.ANY)),
         ],
-        [],
+        swap.scratch,
         2 * tokens * width * 2 * hidden,
         tokens * width * 16 + tokens * hidden * 4 + width * hidden * 4,
+        collective=4,
     )(normed, mine, other, params, in_w, in_b, out_w)
 
 
@@ -441,7 +533,7 @@
 
 
 def self_tile(grad, mine, other, pr_ref, n, r, q_ref, wt, ot, same, sum_ref, keep_ref, send_ref,
-              first, here):
+              first, here, between=None):
     e = grad + (mine.astype(F32) + other.astype(F32))
     dh = norm_back(e, n, r, pr_ref[3:4, :])
     dhb = dh.astype(BF)
@@ -451,6 +543,8 @@
     dc = nn(dhb, ot[...]).astype(BF)
     grads = [[], [], []]
     for p in range(here // 128):
+        if between is not None:
+            between(p)
         q = q_ref[:, 128 * p : 128 * p + 128]
         k = q_ref[:, here + 128 * p : here + 128 * p + 128]
         v = q_ref[:, 2 * here + 128 * p : 2 * here + 128 * p + 128]
@@ -741,35 +835,7 @@
 
 ORDERS = ((0, 1, 2, 3), (1, 2, 0, 3), (2, 0, 1, 3))
 LINKS = (None, 0, 1, 2, 3)
-MESH = pl.DeviceIdType.MESH
-
-
-def digit(bit):
-    return (lax.axis_index("dp") // (1 << bit)) % 2
-
-
-def partner(bit):
-    dp_at, mp_at = lax.axis_index("dp"), lax.axis_index("mp")
-    if bit is None:
-        return {"dp": dp_at, "mp": 1 - mp_at}
-    return {"dp": dp_at + (1 << bit) - 2 * (1 << bit) * digit(bit), "mp": mp_at}
-
-
-def remote(source, target, send_sem, got_sem, bit):
-    return pltpu.make_async_remote_copy(
-        src_ref=source, dst_ref=target, send_sem=send_sem, recv_sem=got_sem,
-        device_id=partner(bit), device_id_type=MESH,
-    )
-
-
-def greet():
-    barrier = pltpu.get_barrier_semaphore()
-    for bit in LINKS:
-        pl.semaphore_signal(barrier, inc=1, device_id=partner(bit), device_id_type=MESH)
-
-
-def met():
-    pl.semaphore_wait(pltpu.get_barrier_semaphore(), len(LINKS))
+FFN_STEPS = ((2, 0), (3, 2))
 
 
 class Stream:
@@ -885,20 +951,20 @@
 
         @pl.when(at == 0)
         def _():
-            greet()
+            greet(LINKS)
             for load in loads:
                 load.start()
             lt[...] = l0_ref[...].T
             sum_ref[...] = jnp.zeros_like(sum_ref)
-            met()
+            met(LINKS)
             part_copy.start()
+            for which, stream in enumerate(ffn):
+                loads[2 * which].wait()
+                loads[2 * which + 1].wait()
+                stream.fold(0, stream.pairs[1])
+                stream.start(1)
             acc[...] = nn(lt[...], r0_ref[...])
             full[:, :here] = acc[...].astype(BF)
-            for load in loads:
-                load.wait()
-            for stream in ffn:
-                stream.fold(0, stream.pairs[1])
-                stream.start(1)
 
         @pl.when(at == 1)
         def _():
@@ -913,17 +979,18 @@
             ot[...] = o_ref[...].T
             part_copy.wait()
 
-        @pl.when(at == begin + 2)
-        def _():
-            for stream in ffn:
-                stream.advance(1)
-
-        @pl.when(at == begin + 4)
-        def _():
-            for stream in ffn:
-                stream.advance(2)
-            for stream in cross:
-                stream.start(0)
+        def between(pair):
+            for t, (step, place) in enumerate(FFN_STEPS):
+                if pair != place:
+                    continue
+
+                @pl.when(at == begin + step)
+                def _(t=t):
+                    for stream in ffn:
+                        stream.advance(t + 1)
+                    if t == 1:
+                        for stream in cross:
+                            stream.start(0)
 
         @pl.when((at >= begin) & (at < after_self))
         def _():
@@ -931,6 +998,7 @@
             dhb, dqkv = self_tile(
                 g_ref[...], mine_ref[...], other[i], pr_ref, n_ref[...], r_ref[...], q_ref,
                 wt, ot, ic_ref[...] == ir_ref[0], sum_ref, keep_ref, send_ref, side == 0, here,
+                between,
             )
             for j in range(tiles):
                 @pl.when(i == j)
@@ -1030,7 +1098,8 @@
         firsts = [refs[2 * i : 2 * i + 2] for i in range(6)]
         out_ref, cross_ref, self_ref, kv_ref, sum_ref = refs[12:17]
         rows, acc, wt, send, got, send_sem, got_sem, sum_now, sum_got, sum_sems = refs[17:27]
-        rest = refs[27:]
+        p_all, g_all, load_sems, out_sems = refs[27:31]
+        rest = refs[31:]
         for which, stream in enumerate(cross):
             rest = stream.bind(rest, 2, firsts[which])
         for which, stream in enumerate(selves):
@@ -1043,57 +1112,81 @@
         def patch_copy(tile):
             return remote(send.at[tile], got.at[tile], send_sem.at[tile], got_sem.at[tile], None)
 
+        def loads(tile):
+            images_at = pl.ds(tile * group, group)
+            rows_at = pl.ds(pl.multiple_of(tile * group * padded, 16), group * padded)
+            return (
+                pltpu.make_async_copy(p_ref.at[images_at], p_all.at[tile], load_sems.at[2 * tile]),
+                pltpu.make_async_copy(g_ref.at[rows_at], g_all.at[tile], load_sems.at[2 * tile + 1]),
+            )
+
+        def store(tile):
+            images_at = pl.ds(tile * group, group)
+            return pltpu.make_async_copy(send.at[tile], out_ref.at[images_at], out_sems.at[tile])
+
         def sum_copy(bit):
             return remote(sum_now.at[bit], sum_got.at[bit], sum_sems.at[bit],
                           sum_sems.at[4 + bit], bit)
 
         @pl.when(at == 0)
         def _():
-            greet()
+            greet(LINKS)
+            for tile in range(steps):
+                for load in loads(tile):
+                    load.start(priority=1)
             rows[...] = jnp.zeros_like(rows)
             sum_now[0, :8] = s3_ref[...]
             sum_now[0, 8:12] = s1_ref[0:4]
             sum_now[0, 12:16] = s2_ref[0:4]
-            met()
+            met(LINKS)
+            sum_copy(0).start()
             for stream in selves:
                 stream.start(0)
-            sum_copy(0).start()
             for stream in cross:
                 stream.start(1)
             wt[:width, :] = w_ref[0].T
             wt[width:, :] = w_ref[1].T
 
-        for bit in range(4):
-            @pl.when(at == bit + 1)
-            def _(bit=bit):
-                sum_copy(bit).wait()
-                total = sum_now[bit] + sum_got[bit]
-                if bit == 3:
-                    sum_ref[...] = total
-                else:
-                    sum_now[bit + 1] = total
-                    sum_copy(bit + 1).start()
-
-        def plan(step, streams, t):
-            @pl.when(at == step)
-            def _():
-                for stream in streams:
-                    stream.advance(t)
-
-        plan(3, cross, 1)
-        plan(5, cross, 2)
-        plan(5, selves, 0)
-        plan(9, selves, 1)
-        plan(11, selves, 2)
-        plan(12, kvs, 0)
-        plan(13, kvs, 1)
-        plan(14, kvs, 2)
+        def sum_next(bit):
+            sum_copy(bit).wait()
+            sum_now[bit + 1] = sum_now[bit] + sum_got[bit]
+            sum_copy(bit + 1).start()
+
+        def advance(streams, t):
+            for stream in streams:
+                stream.advance(t)
+
+        @pl.when(at == steps - 1)
+        def _():
+            sum_next(0)
+            advance(selves, 0)
+            advance(cross, 1)
+
+        @pl.when(at == steps + 1)
+        def _():
+            sum_next(1)
+            advance(selves, 1)
+            for stream in kvs:
+                stream.start(0)
+            advance(cross, 2)
+
+        @pl.when(at == steps + 3)
+        def _():
+            sum_next(2)
+            advance(selves, 2)
+
+        for step in range(3):
+            @pl.when(at == 2 * steps + (1, 3, 4)[step])
+            def _(step=step):
+                advance(kvs, step)
 
         @pl.when(at < steps)
         def _():
+            for load in loads(at):
+                load.wait()
             for i in range(group):
-                rows[padded * i : padded * i + count, :] = p_ref[i]
-            new = tn(rows[...], g_ref[...])
+                rows[padded * i : padded * i + count, :] = p_all[at, i]
+            new = tn(rows[...], g_all[at])
 
             @pl.when(at == 0)
             def _():
@@ -1108,16 +1201,15 @@
                 for which, stream in enumerate(kvs):
                     split_shards(acc, slice(which * third, (which + 1) * third), stream.pairs[0],
                                  stream.order[0], size)
-                    stream.start(0)
-
-        def product(half_at):
+
+        def product(tile, half_at):
             lanes = pl.ds(pl.multiple_of(half_at * half, 128), half)
-            return nn(g_ref[...], wt[:, lanes])
+            return nn(g_all[tile], wt[:, lanes])
 
         @pl.when((at >= steps) & (at < 2 * steps))
         def _():
             tile = at - steps
-            out = product(1 - side)
+            out = product(tile, 1 - side)
             for i in range(group):
                 send[tile, i] = out[padded * i : padded * i + count].astype(BF)
             patch_copy(tile).start()
@@ -1125,23 +1217,28 @@
         @pl.when(at >= 2 * steps)
         def _():
             tile = at - 2 * steps
-            out = product(side)
+            out = product(tile, side)
             patch_copy(tile).wait()
             for i in range(group):
                 mine = out[padded * i : padded * i + count]
-                out_ref[i] = (mine + got[tile, i].astype(F32)).astype(BF)
+                send[tile, i] = (mine + got[tile, i].astype(F32)).astype(BF)
+            store(tile).start(priority=1)
 
         @pl.when(at == 3 * steps - 1)
         def _():
+            sum_copy(3).wait()
+            sum_ref[...] = sum_now[3] + sum_got[3]
             for target, streams in ((cross_ref, cross), (self_ref, selves), (kv_ref, kvs)):
                 for which, stream in enumerate(streams):
                     lo = which * stream.columns
                     target[:, lo : lo + stream.columns] = stream.finish()
+            for tile in range(steps):
+                store(tile).wait()
 
     anywhere = pl.BlockSpec(memory_space=pl.ANY)
     ins = [
-        pl.BlockSpec((group, count, visual), lambda i: (jnp.minimum(i, steps - 1), 0, 0)),
-        pl.BlockSpec((group * padded, wide), lambda i: (i % steps, 0)),
+        anywhere,
+        anywhere,
         whole(cross_kv.shape),
     ] + [whole(s.shape) for s in sums]
     operands = [patches, pair, cross_kv, *sums]
@@ -1159,6 +1256,10 @@
         pltpu.VMEM((4, 16, wide), F32),
         pltpu.VMEM((4, 16, wide), F32),
         pltpu.SemaphoreType.DMA((8,)),
+        pltpu.VMEM((steps, group, count, visual), BF),
+        pltpu.VMEM((steps, group * padded, wide), BF),
+        pltpu.SemaphoreType.DMA((2 * steps,)),
+        pltpu.SemaphoreType.DMA((steps,)),
     ]
     for stream in cross:
         scratch += stream.scratch(2)
@@ -1172,8 +1273,7 @@
         3 * steps,
         ins,
         [
-            ((images, count, half), BF,
-             pl.BlockSpec((group, count, half), lambda i: (jnp.maximum(i - 2 * steps, 0), 0, 0))),
+            ((images, count, half), BF, anywhere),
             small_out((small, wide)),
             small_out((small, 3 * self_cols)),
             small_out((size, wide)),
@@ -1365,7 +1465,6 @@
             jnp.concatenate((other, own), axis=1),
         )
 
-    text_full = both(text)
     params = both(jnp.concatenate((branch_bias, norm_gain, norm_bias), axis=0)).astype(F32)
     cot_full = both(cotangent)
 
@@ -1377,18 +1476,19 @@
     qkv_b = jnp.concatenate((self_bias[0].astype(F32), zero, self_bias[1].astype(F32)))[None]
 
     keys, values = project_patches(patches, cross_kv, cross_bias, padded)
-    qkv, context, part_one = self_forward(
-        text_full, self_qkv, qkv_b, self_out, ids_col, ids_row, tile
+    keys, cot_full = lax.optimization_barrier((keys, cot_full))
+    qkv, context, part_one, text_full = self_forward(
+        side, text, swap_mp(text), self_qkv, qkv_b, self_out, ids_col, ids_row, tile
     )
-    n_one, r_one, y_one, query, cross_ctx, part_two = cross_forward(
+    n_one, r_one, y_one, query, cross_ctx, part_two, other_two = cross_forward(
         picks, text_full, part_one, swap_mp(part_one), params, cross_query, cross_bias,
         keys, values, cross_out, tile, length, count, padded,
     )
-    n_two, r_two, y_two, act, slope, part_three = ffn_forward(
-        n_one, part_two, swap_mp(part_two), params, ffn_in, ffn_in_bias[None], ffn_out, tile
+    n_two, r_two, y_two, act, slope, part_three, other_three = ffn_forward(
+        n_one, part_two, other_two.reshape(tokens, -1), params, ffn_in, ffn_in_bias[None], ffn_out, tile
     )
     joined, dh_three, dhb_three, du, part_four, sums_three = ffn_backward(
-        side, n_two, part_three, swap_mp(part_three), params, cot_full, slope, ffn_in, ffn_out,
+        side, n_two, part_three, other_three.reshape(tokens, -1), params, cot_full, slope, ffn_in, ffn_out,
         tile,
     )
     other_four = swap_mp(part_four)

time: 259 us -> 243 us (0.938)
  waiting for transfers between devices: 6.89 us -> 0.02 us
  Pallas kernels: 223 us -> 220 us
  other arithmetic: 9.05 us -> 6.18 us
    pallas_call x1, Pallas kernels: 59.9 us -> 49.9 us  [patch_backward(): call(body, 'patch_backward', 3 * steps, ins, [((images, count, half), BF,...]
    ppermute x8 -> x6, waiting for transfers between devices: 6.88 us -> 0.02 us  [swap_mp(): return lax.ppermute(value, 'mp', [(0, 1), (1, 0)])]
    pallas_call x1, Pallas kernels: 12.1 us -> 15.3 us  [ffn_forward(): call(body, 'ffn_forward', tokens // tile, [full, full, full, whole(params...]
    select_n x2 -> x1, other arithmetic: 4.49 us -> 1.61 us  [both(): jnp.where(mp_at == 0, jnp.concatenate((own, other), axis=1), jnp.concaten...]
    unnamed x28 -> x26, local copies, waits for them, and re-layouts: 6.84 us -> 5.47 us
  transfers between devices with their start and end apart: 11 -> 9, of which waited for: 2 -> 0; matrix products, arithmetic and copies ran while one was open for 3% -> 3% of each run, Pallas kernels for 45% -> 44%
where the time goes in v3:
time: 243 us; the launch traced here: 242 us
  Pallas kernels  220 us (91%)
  local copies, waits for them, and re-layouts  8.36 us (3%)
  starting transfers between devices  7.5 us (3%)
  other arithmetic  6.18 us (3%)
    pallas_call x1, Pallas kernels, patch_backward(): call(body, 'patch_backward', 3 * steps, ins, [((images, count, half), BF,...  49.9 us
    pallas_call x1, Pallas kernels, rows_backward(): call(body, 'rows_backward', steps, ins, outs, scratch, 2 * tokens * width...  41.8 us
    pallas_call x1, Pallas kernels, cross_backward(): call(body, 'cross_backward', steps, [full, full, full, whole(params.shape...  30 us
    pallas_call x1, Pallas kernels, cross_forward(): call(body, 'cross_forward', tokens // tile, [full, full, full, whole(para...  21.7 us
    pallas_call x1, Pallas kernels, ffn_forward(): call(body, 'ffn_forward', tokens // tile, [full, full, full, whole(params...  15.3 us
    pallas_call x1, Pallas kernels, ffn_backward(): call(body, 'ffn_backward', tokens // tile, [full, full, full, whole(param...  14.9 us
    pallas_call x1, Pallas kernels, grad_weight(): call(body, name, total, specs, outs, [pltpu.VMEM((width, tokens), BF), pl...  14.7 us
    pallas_call x1, Pallas kernels, self_forward(): call(body, 'self_forward', tokens // tile, [tiled((tile, here)), tiled((t...  11.7 us
  transfers between devices with their start and end apart: 9, of which 0 were waited for; matrix products, arithmetic and copies ran while one was open for 3% of the time, Pallas kernels for 44%

profile of v3, /device:TPU:0, one launch (start us, length us, event | category | flops | bytes accessed | tf_op | source)
XLA Modules:
  0.0 242.5 jit_solution(3981854869430937375)
XLA Ops:
  0.6 0.5 collective-permute-start
  1.2 0.8 broadcast_add_fusion
  2.0 0.7 reshape.76.ir_ref.refs_20_
  2.6 1.0 reshape.85.ic_ref.refs_19_
  3.7 0.8 convert_reduce_fusion.1
  4.5 0.6 broadcast_in_dim.11.b_ref
  5.1 0.0 collective-permute-done.z_ref
  5.1 0.0 copy-start.11
  5.1 0.9 copy-done.11
  5.9 0.0 copy-start.7
  5.9 0.0 copy-start.8
  5.9 0.0 copy-start.9
  5.9 0.0 copy-start.5
  5.9 11.7 %self_forward.1 = (bf16[1000,1152]{1,0:T(8,128)(2,1)}, bf16[1000,384]{1,0:T(8,128)(2,1)}, bf16[1000,768]{1,0:T(8,128)(2,1)}, bf16[1000,768]{1,0:T(8,128)(2,1)}) custom-call(s32[1]{0:T(128)} %bitcast.side_ref, bf16[1000,384]{1,0:T(8,128)(2,1)} %a_ref.1, bf16[1000,384]{1,0:T(8,128)(2,1)} %copy-done.11, bf16[3,768,384]{2,1,0:T(8,128)(2,1)} %refs_17_.1, ...), custom_call_target="tpu_custom_call" | custom-call | flops 2359296000 | bytes 8503296 | tf_op jit(solution)/shard_map/self_forward/pallas_call | solution.py:220
  17.6 0.1 collective-permute-start.1
  17.7 0.0 copy-done.7
  17.7 0.0 copy-done.8
  17.7 0.0 copy-done.9
  17.8 0.5 collective-permute-start.2
  18.3 0.0 copy-done.5
  18.3 0.1 collective-permute-start.3
  18.4 0.0 copy-start.12
  18.4 11.2 %project_patches.1 = (bf16[4000,384]{1,0:T(8,128)(2,1)}, bf16[4000,384]{1,0:T(8,128)(2,1)}) custom-call(bf16[25,145,1024]{2,1,0:T(8,128)(2,1)} %p_ref.3, bf16[2,1024,384]{2,1,0:T(8,128)(2,1)} %w_ref.13, bf16[2,384]{1,0:T(2,128)(2,1)} %b_ref.3), custom_call_target="tpu_custom_call" | custom-call | flops 6291456000 | bytes 15140864 | tf_op jit(solution)/shard_map/project_patches/pallas_call | solution.py:174
  29.6 0.0 copy-done.12
  29.6 0.5 broadcast_subtract_fusion.pick
  30.1 0.0 copy-done.10
  30.1 0.6 broadcast_in_dim.12.b_ref
  30.7 0.0 collective-permute-done.2
  30.7 0.6 fusion.pr_ref.refs_13_
  31.3 0.0 collective-permute-done.3
  31.3 1.6 maximum_select_fusion.e_ref
  32.9 0.0 collective-permute-done.1.t_ref
  32.9 0.0 copy-start.1
  32.9 1.1 copy-done.1
  34.1 21.7 %cross_forward.1 = (f32[1000,768]{1,0:T(8,128)}, f32[1000,1]{1,0:T(8,128)}, bf16[1000,768]{1,0:T(8,128)(2,1)}, bf16[1000,384]{1,0:T(8,128)(2,1)}, bf16[1000,384]...) custom-call(s32[25]{0:T(128)} %broadcast_subtract_fusion.pick, ...), custom_call_target="tpu_custom_call" | custom-call | flops 2162688000 | bytes 16896000 | tf_op jit(solution)/shard_map/cross_forward/pallas_call | solution.py:309
  55.7 15.3 %ffn_forward.1 = (f32[1000,768]{1,0:T(8,128)}, f32[1000,1]{1,0:T(8,128)}, bf16[1000,768]{1,0:T(8,128)(2,1)}, bf16[1000,1536]{1,0:T(8,128)(2,1)}, bf16[1000,1536]...) custom-call(f32[1000,768]{1,0:T(8,128)} %get-tuple-element.101.n1_ref.refs_14_, ...), custom_call_target="tpu_custom_call" | custom-call | flops 4718592000 | bytes 23150592 | tf_op jit(solution)/shard_map/ffn_forward/pallas_call | solution.py:365
  71.1 14.9 %ffn_backward.1 = (f32[1000,384]{1,0:T(8,128)}, f32[1000,768]{1,0:T(8,128)}, bf16[1000,768]{1,0:T(8,128)(2,1)}, bf16[1000,1536]{1,0:T(8,128)(2,1)}, bf16[1000,768]{1,0:T(8,128)(2,1)}, /*index=5*/f32[8,768]{1,0:T(8,128)}) custom-call(s32[1]{0:T(128)} %bitcast.side_ref, f32[1000,768]{1,0:T(8,128)} %get-tuple-element.104.n2_ref.n_ref, ...), custom_call_target="tpu_custom_call" | custom-call | flops 4718592000 | bytes 27758592 | tf_op jit(solution)/shard_map/ffn_backward/pallas_call | solution.py:425
  86.0 0.4 collective-permute-start.4
  86.3 0.5 shift-right-arithmetic_and_fusion.bits_ref
  86.9 14.7 %grad_ffn.1 = (bf16[8,48,1024]{2,1,0:T(8,128)(2,1)}, bf16[8,48,1024]{2,1,0:T(8,128)(2,1)}, bf16[8,48,1024]{2,1,0:T(8,128)(2,1)}, bf16[8,48,1024]{2,1,0:T(8,128)(...) custom-call(s32[4]{0:T(128)} %shift-right-arithmetic_and_fusion.bits_ref, ...), custom_call_target="tpu_custom_call" | custom-call | flops 4718592000 | bytes 12398592 | tf_op jit(solution)/shard_map/grad_ffn/pallas_call | solution.py:769
  101.6 2.7 %collective-permute-start.5 = (bf16[8,48,1024]{2,1,0:T(8,128)(2,1)}, bf16[8,48,1024]{2,1,0:T(8,128)(2,1)S(1)}, u32[]{:S(2)}, u32[]{:S(2)}) collective-permute-start(bf16[8,48,1024]{2,1,0:T(8,128)(2,1)} %get-tuple-element.116), channel_id=1, source_target_pairs={{0,2},{2,0},{4,6},{6,4},{8,10},{10,8},{12,14},{14,12},{16,18},{18,... | collective-permute-start | bytes 2359304 | tf_op jit(solution)/shard_map/ppermute | solution.py:1357
  104.3 1.5 collective-permute-start.6
  105.8 1.6 collective-permute-start.7
  107.4 0.0 collective-permute-done.4.t_ref
  107.4 0.0 copy-start
  107.4 1.1 copy-done
  108.5 30.0 %cross_backward.1 = (f32[1000,768]{1,0:T(8,128)}, bf16[1000,768]{1,0:T(8,128)(2,1)}, bf16[1000,384]{1,0:T(8,128)(2,1)}, bf16[1000,768]{1,0:T(8,128)(2,1)}, bf16[4000,768]{1,0:T(8,128)(2,1)}, /*index=5*/f32[8,768]{1,0:T(8,128)}) custom-call(s32[25]{0:T(128)} %broadcast_subtract_fusion.pick, f32[1000,768]{1,0:T(8,128)} %get-tuple-element.110.g_ref, ...), custom_call_target="tpu_custom_call" | custom-call | flops 3637248000 | bytes 27648000 | tf_op jit(solution)/shard_map/cross_backward/pallas_call | solution.py:512
  138.5 0.0 collective-permute-done.5.refs_1_
  138.5 0.0 copy-start.2
  138.5 0.0 collective-permute-done.6.refs_3_
  138.5 0.0 copy-start.3
  138.5 0.0 collective-permute-done.7.refs_5_
  138.6 0.0 copy-start.4
  138.6 0.8 copy-done.2
  139.4 0.3 copy-done.3
  139.7 0.3 copy-done.4
  140.0 41.8 %rows_backward.1 = (f32[1000,384]{1,0:T(8,128)}, bf16[1000,384]{1,0:T(8,128)(2,1)}, f32[8,768]{1,0:T(8,128)}, f32[48,3072]{1,0:T(8,128)}, bf16[8,48,512]{2,1,0:T...) custom-call(bf16[8,48,1024]{2,1,0:T(8,128)(2,1)} %get-tuple-element., ...), custom_call_target="tpu_custom_call" | custom-call | flops 5898240000 | bytes 23040000 | tf_op jit(solution)/shard_map/rows_backward/pallas_call | solution.py:1073
  181.8 0.1 collective-permute-start.8
  181.9 49.9 %patch_backward.1 = (bf16[25,145,512]{2,1,0:T(8,128)(2,1)}, f32[48,768]{1,0:T(8,128)}, f32[48,1536]{1,0:T(8,128)}, f32[64,768]{1,0:T(8,128)}, f32[16,768]{1,0:T(8,128)}) custom-call(bf16[25,145,1024]{2,1,0:T(8,128)(2,1)} %p_ref.3, bf16[4000,768]{1,0:T(8,128)(2,1)} %get-tuple-element.122.g_ref, bf16[2,1024,384]{2,1,0:T(8,128)(2,1)} %w_ref.13, ...), custom_call_target="tpu_custom_call" | custom-call | flops 12582912000 | bytes 33280000 | tf_op jit(solution)/shard_map/patch_backward/pallas_call | solution.py:1270
  231.8 0.0 collective-permute-done.8.t_ref
  231.8 0.0 copy-start.6
  231.9 0.9 copy-done.6
  232.7 8.4 %finish.1 = (f32[25,145,512]{2,1,0:T(8,128)}, f32[1000,384]{1,0:T(8,128)}, f32[3,48,384]{2,1,0:T(8,128)}, f32[48,384]{1,0:T(8,128)}, f32[48,384]{1,0:T(8,128)}, ...) custom-call(s32[1]{0:T(128)} %bitcast.side_ref, ...), custom_call_target="tpu_custom_call" | custom-call | flops 1856000 | bytes 11136000 | tf_op jit(solution)/shard_map/finish/pallas_call | solution.py:1327
  241.2 1.3 reduce.2
  (5 shorter events, 0.0 us)
Async XLA Ops:
  0.6 4.4 %collective-permute-start = (bf16[1000,384]{1,0:T(8,128)(2,1)}, bf16[1000,384]{1,0:T(8,128)(2,1)S(1)}, u32[]{:S(2)}, u32[]{:S(2)}) collective-permute-start(bf16[1000,384]{1,0:T(8,128)(2,1)} %a_ref.1), channel_id=1, source_target_pairs={{0,1},{1,0},{2,3},{3,2},{4,5},{5,4},{6,7},{7,6},{8,9},{9,8},{10,11... | collective-permute-start | bytes 2304008 | tf_op jit(solution)/shard_map/ppermute | solution.py:1422
  5.1 0.9 copy-start.11
  5.9 11.8 %copy-start.7 = (bf16[3,384]{1,0:T(4,128)(2,1)S(1)}, bf16[3,384]{1,0:T(4,128)(2,1)}, u32[]{:S(2)}) copy-start(bf16[3,384]{1,0:T(4,128)(2,1)} %param.34) | copy-start | bytes 6916
  5.9 11.8 %copy-start.8 = (bf16[3,384]{1,0:T(4,128)(2,1)S(1)}, bf16[3,384]{1,0:T(4,128)(2,1)}, u32[]{:S(2)}) copy-start(bf16[3,384]{1,0:T(4,128)(2,1)} %param.33) | copy-start | bytes 6916
  5.9 11.8 %copy-start.9 = (bf16[3,384]{1,0:T(4,128)(2,1)S(1)}, bf16[3,384]{1,0:T(4,128)(2,1)}, u32[]{:S(2)}) copy-start(bf16[3,384]{1,0:T(4,128)(2,1)} %param.32) | copy-start | bytes 6916
  5.9 12.3 %copy-start.5 = (bf16[1000,384]{1,0:T(8,128)(2,1)S(1)}, bf16[1000,384]{1,0:T(8,128)(2,1)}, u32[]{:S(2)}) copy-start(bf16[1000,384]{1,0:T(8,128)(2,1)} %param.35) | copy-start | bytes 2304004
  17.6 15.3 %collective-permute-start.1 = (bf16[1000,768]{1,0:T(8,128)(2,1)}, bf16[1000,768]{1,0:T(8,128)(2,1)S(1)}, u32[]{:S(2)}, u32[]{:S(2)}) collective-permute-start(bf16[1000,768]{1,0:T(8,128)(2,1)} %get-tuple-element.97.m_ref), channel_id=1, source_target_pairs={{0,1},{1,0},{2,3},{3,2},{4,5},{5,4},{6,7},{7,6},{8,9},{9,8},{10,11... | collective-permute-start | bytes 4608008 | tf_op jit(solution)/shard_map/ppermute | solution.py:1422
  17.8 12.9 %collective-permute-start.2 = (bf16[9,384]{1,0:T(8,128)(2,1)S(1)}, bf16[9,384]{1,0:T(8,128)(2,1)S(1)}, u32[]{:S(2)}, u32[]{:S(2)}) collective-permute-start(bf16[9,384]{1,0:T(8,128)(2,1)S(1)} %pad_maximum_fusion), channel_id=1, source_target_pairs={{0,1},{1,0},{2,3},{3,2},{4,5},{5,4},{6,7},{7,6},{8,9},{9,8},{10,11... | collective-permute-start | bytes 20744 | tf_op jit(solution)/shard_map/ppermute | solution.py:1422
  18.3 13.0 %collective-permute-start.3 = (bf16[1000,384]{1,0:T(8,128)(2,1)S(1)}, bf16[1000,384]{1,0:T(8,128)(2,1)S(1)}, u32[]{:S(2)}, u32[]{:S(2)}) collective-permute-start(bf16[1000,384]{1,0:T(8,128)(2,1)S(1)} %copy-done.5), channel_id=1, source_target_pairs={{0,1},{1,0},{2,3},{3,2},{4,5},{5,4},{6,7},{7,6},{8,9},{9,8},{10,11... | collective-permute-start | bytes 2304008 | tf_op jit(solution)/shard_map/ppermute | solution.py:1422
  18.4 11.2 %copy-start.12 = (s32[25]{0:T(128)S(1)}, s32[25]{0:T(128)}, u32[]{:S(2)}) copy-start(s32[25]{0:T(128)} %param.21) | copy-start | bytes 304
  18.4 11.7 %copy-start.10 = (bf16[1536]{0:T(1024)(128)(2,1)S(1)}, bf16[1536]{0:T(1024)(128)(2,1)}, u32[]{:S(2)}) copy-start(bf16[1536]{0:T(1024)(128)(2,1)} %param.30) | copy-start | bytes 9220
  32.9 1.1 copy-start.1
  86.0 21.4 %collective-permute-start.4 = (bf16[1000,768]{1,0:T(8,128)(2,1)}, bf16[1000,768]{1,0:T(8,128)(2,1)S(1)}, u32[]{:S(2)}, u32[]{:S(2)}) collective-permute-start(bf16[1000,768]{1,0:T(8,128)(2,1)} %get-tuple-element.119.m_ref), channel_id=1, source_target_pairs={{0,1},{1,0},{2,3},{3,2},{4,5},{5,4},{6,7},{7,6},{8,9},{9,8},{10,11... | collective-permute-start | bytes 4608008 | tf_op jit(solution)/shard_map/ppermute | solution.py:1422
  101.6 36.9 %collective-permute-start.5 = (bf16[8,48,1024]{2,1,0:T(8,128)(2,1)}, bf16[8,48,1024]{2,1,0:T(8,128)(2,1)S(1)}, u32[]{:S(2)}, u32[]{:S(2)}) collective-permute-start(bf16[8,48,1024]{2,1,0:T(8,128)(2,1)} %get-tuple-element.116), channel_id=1, source_target_pairs={{0,2},{2,0},{4,6},{6,4},{8,10},{10,8},{12,14},{14,12},{16,18},{18,... | collective-permute-start | bytes 2359304 | tf_op jit(solution)/shard_map/ppermute | solution.py:1357
  104.3 34.2 %collective-permute-start.6 = (bf16[8,48,1024]{2,1,0:T(8,128)(2,1)}, bf16[8,48,1024]{2,1,0:T(8,128)(2,1)S(1)}, u32[]{:S(2)}, u32[]{:S(2)}) collective-permute-start(bf16[8,48,1024]{2,1,0:T(8,128)(2,1)} %get-tuple-element.117), channel_id=1, source_target_pairs={{0,4},{2,6},{4,0},{6,2},{8,12},{10,14},{12,8},{14,10},{16,20},{18,... | collective-permute-start | bytes 2359304 | tf_op jit(solution)/shard_map/ppermute | solution.py:1357
  105.8 32.8 %collective-permute-start.7 = (bf16[8,48,1024]{2,1,0:T(8,128)(2,1)}, bf16[8,48,1024]{2,1,0:T(8,128)(2,1)S(1)}, u32[]{:S(2)}, u32[]{:S(2)}) collective-permute-start(bf16[8,48,1024]{2,1,0:T(8,128)(2,1)} %get-tuple-element.118), channel_id=1, source_target_pairs={{0,8},{2,10},{4,12},{6,14},{8,0},{10,2},{12,4},{14,6},{16,24},{18,... | collective-permute-start | bytes 2359304 | tf_op jit(solution)/shard_map/ppermute | solution.py:1357
  107.4 1.1 copy-start
  138.5 0.9 copy-start.2
  138.5 1.1 copy-start.3
  138.6 1.4 copy-start.4
  181.8 50.0 %collective-permute-start.8 = (bf16[1000,384]{1,0:T(8,128)(2,1)}, bf16[1000,384]{1,0:T(8,128)(2,1)S(1)}, u32[]{:S(2)}, u32[]{:S(2)}) collective-permute-start(bf16[1000,384]{1,0:T(8,128)(2,1)} %get-tuple-element.155), channel_id=1, source_target_pairs={{0,1},{1,0},{2,3},{3,2},{4,5},{5,4},{6,7},{7,6},{8,9},{9,8},{10,11... | collective-permute-start | bytes 2304008 | tf_op jit(solution)/shard_map/ppermute | solution.py:1422
  231.8 0.9 copy-start.6

commit v4 on v3

--- a/solution.py
+++ b/solution.py
@@ -44,7 +44,7 @@
     return pl.BlockSpec(shape, lambda i, *_: (i,) + zeros)
 
 
-def call(body, name, grid, ins, outs, scratch, flops, nbytes, scalars=0, vmem=60,
+def call(body, name, grid, ins, outs, scratch, flops, nbytes, scalars=0, vmem=63,
          collective=None):
     return pl.pallas_call(
         body,

time: 243 us -> 242 us (level)
  local copies, waits for them, and re-layouts: 8.36 us -> 5.51 us
    unnamed x26 -> x18, local copies, waits for them, and re-layouts: 5.47 us -> 2.62 us
  transfers between devices with their start and end apart: 9 -> 9, of which waited for: 0 -> 0; matrix products, arithmetic and copies ran while one was open for 3% -> 4% of each run, Pallas kernels for 44% -> 44%
where the time goes in v4:
time: 242 us; the launch traced here: 241 us
  Pallas kernels  220 us (91%)
  starting transfers between devices  7.52 us (3%)
  other arithmetic  7.49 us (3%)
  local copies, waits for them, and re-layouts  5.51 us (2%)
    pallas_call x1, Pallas kernels, patch_backward(): call(body, 'patch_backward', 3 * steps, ins, [((images, count, half), BF,...  49.9 us
    pallas_call x1, Pallas kernels, rows_backward(): call(body, 'rows_backward', steps, ins, outs, scratch, 2 * tokens * width...  41.8 us
    pallas_call x1, Pallas kernels, cross_backward(): call(body, 'cross_backward', steps, [full, full, full, whole(params.shape...  30 us
    pallas_call x1, Pallas kernels, cross_forward(): call(body, 'cross_forward', tokens // tile, [full, full, full, whole(para...  21.7 us
    pallas_call x1, Pallas kernels, ffn_forward(): call(body, 'ffn_forward', tokens // tile, [full, full, full, whole(params...  15.3 us
    pallas_call x1, Pallas kernels, ffn_backward(): call(body, 'ffn_backward', tokens // tile, [full, full, full, whole(param...  14.9 us
    pallas_call x1, Pallas kernels, grad_weight(): call(body, name, total, specs, outs, [pltpu.VMEM((width, tokens), BF), pl...  14.7 us
    pallas_call x1, Pallas kernels, self_forward(): call(body, 'self_forward', tokens // tile, [tiled((tile, here)), tiled((t...  11.7 us
  transfers between devices with their start and end apart: 9, of which 0 were waited for; matrix products, arithmetic and copies ran while one was open for 4% of the time, Pallas kernels for 44%

profile of v4, /device:TPU:0, one launch (start us, length us, event | category | flops | bytes accessed | tf_op | source)
XLA Modules:
  0.0 240.9 jit_solution(6935663114706447767)
XLA Ops:
  0.6 0.5 collective-permute-start
  1.2 0.8 broadcast_add_fusion
  2.0 0.7 reshape.76.ir_ref.refs_20_
  2.6 1.0 reshape.85.ic_ref.refs_19_
  3.6 0.8 convert_reduce_fusion.1
  4.4 0.6 broadcast_in_dim.11.b_ref
  5.0 0.0 collective-permute-done.z_ref
  5.0 0.0 copy-start.7
  5.1 0.9 copy-done.7
  5.9 0.0 copy-start.3
  5.9 0.0 copy-start.4
  5.9 0.0 copy-start.5
  5.9 0.0 copy-start.1
  5.9 11.7 %self_forward.1 = (bf16[1000,1152]{1,0:T(8,128)(2,1)}, bf16[1000,384]{1,0:T(8,128)(2,1)}, bf16[1000,768]{1,0:T(8,128)(2,1)}, bf16[1000,768]{1,0:T(8,128)(2,1)}) custom-call(s32[1]{0:T(128)} %bitcast.side_ref, bf16[1000,384]{1,0:T(8,128)(2,1)} %a_ref.1, bf16[1000,384]{1,0:T(8,128)(2,1)} %copy-done.7, bf16[3,768,384]{2,1,0:T(8,128)(2,1)} %refs_17_.1, ...), custom_call_target="tpu_custom_call" | custom-call | flops 2359296000 | bytes 8503296 | tf_op jit(solution)/shard_map/self_forward/pallas_call | solution.py:220
  17.6 0.1 collective-permute-start.1
  17.7 0.0 copy-done.3
  17.7 0.0 copy-done.4
  17.7 0.0 copy-done.5
  17.8 0.5 collective-permute-start.2
  18.3 0.0 copy-done.1
  18.3 0.1 collective-permute-start.3
  18.4 0.0 copy-start.8
  18.4 0.0 copy-start.6
  18.4 11.2 %project_patches.1 = (bf16[4000,384]{1,0:T(8,128)(2,1)}, bf16[4000,384]{1,0:T(8,128)(2,1)}) custom-call(bf16[25,145,1024]{2,1,0:T(8,128)(2,1)} %p_ref.3, bf16[2,1024,384]{2,1,0:T(8,128)(2,1)} %w_ref.13, bf16[2,384]{1,0:T(2,128)(2,1)} %b_ref.3), custom_call_target="tpu_custom_call" | custom-call | flops 6291456000 | bytes 15140864 | tf_op jit(solution)/shard_map/project_patches/pallas_call | solution.py:174
  29.6 0.0 copy-done.8
  29.6 0.5 broadcast_subtract_fusion.pick
  30.1 0.0 copy-done.6
  30.1 0.6 broadcast_in_dim.12.b_ref
  30.7 0.0 collective-permute-done.2
  30.7 0.6 fusion.pr_ref.refs_13_
  31.3 0.0 collective-permute-done.3
  31.3 2.9 %maximum_select_fusion.e_ref = bf16[1000,768]{1,0:T(8,128)(2,1)} fusion(bf16[1000,384]{1,0:T(8,128)(2,1)} %collective-permute-done.3, bf16[1000,384]{1,0:T(8,128)(2,1)S(1)} %copy-done.1, pred[]{:T(512)S(6)} %eq.6), kind=kLoop, calls=%fused_computation | loop fusion | flops 6912000 | bytes 3072001 | tf_op jit(solution)/shard_map/jit(_where)/select_n | solution.py:1462
  34.2 0.0 collective-permute-done.1.t_ref
  34.2 21.7 %cross_forward.1 = (f32[1000,768]{1,0:T(8,128)}, f32[1000,1]{1,0:T(8,128)}, bf16[1000,768]{1,0:T(8,128)(2,1)}, bf16[1000,384]{1,0:T(8,128)(2,1)}, bf16[1000,384]...) custom-call(s32[25]{0:T(128)} %broadcast_subtract_fusion.pick, ...), custom_call_target="tpu_custom_call" | custom-call | flops 2162688000 | bytes 16896000 | tf_op jit(solution)/shard_map/cross_forward/pallas_call | solution.py:309
  55.9 15.3 %ffn_forward.1 = (f32[1000,768]{1,0:T(8,128)}, f32[1000,1]{1,0:T(8,128)}, bf16[1000,768]{1,0:T(8,128)(2,1)}, bf16[1000,1536]{1,0:T(8,128)(2,1)}, bf16[1000,1536]...) custom-call(f32[1000,768]{1,0:T(8,128)} %get-tuple-element.101.n1_ref.refs_14_, ...), custom_call_target="tpu_custom_call" | custom-call | flops 4718592000 | bytes 23150592 | tf_op jit(solution)/shard_map/ffn_forward/pallas_call | solution.py:365
  71.2 14.9 %ffn_backward.1 = (f32[1000,384]{1,0:T(8,128)}, f32[1000,768]{1,0:T(8,128)}, bf16[1000,768]{1,0:T(8,128)(2,1)}, bf16[1000,1536]{1,0:T(8,128)(2,1)}, bf16[1000,768]{1,0:T(8,128)(2,1)}, /*index=5*/f32[8,768]{1,0:T(8,128)}) custom-call(s32[1]{0:T(128)} %bitcast.side_ref, f32[1000,768]{1,0:T(8,128)} %get-tuple-element.104.n2_ref.n_ref, ...), custom_call_target="tpu_custom_call" | custom-call | flops 4718592000 | bytes 27758592 | tf_op jit(solution)/shard_map/ffn_backward/pallas_call | solution.py:425
  86.1 0.4 collective-permute-start.4
  86.5 0.5 shift-right-arithmetic_and_fusion.bits_ref
  87.0 14.7 %grad_ffn.1 = (bf16[8,48,1024]{2,1,0:T(8,128)(2,1)}, bf16[8,48,1024]{2,1,0:T(8,128)(2,1)}, bf16[8,48,1024]{2,1,0:T(8,128)(2,1)}, bf16[8,48,1024]{2,1,0:T(8,128)(...) custom-call(s32[4]{0:T(128)} %shift-right-arithmetic_and_fusion.bits_ref, ...), custom_call_target="tpu_custom_call" | custom-call | flops 4718592000 | bytes 12398592 | tf_op jit(solution)/shard_map/grad_ffn/pallas_call | solution.py:769
  101.7 2.7 %collective-permute-start.5 = (bf16[8,48,1024]{2,1,0:T(8,128)(2,1)}, bf16[8,48,1024]{2,1,0:T(8,128)(2,1)S(1)}, u32[]{:S(2)}, u32[]{:S(2)}) collective-permute-start(bf16[8,48,1024]{2,1,0:T(8,128)(2,1)} %get-tuple-element.116), channel_id=1, source_target_pairs={{0,2},{2,0},{4,6},{6,4},{8,10},{10,8},{12,14},{14,12},{16,18},{18,... | collective-permute-start | bytes 2359304 | tf_op jit(solution)/shard_map/ppermute | solution.py:1357
  104.4 1.5 collective-permute-start.6
  105.9 1.6 collective-permute-start.7
  107.5 0.0 collective-permute-done.4.t_ref
  107.5 30.0 %cross_backward.1 = (f32[1000,768]{1,0:T(8,128)}, bf16[1000,768]{1,0:T(8,128)(2,1)}, bf16[1000,384]{1,0:T(8,128)(2,1)}, bf16[1000,768]{1,0:T(8,128)(2,1)}, bf16[4000,768]{1,0:T(8,128)(2,1)}, /*index=5*/f32[8,768]{1,0:T(8,128)}) custom-call(s32[25]{0:T(128)} %broadcast_subtract_fusion.pick, f32[1000,768]{1,0:T(8,128)} %get-tuple-element.110.g_ref, ...), custom_call_target="tpu_custom_call" | custom-call | flops 3637248000 | bytes 27648000 | tf_op jit(solution)/shard_map/cross_backward/pallas_call | solution.py:512
  137.5 0.0 collective-permute-done.5.refs_1_
  137.5 0.0 copy-start
  137.5 0.0 collective-permute-done.6.refs_3_
  137.6 0.0 collective-permute-done.7.refs_5_
  137.6 0.9 copy-done
  138.4 41.8 %rows_backward.1 = (f32[1000,384]{1,0:T(8,128)}, bf16[1000,384]{1,0:T(8,128)(2,1)}, f32[8,768]{1,0:T(8,128)}, f32[48,3072]{1,0:T(8,128)}, bf16[8,48,512]{2,1,0:T...) custom-call(bf16[8,48,1024]{2,1,0:T(8,128)(2,1)} %get-tuple-element., ...), custom_call_target="tpu_custom_call" | custom-call | flops 5898240000 | bytes 23040000 | tf_op jit(solution)/shard_map/rows_backward/pallas_call | solution.py:1073
  180.2 0.1 collective-permute-start.8
  180.3 49.9 %patch_backward.1 = (bf16[25,145,512]{2,1,0:T(8,128)(2,1)}, f32[48,768]{1,0:T(8,128)}, f32[48,1536]{1,0:T(8,128)}, f32[64,768]{1,0:T(8,128)}, f32[16,768]{1,0:T(8,128)}) custom-call(bf16[25,145,1024]{2,1,0:T(8,128)(2,1)} %p_ref.3, bf16[4000,768]{1,0:T(8,128)(2,1)} %get-tuple-element.122.g_ref, bf16[2,1024,384]{2,1,0:T(8,128)(2,1)} %w_ref.13, ...), custom_call_target="tpu_custom_call" | custom-call | flops 12582912000 | bytes 33280000 | tf_op jit(solution)/shard_map/patch_backward/pallas_call | solution.py:1270
  230.2 0.0 collective-permute-done.8.t_ref
  230.2 0.0 copy-start.2
  230.2 0.9 copy-done.2
  231.1 8.4 %finish.1 = (f32[25,145,512]{2,1,0:T(8,128)}, f32[1000,384]{1,0:T(8,128)}, f32[3,48,384]{2,1,0:T(8,128)}, f32[48,384]{1,0:T(8,128)}, f32[48,384]{1,0:T(8,128)}, ...) custom-call(s32[1]{0:T(128)} %bitcast.side_ref, ...), custom_call_target="tpu_custom_call" | custom-call | flops 1856000 | bytes 11136000 | tf_op jit(solution)/shard_map/finish/pallas_call | solution.py:1327
  239.6 1.3 reduce.2
  (4 shorter events, 0.0 us)
Async XLA Ops:
  0.6 4.4 %collective-permute-start = (bf16[1000,384]{1,0:T(8,128)(2,1)}, bf16[1000,384]{1,0:T(8,128)(2,1)S(1)}, u32[]{:S(2)}, u32[]{:S(2)}) collective-permute-start(bf16[1000,384]{1,0:T(8,128)(2,1)} %a_ref.1), channel_id=1, source_target_pairs={{0,1},{1,0},{2,3},{3,2},{4,5},{5,4},{6,7},{7,6},{8,9},{9,8},{10,11... | collective-permute-start | bytes 2304008 | tf_op jit(solution)/shard_map/ppermute | solution.py:1422
  5.0 0.9 copy-start.7
  5.9 11.8 %copy-start.3 = (bf16[3,384]{1,0:T(4,128)(2,1)S(1)}, bf16[3,384]{1,0:T(4,128)(2,1)}, u32[]{:S(2)}) copy-start(bf16[3,384]{1,0:T(4,128)(2,1)} %param.34) | copy-start | bytes 6916
  5.9 11.8 %copy-start.4 = (bf16[3,384]{1,0:T(4,128)(2,1)S(1)}, bf16[3,384]{1,0:T(4,128)(2,1)}, u32[]{:S(2)}) copy-start(bf16[3,384]{1,0:T(4,128)(2,1)} %param.33) | copy-start | bytes 6916
  5.9 11.8 %copy-start.5 = (bf16[3,384]{1,0:T(4,128)(2,1)S(1)}, bf16[3,384]{1,0:T(4,128)(2,1)}, u32[]{:S(2)}) copy-start(bf16[3,384]{1,0:T(4,128)(2,1)} %param.32) | copy-start | bytes 6916
  5.9 12.3 %copy-start.1 = (bf16[1000,384]{1,0:T(8,128)(2,1)S(1)}, bf16[1000,384]{1,0:T(8,128)(2,1)}, u32[]{:S(2)}) copy-start(bf16[1000,384]{1,0:T(8,128)(2,1)} %param.35) | copy-start | bytes 2304004
  17.6 16.6 %collective-permute-start.1 = (bf16[1000,768]{1,0:T(8,128)(2,1)}, bf16[1000,768]{1,0:T(8,128)(2,1)}, u32[]{:S(2)}, u32[]{:S(2)}) collective-permute-start(bf16[1000,768]{1,0:T(8,128)(2,1)} %get-tuple-element.97.m_ref), channel_id=1, source_target_pairs={{0,1},{1,0},{2,3},{3,2},{4,5},{5,4},{6,7},{7,6},{8,9},{9,8},{10,11... | collective-permute-start | bytes 4608008 | tf_op jit(solution)/shard_map/ppermute | solution.py:1422
  17.8 12.9 %collective-permute-start.2 = (bf16[9,384]{1,0:T(8,128)(2,1)S(1)}, bf16[9,384]{1,0:T(8,128)(2,1)S(1)}, u32[]{:S(2)}, u32[]{:S(2)}) collective-permute-start(bf16[9,384]{1,0:T(8,128)(2,1)S(1)} %pad_maximum_fusion), channel_id=1, source_target_pairs={{0,1},{1,0},{2,3},{3,2},{4,5},{5,4},{6,7},{7,6},{8,9},{9,8},{10,11... | collective-permute-start | bytes 20744 | tf_op jit(solution)/shard_map/ppermute | solution.py:1422
  18.3 13.0 %collective-permute-start.3 = (bf16[1000,384]{1,0:T(8,128)(2,1)S(1)}, bf16[1000,384]{1,0:T(8,128)(2,1)}, u32[]{:S(2)}, u32[]{:S(2)}) collective-permute-start(bf16[1000,384]{1,0:T(8,128)(2,1)S(1)} %copy-done.1), channel_id=1, source_target_pairs={{0,1},{1,0},{2,3},{3,2},{4,5},{5,4},{6,7},{7,6},{8,9},{9,8},{10,11... | collective-permute-start | bytes 2304008 | tf_op jit(solution)/shard_map/ppermute | solution.py:1422
  18.4 11.2 %copy-start.8 = (s32[25]{0:T(128)S(1)}, s32[25]{0:T(128)}, u32[]{:S(2)}) copy-start(s32[25]{0:T(128)} %param.21) | copy-start | bytes 304
  18.4 11.7 %copy-start.6 = (bf16[1536]{0:T(1024)(128)(2,1)S(1)}, bf16[1536]{0:T(1024)(128)(2,1)}, u32[]{:S(2)}) copy-start(bf16[1536]{0:T(1024)(128)(2,1)} %param.30) | copy-start | bytes 9220
  86.1 21.4 %collective-permute-start.4 = (bf16[1000,768]{1,0:T(8,128)(2,1)}, bf16[1000,768]{1,0:T(8,128)(2,1)}, u32[]{:S(2)}, u32[]{:S(2)}) collective-permute-start(bf16[1000,768]{1,0:T(8,128)(2,1)} %get-tuple-element.119.m_ref), channel_id=1, source_target_pairs={{0,1},{1,0},{2,3},{3,2},{4,5},{5,4},{6,7},{7,6},{8,9},{9,8},{10,11... | collective-permute-start | bytes 4608008 | tf_op jit(solution)/shard_map/ppermute | solution.py:1422
  101.7 35.8 %collective-permute-start.5 = (bf16[8,48,1024]{2,1,0:T(8,128)(2,1)}, bf16[8,48,1024]{2,1,0:T(8,128)(2,1)S(1)}, u32[]{:S(2)}, u32[]{:S(2)}) collective-permute-start(bf16[8,48,1024]{2,1,0:T(8,128)(2,1)} %get-tuple-element.116), channel_id=1, source_target_pairs={{0,2},{2,0},{4,6},{6,4},{8,10},{10,8},{12,14},{14,12},{16,18},{18,... | collective-permute-start | bytes 2359304 | tf_op jit(solution)/shard_map/ppermute | solution.py:1357
  104.4 33.1 %collective-permute-start.6 = (bf16[8,48,1024]{2,1,0:T(8,128)(2,1)}, bf16[8,48,1024]{2,1,0:T(8,128)(2,1)}, u32[]{:S(2)}, u32[]{:S(2)}) collective-permute-start(bf16[8,48,1024]{2,1,0:T(8,128)(2,1)} %get-tuple-element.117), channel_id=1, source_target_pairs={{0,4},{2,6},{4,0},{6,2},{8,12},{10,14},{12,8},{14,10},{16,20},{18,... | collective-permute-start | bytes 2359304 | tf_op jit(solution)/shard_map/ppermute | solution.py:1357
  105.9 31.6 %collective-permute-start.7 = (bf16[8,48,1024]{2,1,0:T(8,128)(2,1)}, bf16[8,48,1024]{2,1,0:T(8,128)(2,1)}, u32[]{:S(2)}, u32[]{:S(2)}) collective-permute-start(bf16[8,48,1024]{2,1,0:T(8,128)(2,1)} %get-tuple-element.118), channel_id=1, source_target_pairs={{0,8},{2,10},{4,12},{6,14},{8,0},{10,2},{12,4},{14,6},{16,24},{18,... | collective-permute-start | bytes 2359304 | tf_op jit(solution)/shard_map/ppermute | solution.py:1357
  137.5 0.9 copy-start
  180.2 50.0 %collective-permute-start.8 = (bf16[1000,384]{1,0:T(8,128)(2,1)}, bf16[1000,384]{1,0:T(8,128)(2,1)S(1)}, u32[]{:S(2)}, u32[]{:S(2)}) collective-permute-start(bf16[1000,384]{1,0:T(8,128)(2,1)} %get-tuple-element.155), channel_id=1, source_target_pairs={{0,1},{1,0},{2,3},{3,2},{4,5},{5,4},{6,7},{7,6},{8,9},{9,8},{10,11... | collective-permute-start | bytes 2304008 | tf_op jit(solution)/shard_map/ppermute | solution.py:1422
  230.2 0.9 copy-start.2

commit v5 on v4

--- a/solution.py
+++ b/solution.py
@@ -974,6 +974,7 @@
             for which, stream in enumerate(cross):
                 split_shards(full, slice(which * third, (which + 1) * third), stream.pairs[0],
                              stream.order[0], size)
+                stream.start(0)
             for s in range(3):
                 wt[s * here : (s + 1) * here, :] = w_ref[s].T
             ot[...] = o_ref[...].T
@@ -988,9 +989,6 @@
                 def _(t=t):
                     for stream in ffn:
                         stream.advance(t + 1)
-                    if t == 1:
-                        for stream in cross:
-                            stream.start(0)
 
         @pl.when((at >= begin) & (at < after_self))
         def _():

time: 242 us -> 242 us (level)
  no operation moved by 1% of the time
where the time goes in v5:
time: 242 us; the launch traced here: 241 us
  Pallas kernels  220 us (91%)
  starting transfers between devices  7.52 us (3%)
  other arithmetic  7.49 us (3%)
  local copies, waits for them, and re-layouts  5.51 us (2%)
    pallas_call x1, Pallas kernels, patch_backward(): call(body, 'patch_backward', 3 * steps, ins, [((images, count, half), BF,...  49.6 us
    pallas_call x1, Pallas kernels, rows_backward(): call(body, 'rows_backward', steps, ins, outs, scratch, 2 * tokens * width...  42.2 us
    pallas_call x1, Pallas kernels, cross_backward(): call(body, 'cross_backward', steps, [full, full, full, whole(params.shape...  30 us
    pallas_call x1, Pallas kernels, cross_forward(): call(body, 'cross_forward', tokens // tile, [full, full, full, whole(para...  21.7 us
    pallas_call x1, Pallas kernels, ffn_forward(): call(body, 'ffn_forward', tokens // tile, [full, full, full, whole(params...  15.3 us
    pallas_call x1, Pallas kernels, ffn_backward(): call(body, 'ffn_backward', tokens // tile, [full, full, full, whole(param...  14.9 us
    pallas_call x1, Pallas kernels, grad_weight(): call(body, name, total, specs, outs, [pltpu.VMEM((width, tokens), BF), pl...  14.7 us
    pallas_call x1, Pallas kernels, self_forward(): call(body, 'self_forward', tokens // tile, [tiled((tile, here)), tiled((t...  11.7 us
  transfers between devices with their start and end apart: 9, of which 0 were waited for; matrix products, arithmetic and copies ran while one was open for 4% of the time, Pallas kernels for 44%

profile of v5, /device:TPU:0, one launch (start us, length us, event | category | flops | bytes accessed | tf_op | source)
XLA Modules:
  0.0 241.0 jit_solution(4156801900119818292)
XLA Ops:
  0.6 0.5 collective-permute-start
  1.2 0.8 broadcast_add_fusion
  2.0 0.7 reshape.76.ir_ref.refs_20_
  2.6 1.0 reshape.85.ic_ref.refs_19_
  3.6 0.8 convert_reduce_fusion.1
  4.4 0.6 broadcast_in_dim.11.b_ref
  5.0 0.0 collective-permute-done.z_ref
  5.0 0.0 copy-start.7
  5.1 0.9 copy-done.7
  5.9 0.0 copy-start.3
  5.9 0.0 copy-start.4
  5.9 0.0 copy-start.5
  5.9 0.0 copy-start.1
  5.9 11.7 %self_forward.1 = (bf16[1000,1152]{1,0:T(8,128)(2,1)}, bf16[1000,384]{1,0:T(8,128)(2,1)}, bf16[1000,768]{1,0:T(8,128)(2,1)}, bf16[1000,768]{1,0:T(8,128)(2,1)}) custom-call(s32[1]{0:T(128)} %bitcast.side_ref, bf16[1000,384]{1,0:T(8,128)(2,1)} %a_ref.1, bf16[1000,384]{1,0:T(8,128)(2,1)} %copy-done.7, bf16[3,768,384]{2,1,0:T(8,128)(2,1)} %refs_17_.1, ...), custom_call_target="tpu_custom_call" | custom-call | flops 2359296000 | bytes 8503296 | tf_op jit(solution)/shard_map/self_forward/pallas_call | solution.py:220
  17.6 0.1 collective-permute-start.1
  17.7 0.0 copy-done.3
  17.7 0.0 copy-done.4
  17.7 0.0 copy-done.5
  17.8 0.5 collective-permute-start.2
  18.3 0.0 copy-done.1
  18.3 0.1 collective-permute-start.3
  18.4 0.0 copy-start.8
  18.4 0.0 copy-start.6
  18.4 11.2 %project_patches.1 = (bf16[4000,384]{1,0:T(8,128)(2,1)}, bf16[4000,384]{1,0:T(8,128)(2,1)}) custom-call(bf16[25,145,1024]{2,1,0:T(8,128)(2,1)} %p_ref.3, bf16[2,1024,384]{2,1,0:T(8,128)(2,1)} %w_ref.13, bf16[2,384]{1,0:T(2,128)(2,1)} %b_ref.3), custom_call_target="tpu_custom_call" | custom-call | flops 6291456000 | bytes 15140864 | tf_op jit(solution)/shard_map/project_patches/pallas_call | solution.py:174
  29.6 0.0 copy-done.8
  29.6 0.5 broadcast_subtract_fusion.pick
  30.1 0.0 copy-done.6
  30.1 0.6 broadcast_in_dim.12.b_ref
  30.7 0.0 collective-permute-done.2
  30.7 0.6 fusion.pr_ref.refs_13_
  31.3 0.0 collective-permute-done.3
  31.3 2.9 %maximum_select_fusion.e_ref = bf16[1000,768]{1,0:T(8,128)(2,1)} fusion(bf16[1000,384]{1,0:T(8,128)(2,1)} %collective-permute-done.3, bf16[1000,384]{1,0:T(8,128)(2,1)S(1)} %copy-done.1, pred[]{:T(512)S(6)} %eq.6), kind=kLoop, calls=%fused_computation | loop fusion | flops 6912000 | bytes 3072001 | tf_op jit(solution)/shard_map/jit(_where)/select_n | solution.py:1460
  34.2 0.0 collective-permute-done.1.t_ref
  34.2 21.7 %cross_forward.1 = (f32[1000,768]{1,0:T(8,128)}, f32[1000,1]{1,0:T(8,128)}, bf16[1000,768]{1,0:T(8,128)(2,1)}, bf16[1000,384]{1,0:T(8,128)(2,1)}, bf16[1000,384]...) custom-call(s32[25]{0:T(128)} %broadcast_subtract_fusion.pick, ...), custom_call_target="tpu_custom_call" | custom-call | flops 2162688000 | bytes 16896000 | tf_op jit(solution)/shard_map/cross_forward/pallas_call | solution.py:309
  55.9 15.3 %ffn_forward.1 = (f32[1000,768]{1,0:T(8,128)}, f32[1000,1]{1,0:T(8,128)}, bf16[1000,768]{1,0:T(8,128)(2,1)}, bf16[1000,1536]{1,0:T(8,128)(2,1)}, bf16[1000,1536]...) custom-call(f32[1000,768]{1,0:T(8,128)} %get-tuple-element.101.n1_ref.refs_14_, ...), custom_call_target="tpu_custom_call" | custom-call | flops 4718592000 | bytes 23150592 | tf_op jit(solution)/shard_map/ffn_forward/pallas_call | solution.py:365
  71.2 14.9 %ffn_backward.1 = (f32[1000,384]{1,0:T(8,128)}, f32[1000,768]{1,0:T(8,128)}, bf16[1000,768]{1,0:T(8,128)(2,1)}, bf16[1000,1536]{1,0:T(8,128)(2,1)}, bf16[1000,768]{1,0:T(8,128)(2,1)}, /*index=5*/f32[8,768]{1,0:T(8,128)}) custom-call(s32[1]{0:T(128)} %bitcast.side_ref, f32[1000,768]{1,0:T(8,128)} %get-tuple-element.104.n2_ref.n_ref, ...), custom_call_target="tpu_custom_call" | custom-call | flops 4718592000 | bytes 27758592 | tf_op jit(solution)/shard_map/ffn_backward/pallas_call | solution.py:425
  86.1 0.4 collective-permute-start.4
  86.5 0.5 shift-right-arithmetic_and_fusion.bits_ref
  87.0 14.7 %grad_ffn.1 = (bf16[8,48,1024]{2,1,0:T(8,128)(2,1)}, bf16[8,48,1024]{2,1,0:T(8,128)(2,1)}, bf16[8,48,1024]{2,1,0:T(8,128)(2,1)}, bf16[8,48,1024]{2,1,0:T(8,128)(...) custom-call(s32[4]{0:T(128)} %shift-right-arithmetic_and_fusion.bits_ref, ...), custom_call_target="tpu_custom_call" | custom-call | flops 4718592000 | bytes 12398592 | tf_op jit(solution)/shard_map/grad_ffn/pallas_call | solution.py:769
  101.7 2.7 %collective-permute-start.5 = (bf16[8,48,1024]{2,1,0:T(8,128)(2,1)}, bf16[8,48,1024]{2,1,0:T(8,128)(2,1)S(1)}, u32[]{:S(2)}, u32[]{:S(2)}) collective-permute-start(bf16[8,48,1024]{2,1,0:T(8,128)(2,1)} %get-tuple-element.116), channel_id=1, source_target_pairs={{0,2},{2,0},{4,6},{6,4},{8,10},{10,8},{12,14},{14,12},{16,18},{18,... | collective-permute-start | bytes 2359304 | tf_op jit(solution)/shard_map/ppermute | solution.py:1355
  104.4 1.5 collective-permute-start.6
  105.9 1.6 collective-permute-start.7
  107.5 0.0 collective-permute-done.4.t_ref
  107.5 30.0 %cross_backward.1 = (f32[1000,768]{1,0:T(8,128)}, bf16[1000,768]{1,0:T(8,128)(2,1)}, bf16[1000,384]{1,0:T(8,128)(2,1)}, bf16[1000,768]{1,0:T(8,128)(2,1)}, bf16[4000,768]{1,0:T(8,128)(2,1)}, /*index=5*/f32[8,768]{1,0:T(8,128)}) custom-call(s32[25]{0:T(128)} %broadcast_subtract_fusion.pick, f32[1000,768]{1,0:T(8,128)} %get-tuple-element.110.g_ref, ...), custom_call_target="tpu_custom_call" | custom-call | flops 3637248000 | bytes 27648000 | tf_op jit(solution)/shard_map/cross_backward/pallas_call | solution.py:512
  137.5 0.0 collective-permute-done.5.refs_1_
  137.5 0.0 copy-start
  137.6 0.0 collective-permute-done.6.refs_3_
  137.6 0.0 collective-permute-done.7.refs_5_
  137.6 0.9 copy-done
  138.4 42.2 %rows_backward.1 = (f32[1000,384]{1,0:T(8,128)}, bf16[1000,384]{1,0:T(8,128)(2,1)}, f32[8,768]{1,0:T(8,128)}, f32[48,3072]{1,0:T(8,128)}, bf16[8,48,512]{2,1,0:T...) custom-call(bf16[8,48,1024]{2,1,0:T(8,128)(2,1)} %get-tuple-element., ...), custom_call_target="tpu_custom_call" | custom-call | flops 5898240000 | bytes 23040000 | tf_op jit(solution)/shard_map/rows_backward/pallas_call | solution.py:1071
  180.7 0.1 collective-permute-start.8
  180.8 49.6 %patch_backward.1 = (bf16[25,145,512]{2,1,0:T(8,128)(2,1)}, f32[48,768]{1,0:T(8,128)}, f32[48,1536]{1,0:T(8,128)}, f32[64,768]{1,0:T(8,128)}, f32[16,768]{1,0:T(8,128)}) custom-call(bf16[25,145,1024]{2,1,0:T(8,128)(2,1)} %p_ref.3, bf16[4000,768]{1,0:T(8,128)(2,1)} %get-tuple-element.122.g_ref, bf16[2,1024,384]{2,1,0:T(8,128)(2,1)} %w_ref.13, ...), custom_call_target="tpu_custom_call" | custom-call | flops 12582912000 | bytes 33280000 | tf_op jit(solution)/shard_map/patch_backward/pallas_call | solution.py:1268
  230.3 0.0 collective-permute-done.8.t_ref
  230.3 0.0 copy-start.2
  230.4 0.9 copy-done.2
  231.2 8.4 %finish.1 = (f32[25,145,512]{2,1,0:T(8,128)}, f32[1000,384]{1,0:T(8,128)}, f32[3,48,384]{2,1,0:T(8,128)}, f32[48,384]{1,0:T(8,128)}, f32[48,384]{1,0:T(8,128)}, ...) custom-call(s32[1]{0:T(128)} %bitcast.side_ref, ...), custom_call_target="tpu_custom_call" | custom-call | flops 1856000 | bytes 11136000 | tf_op jit(solution)/shard_map/finish/pallas_call | solution.py:1325
  239.7 1.3 reduce.2
  (4 shorter events, 0.0 us)
Async XLA Ops:
  0.6 4.4 %collective-permute-start = (bf16[1000,384]{1,0:T(8,128)(2,1)}, bf16[1000,384]{1,0:T(8,128)(2,1)S(1)}, u32[]{:S(2)}, u32[]{:S(2)}) collective-permute-start(bf16[1000,384]{1,0:T(8,128)(2,1)} %a_ref.1), channel_id=1, source_target_pairs={{0,1},{1,0},{2,3},{3,2},{4,5},{5,4},{6,7},{7,6},{8,9},{9,8},{10,11... | collective-permute-start | bytes 2304008 | tf_op jit(solution)/shard_map/ppermute | solution.py:1420
  5.0 0.9 copy-start.7
  5.9 11.8 %copy-start.3 = (bf16[3,384]{1,0:T(4,128)(2,1)S(1)}, bf16[3,384]{1,0:T(4,128)(2,1)}, u32[]{:S(2)}) copy-start(bf16[3,384]{1,0:T(4,128)(2,1)} %param.34) | copy-start | bytes 6916
  5.9 11.8 %copy-start.4 = (bf16[3,384]{1,0:T(4,128)(2,1)S(1)}, bf16[3,384]{1,0:T(4,128)(2,1)}, u32[]{:S(2)}) copy-start(bf16[3,384]{1,0:T(4,128)(2,1)} %param.33) | copy-start | bytes 6916
  5.9 11.8 %copy-start.5 = (bf16[3,384]{1,0:T(4,128)(2,1)S(1)}, bf16[3,384]{1,0:T(4,128)(2,1)}, u32[]{:S(2)}) copy-start(bf16[3,384]{1,0:T(4,128)(2,1)} %param.32) | copy-start | bytes 6916
  5.9 12.3 %copy-start.1 = (bf16[1000,384]{1,0:T(8,128)(2,1)S(1)}, bf16[1000,384]{1,0:T(8,128)(2,1)}, u32[]{:S(2)}) copy-start(bf16[1000,384]{1,0:T(8,128)(2,1)} %param.35) | copy-start | bytes 2304004
  17.6 16.6 %collective-permute-start.1 = (bf16[1000,768]{1,0:T(8,128)(2,1)}, bf16[1000,768]{1,0:T(8,128)(2,1)}, u32[]{:S(2)}, u32[]{:S(2)}) collective-permute-start(bf16[1000,768]{1,0:T(8,128)(2,1)} %get-tuple-element.97.m_ref), channel_id=1, source_target_pairs={{0,1},{1,0},{2,3},{3,2},{4,5},{5,4},{6,7},{7,6},{8,9},{9,8},{10,11... | collective-permute-start | bytes 4608008 | tf_op jit(solution)/shard_map/ppermute | solution.py:1420
  17.8 12.9 %collective-permute-start.2 = (bf16[9,384]{1,0:T(8,128)(2,1)S(1)}, bf16[9,384]{1,0:T(8,128)(2,1)S(1)}, u32[]{:S(2)}, u32[]{:S(2)}) collective-permute-start(bf16[9,384]{1,0:T(8,128)(2,1)S(1)} %pad_maximum_fusion), channel_id=1, source_target_pairs={{0,1},{1,0},{2,3},{3,2},{4,5},{5,4},{6,7},{7,6},{8,9},{9,8},{10,11... | collective-permute-start | bytes 20744 | tf_op jit(solution)/shard_map/ppermute | solution.py:1420
  18.3 13.0 %collective-permute-start.3 = (bf16[1000,384]{1,0:T(8,128)(2,1)S(1)}, bf16[1000,384]{1,0:T(8,128)(2,1)}, u32[]{:S(2)}, u32[]{:S(2)}) collective-permute-start(bf16[1000,384]{1,0:T(8,128)(2,1)S(1)} %copy-done.1), channel_id=1, source_target_pairs={{0,1},{1,0},{2,3},{3,2},{4,5},{5,4},{6,7},{7,6},{8,9},{9,8},{10,11... | collective-permute-start | bytes 2304008 | tf_op jit(solution)/shard_map/ppermute | solution.py:1420
  18.4 11.2 %copy-start.8 = (s32[25]{0:T(128)S(1)}, s32[25]{0:T(128)}, u32[]{:S(2)}) copy-start(s32[25]{0:T(128)} %param.21) | copy-start | bytes 304
  18.4 11.7 %copy-start.6 = (bf16[1536]{0:T(1024)(128)(2,1)S(1)}, bf16[1536]{0:T(1024)(128)(2,1)}, u32[]{:S(2)}) copy-start(bf16[1536]{0:T(1024)(128)(2,1)} %param.30) | copy-start | bytes 9220
  86.1 21.4 %collective-permute-start.4 = (bf16[1000,768]{1,0:T(8,128)(2,1)}, bf16[1000,768]{1,0:T(8,128)(2,1)}, u32[]{:S(2)}, u32[]{:S(2)}) collective-permute-start(bf16[1000,768]{1,0:T(8,128)(2,1)} %get-tuple-element.119.m_ref), channel_id=1, source_target_pairs={{0,1},{1,0},{2,3},{3,2},{4,5},{5,4},{6,7},{7,6},{8,9},{9,8},{10,11... | collective-permute-start | bytes 4608008 | tf_op jit(solution)/shard_map/ppermute | solution.py:1420
  101.7 35.8 %collective-permute-start.5 = (bf16[8,48,1024]{2,1,0:T(8,128)(2,1)}, bf16[8,48,1024]{2,1,0:T(8,128)(2,1)S(1)}, u32[]{:S(2)}, u32[]{:S(2)}) collective-permute-start(bf16[8,48,1024]{2,1,0:T(8,128)(2,1)} %get-tuple-element.116), channel_id=1, source_target_pairs={{0,2},{2,0},{4,6},{6,4},{8,10},{10,8},{12,14},{14,12},{16,18},{18,... | collective-permute-start | bytes 2359304 | tf_op jit(solution)/shard_map/ppermute | solution.py:1355
  104.4 33.1 %collective-permute-start.6 = (bf16[8,48,1024]{2,1,0:T(8,128)(2,1)}, bf16[8,48,1024]{2,1,0:T(8,128)(2,1)}, u32[]{:S(2)}, u32[]{:S(2)}) collective-permute-start(bf16[8,48,1024]{2,1,0:T(8,128)(2,1)} %get-tuple-element.117), channel_id=1, source_target_pairs={{0,4},{2,6},{4,0},{6,2},{8,12},{10,14},{12,8},{14,10},{16,20},{18,... | collective-permute-start | bytes 2359304 | tf_op jit(solution)/shard_map/ppermute | solution.py:1355
  105.9 31.6 %collective-permute-start.7 = (bf16[8,48,1024]{2,1,0:T(8,128)(2,1)}, bf16[8,48,1024]{2,1,0:T(8,128)(2,1)}, u32[]{:S(2)}, u32[]{:S(2)}) collective-permute-start(bf16[8,48,1024]{2,1,0:T(8,128)(2,1)} %get-tuple-element.118), channel_id=1, source_target_pairs={{0,8},{2,10},{4,12},{6,14},{8,0},{10,2},{12,4},{14,6},{16,24},{18,... | collective-permute-start | bytes 2359304 | tf_op jit(solution)/shard_map/ppermute | solution.py:1355
  137.5 0.9 copy-start
  180.7 49.7 %collective-permute-start.8 = (bf16[1000,384]{1,0:T(8,128)(2,1)}, bf16[1000,384]{1,0:T(8,128)(2,1)S(1)}, u32[]{:S(2)}, u32[]{:S(2)}) collective-permute-start(bf16[1000,384]{1,0:T(8,128)(2,1)} %get-tuple-element.155), channel_id=1, source_target_pairs={{0,1},{1,0},{2,3},{3,2},{4,5},{5,4},{6,7},{7,6},{8,9},{9,8},{10,11... | collective-permute-start | bytes 2304008 | tf_op jit(solution)/shard_map/ppermute | solution.py:1420
  230.3 0.9 copy-start.2
